TPU v7x, 32 devices: a whole 2x2x4 slice. The times are simulated.
32 devices in a mesh: cells: 8 (over z, y), depth: 4 (over x, core).
Axes of the slice: x: 2, y: 2, z: 4, core: 2. Of those that a mesh axis runs over, the one named last changes fastest.
Arguments:
- x_in: float32 [2, 4096, 256], P(None, ('cells', 'depth')), may hold values from -6 to 6
- vec_in: float32 [2, 3, 4096, 256], P(None, None, ('cells', 'depth')), may hold values from -6 to 6
- cot_x: float32 [2, 4096, 256], P(None, ('cells', 'depth')), may hold values from -6 to 6
- cot_vec: float32 [2, 3, 4096, 256], P(None, None, ('cells', 'depth')), may hold values from -6 to 6
- mats: float32 [753664], P('cells')
- vecs: float32 [3584], P('cells')
- mats_first: float32 [753664], P('cells')
- mats_second: float32 [753664], P('cells')
- vecs_first: float32 [3584], P('cells')
- vecs_second: float32 [3584], P('cells')
- atom_count: int32 [2, 32], P(None, ('cells', 'depth')), may hold values from 64 to 128, as said below
- neighbours: int32 [2, 64, 4096], P(None, None, ('cells', 'depth')), may hold values from 0 to 1663, as said below
- edge_mask: int32 [2, 64, 4096], P(None, None, ('cells', 'depth')), may hold values from 0 to 1, as said below
- edge_vec: float32 [2, 3, 64, 4096], P(None, None, None, ('cells', 'depth')), may hold values from -2.8 to 2.8, as said below
- send_list: int32 [2, 192, 256], P(None, ('cells', 'depth')), may hold values from 0 to 127, as said below
Outputs:
- out_x: float32 [2, 4096, 256], P(None, ('cells', 'depth'))
- out_vec: float32 [2, 3, 4096, 256], P(None, None, ('cells', 'depth'))
- grad_x: float32 [2, 4096, 256], P(None, ('cells', 'depth'))
- grad_vec: float32 [2, 3, 4096, 256], P(None, None, ('cells', 'depth'))
- grad_mats: float32 [753664], P('cells')
- grad_vecs: float32 [3584], P('cells')
- new_mats: float32 [753664], P('cells')
- new_vecs: float32 [3584], P('cells')
- new_mats_first: float32 [753664], P('cells')
- new_mats_second: float32 [753664], P('cells')
- new_vecs_first: float32 [3584], P('cells')
- new_vecs_second: float32 [3584], P('cells')
Inputs may be any that keep to these rules, and one draw needn't show every extreme that they name: `atom_count`: in every micro-batch some domain holds exactly 128 real atoms. `edge_mask`: live edges of an atom are its first slots: 4 to 64 for each real atom, none for padding atoms; some atom has 64 in every micro-batch. `neighbours`: A slot below the domain's atom count is an own atom; slot 128 + f * 256 + h is the h-th atom received across face f; never a padding atom. `send_list`: every entry is below its domain's atom count; entries may repeat. `edge_vec`: each component's magnitude is 0.3 or more.
All inputs are finite; a program needn't handle non-finite values.
Results may differ from a plain program's by a relative error of at most 0.012.
The roundings to bfloat16 on the way count: a program that leaves them out, or rounds other values in their place, can miss the bound.
Values may be sent and summed in bfloat16 or wider, within the bound.
A program may use at most 512 MiB of HBM per device.

v0:
```python
from functools import partial
import math

import jax
import jax.numpy as jnp
from jax import lax
from jax.sharding import PartitionSpec as P

HEADS = 8
NR = 32
FOLD = 4
STEP = 3


norm_eps = 1e-05
cut_radius = 5.0
beta_one = 0.5
beta_two = 0.5
learn_rate = 0.05
decay_rate = 0.01
adam_eps = 1e-08


def from_behind(shard, axis, by):
    length = lax.axis_size(axis)
    return lax.ppermute(shard, axis, [(i, (i + by) % length) for i in range(length)])


def unpack_mats(flat_array, feat_width, basis_count):
    shapes = (
        (feat_width, feat_width),
        (feat_width, feat_width),
        (feat_width, 3 * feat_width),
        (feat_width, 3 * feat_width),
        (feat_width, 3 * feat_width),
        (basis_count, feat_width),
        (basis_count, 3 * feat_width),
    )
    pieces = []
    offset = 0
    for shape_one in shapes:
        length = shape_one[0] * shape_one[1]
        pieces.append(flat_array[offset : offset + length].reshape(shape_one))
        offset = offset + length
    return pieces


def unpack_vecs(flat_array, feat_width):
    lengths = (
        feat_width,
        feat_width,
        feat_width,
        feat_width,
        3 * feat_width,
        3 * feat_width,
        feat_width,
        3 * feat_width,
    )
    pieces = []
    offset = 0
    for length in lengths:
        pieces.append(flat_array[offset : offset + length])
        offset = offset + length
    return pieces


def layer_norm(x_rows, gain, shift):
    mean_val = jnp.mean(x_rows, axis=-1, keepdims=True)
    centered = x_rows - mean_val
    variance = jnp.mean(centered * centered, axis=-1, keepdims=True)
    return centered * lax.rsqrt(variance + norm_eps) * gain + shift


def radial_terms(edge_geom, edge_live):
    radius = jnp.sqrt(jnp.sum(edge_geom * edge_geom, axis=0))
    unit_dir = edge_geom / radius
    live_float = edge_live.astype(jnp.float32)
    cosine_cut = 0.5 * (jnp.cos(math.pi * radius / cut_radius) + 1.0) * live_float
    start_value = math.exp(-cut_radius)
    centers = jnp.linspace(start_value, 1.0, NR).astype(jnp.float32)
    width_coef = (2.0 / NR * (1.0 - start_value)) ** (-2)
    decayed = jnp.exp(-(5.0 / cut_radius) * radius)
    basis = cosine_cut[..., None] * jnp.exp(-width_coef * (decayed[..., None] - centers) ** 2)
    return (unit_dir, cosine_cut, basis)


def message_sum(
    query_rows,
    key_edge,
    value_edge,
    vec_edge,
    filt_key,
    filt_value,
    cosine_cut,
    unit_dir,
    live_float,
):
    feat_width = query_rows.shape[-1]
    edge_shape = key_edge.shape[:2]
    head_shape = edge_shape + (HEADS, feat_width // HEADS)
    product_qk = query_rows[None] * key_edge * jax.nn.silu(filt_key)
    scores = jnp.sum(product_qk.reshape(head_shape), axis=-1)
    attention = jax.nn.silu(scores) * cosine_cut[..., None]
    gated = value_edge * jax.nn.silu(filt_value)
    x_part = gated[..., :feat_width]
    vec_gate = gated[..., feat_width : 2 * feat_width]
    dir_gate = gated[..., 2 * feat_width :]
    x_msg = (x_part.reshape(head_shape) * attention[..., None]).reshape(edge_shape + (feat_width,))
    x_agg = jnp.sum(x_msg, axis=0)
    vec_msg = (vec_edge * vec_gate[None] + dir_gate[None] * unit_dir[..., None]) * live_float[
        None, :, :, None
    ]
    vec_agg = jnp.sum(vec_msg, axis=1)
    return (x_agg, vec_agg)


def branch_out(out_all, vec_proj, vec_agg, atom_live):
    feat_width = vec_agg.shape[-1]
    out_one = out_all[:, :feat_width]
    out_two = out_all[:, feat_width : 2 * feat_width]
    out_three = out_all[:, 2 * feat_width :]
    proj_one = vec_proj[..., :feat_width]
    proj_two = vec_proj[..., feat_width : 2 * feat_width]
    proj_three = vec_proj[..., 2 * feat_width :]
    vec_dot = jnp.sum(proj_one * proj_two, axis=0)
    delta_x = (vec_dot * out_two + out_three) * atom_live[:, None]
    delta_vec = (proj_three * out_one[None] + vec_agg) * atom_live[None, :, None]
    return (delta_x, delta_vec)


def by_block(array, atom_axis, block_atoms):
    shape_now = array.shape
    reshaped = array.reshape(
        shape_now[:atom_axis]
        + (shape_now[atom_axis] // block_atoms, block_atoms)
        + shape_now[atom_axis + 1 :]
    )
    return jnp.moveaxis(reshaped, atom_axis, 0)


def fetch_weights(mats, vecs):
    return (
        lax.all_gather(mats.astype(jnp.bfloat16), "cells", axis=0, tiled=True),
        lax.all_gather(vecs.astype(jnp.bfloat16), "cells", axis=0, tiled=True),
    )


def reduce_grads(grad_mats, grad_vecs):
    shard_mats, shard_vecs = (
        lax.psum_scatter(grad_mats, "cells", scatter_dimension=0, tiled=True),
        lax.psum_scatter(grad_vecs, "cells", scatter_dimension=0, tiled=True),
    )
    return lax.psum((shard_mats, shard_vecs), "depth")


def micro_step(
    x_rows,
    vec_rows,
    cot_rows,
    cot_vecs,
    fetched,
    live_count,
    nbr_rows,
    edge_live,
    edge_geom,
    send_rows,
):
    f32 = jnp.float32
    bf16 = jnp.bfloat16
    mats_low, vecs_low = fetched
    feat_width = x_rows.shape[-1]
    atoms_dev = x_rows.shape[0]
    halo_rows = send_rows.shape[-1]
    slot_count = atoms_dev + 6 * halo_rows
    w_query, w_key, w_value, w_vector, w_out, w_fkey, w_fvalue = unpack_mats(
        mats_low, feat_width, NR
    )
    small_params = [vector_piece.astype(f32) for vector_piece in unpack_vecs(vecs_low, feat_width)]
    ln_gain, ln_shift, b_query, b_key, b_value, b_out, b_fkey, b_fvalue = small_params
    atom_live = (jnp.arange(atoms_dev) < live_count[0]).astype(f32)
    normed, norm_pull = jax.vjp(layer_norm, x_rows, ln_gain, ln_shift)
    norm_low = normed.astype(bf16)
    vec_low = vec_rows.astype(bf16)
    own_stack = jnp.concatenate([norm_low[None], vec_low], axis=0)
    received = []
    for face_idx, offset in enumerate((1, -1, FOLD, -FOLD)):
        received.append(from_behind(own_stack[:, send_rows[face_idx]], "cells", offset))
    for face_idx, offset in ((4, 1), (5, -1)):
        received.append(from_behind(own_stack[:, send_rows[face_idx]], "depth", offset))
    table_stack = jnp.concatenate([own_stack] + received, axis=1)
    table_x = table_stack[0]
    table_vec = table_stack[1:]
    query = (jnp.dot(norm_low, w_query, preferred_element_type=f32) + b_query).astype(bf16)
    keys = (jnp.dot(table_x, w_key, preferred_element_type=f32) + b_key).astype(bf16)
    values = (jnp.dot(table_x, w_value, preferred_element_type=f32) + b_value).astype(bf16)
    vec_proj = jnp.einsum("cai,io->cao", vec_low, w_vector, preferred_element_type=f32)
    unit_dir, cosine_cut, basis = radial_terms(edge_geom, edge_live)
    basis_low = basis.astype(bf16)
    live_float = edge_live.astype(f32)
    block_atoms = min(32, atoms_dev)
    blocked = (
        by_block(query, 0, block_atoms),
        by_block(nbr_rows, 1, block_atoms),
        by_block(basis_low, 1, block_atoms),
        by_block(cosine_cut, 1, block_atoms),
        by_block(unit_dir, 2, block_atoms),
        by_block(live_float, 1, block_atoms),
    )

    def edge_inputs(query_blk, nbr_blk, basis_blk):
        key_edge = keys[nbr_blk].astype(f32)
        value_edge = values[nbr_blk].astype(f32)
        vec_edge = table_vec[:, nbr_blk].astype(f32)
        filt_key = jnp.einsum("kbr,rf->kbf", basis_blk, w_fkey, preferred_element_type=f32) + b_fkey
        filt_value = (
            jnp.einsum("kbr,rf->kbf", basis_blk, w_fvalue, preferred_element_type=f32) + b_fvalue
        )
        return (query_blk.astype(f32), key_edge, value_edge, vec_edge, filt_key, filt_value)

    def forward_block(carry, items):
        query_blk, nbr_blk, basis_blk, cut_blk, unit_blk, live_blk = items
        sums = message_sum(*edge_inputs(query_blk, nbr_blk, basis_blk), cut_blk, unit_blk, live_blk)
        return (carry, sums)

    unused, (agg_blocks, vagg_blocks) = lax.scan(forward_block, 0, blocked)
    x_agg = agg_blocks.reshape(atoms_dev, feat_width)
    vec_agg = jnp.moveaxis(vagg_blocks, 0, 1).reshape(3, atoms_dev, feat_width)
    agg_low = x_agg.astype(bf16)
    out_all = jnp.dot(agg_low, w_out, preferred_element_type=f32) + b_out
    (delta_x, delta_vec), branch_pull = jax.vjp(
        partial(branch_out, atom_live=atom_live), out_all, vec_proj, vec_agg
    )
    out_x = x_rows + delta_x
    out_vec = vec_rows + delta_vec
    g_out, g_proj, g_vagg = branch_pull((cot_rows, cot_vecs))
    g_out_low = g_out.astype(bf16)
    g_proj_low = g_proj.astype(bf16)
    grad_wout = jnp.dot(agg_low.T, g_out_low, preferred_element_type=f32)
    grad_bout = jnp.sum(g_out_low.astype(f32), axis=0)
    g_agg = jnp.dot(g_out_low, w_out.T, preferred_element_type=f32)
    grad_wvec = jnp.einsum("cai,cao->io", vec_low, g_proj_low, preferred_element_type=f32)
    g_vec_own = jnp.einsum("cao,io->cai", g_proj_low, w_vector, preferred_element_type=f32)

    def backward_block(carry, items):
        gw_fkey, gw_fvalue, gb_fkey, gb_fvalue = carry
        query_blk, nbr_blk, basis_blk, cut_blk, unit_blk, live_blk, gagg_blk, gvagg_blk = items
        inputs = edge_inputs(query_blk, nbr_blk, basis_blk)
        sums, edge_pull = jax.vjp(
            partial(message_sum, cosine_cut=cut_blk, unit_dir=unit_blk, live_float=live_blk),
            *inputs
        )
        g_query_blk, g_kedge, g_vedge, g_vecedge, g_fkey, g_fvalue = edge_pull(
            (gagg_blk, gvagg_blk)
        )
        fkey_low = g_fkey.astype(bf16)
        fvalue_low = g_fvalue.astype(bf16)
        gw_fkey = gw_fkey + jnp.einsum(
            "kbr,kbf->rf", basis_blk, fkey_low, preferred_element_type=f32
        )
        gw_fvalue = gw_fvalue + jnp.einsum(
            "kbr,kbf->rf", basis_blk, fvalue_low, preferred_element_type=f32
        )
        gb_fkey = gb_fkey + jnp.sum(fkey_low.astype(f32), axis=(0, 1))
        gb_fvalue = gb_fvalue + jnp.sum(fvalue_low.astype(f32), axis=(0, 1))
        edge_grads = (g_kedge, g_vedge, jnp.moveaxis(g_vecedge, 0, 2))
        return ((gw_fkey, gw_fvalue, gb_fkey, gb_fvalue), (g_query_blk, edge_grads))

    start_carry = (
        jnp.zeros(w_fkey.shape, f32),
        jnp.zeros(w_fvalue.shape, f32),
        jnp.zeros((feat_width,), f32),
        jnp.zeros((3 * feat_width,), f32),
    )
    back_items = blocked + (by_block(g_agg, 0, block_atoms), by_block(g_vagg, 1, block_atoms))
    end_carry, (dq_blocks, edge_stacks) = lax.scan(backward_block, start_carry, back_items)
    gw_fkey, gw_fvalue, gb_fkey, gb_fvalue = end_carry
    kedge_all, vedge_all, vecedge_all = edge_stacks
    flat_nbr = blocked[1].reshape(-1)
    tab_key = jax.ops.segment_sum(
        kedge_all.reshape(-1, feat_width), flat_nbr, num_segments=slot_count
    )
    tab_value = jax.ops.segment_sum(
        vedge_all.reshape(-1, 3 * feat_width), flat_nbr, num_segments=slot_count
    )
    tab_vec = jax.ops.segment_sum(
        vecedge_all.reshape(-1, 3, feat_width), flat_nbr, num_segments=slot_count
    )
    g_query = dq_blocks.reshape(atoms_dev, feat_width).astype(bf16)
    grad_wq = jnp.dot(norm_low.T, g_query, preferred_element_type=f32)
    grad_bq = jnp.sum(g_query.astype(f32), axis=0)
    g_keys = tab_key.astype(bf16)
    g_values = tab_value.astype(bf16)
    grad_wk = jnp.dot(table_x.T, g_keys, preferred_element_type=f32)
    grad_bk = jnp.sum(g_keys.astype(f32), axis=0)
    grad_wv = jnp.dot(table_x.T, g_values, preferred_element_type=f32)
    grad_bv = jnp.sum(g_values.astype(f32), axis=0)
    g_table_x = jnp.dot(g_keys, w_key.T, preferred_element_type=f32) + jnp.dot(
        g_values, w_value.T, preferred_element_type=f32
    )
    g_table = jnp.concatenate([g_table_x[None], jnp.moveaxis(tab_vec, 1, 0)], axis=0)
    g_norm_own = jnp.dot(g_query, w_query.T, preferred_element_type=f32)
    g_own = g_table[:, :atoms_dev] + jnp.concatenate([g_norm_own[None], g_vec_own], axis=0)
    returned = jnp.zeros((4, atoms_dev, feat_width), f32)
    for face_idx, offset in enumerate((1, -1, FOLD, -FOLD)):
        rows_face = g_table[
            :, atoms_dev + face_idx * halo_rows : atoms_dev + (face_idx + 1) * halo_rows
        ].astype(bf16)
        coming = from_behind(rows_face, "cells", -offset)
        returned = returned.at[:, send_rows[face_idx]].add(coming.astype(f32))
    for face_idx, offset in ((4, 1), (5, -1)):
        rows_face = g_table[
            :, atoms_dev + face_idx * halo_rows : atoms_dev + (face_idx + 1) * halo_rows
        ].astype(bf16)
        coming = from_behind(rows_face, "depth", -offset)
        returned = returned.at[:, send_rows[face_idx]].add(coming.astype(f32))
    g_total = g_own + returned
    g_x_norm, grad_gain, grad_shift = norm_pull(g_total[0])
    grad_x = cot_rows + g_x_norm
    grad_vec = cot_vecs + g_total[1:]
    grad_mats = jnp.concatenate(
        [
            grad_piece.reshape(-1)
            for grad_piece in (grad_wq, grad_wk, grad_wv, grad_wvec, grad_wout, gw_fkey, gw_fvalue)
        ]
    )
    grad_vecs = jnp.concatenate(
        [grad_gain, grad_shift, grad_bq, grad_bk, grad_bv, grad_bout, gb_fkey, gb_fvalue]
    )
    return (out_x, out_vec, grad_x, grad_vec, grad_mats, grad_vecs)


def adam_update(weight, grad, first, second):
    first_new = beta_one * first + (1.0 - beta_one) * grad
    second_new = beta_two * second + (1.0 - beta_two) * grad * grad
    first_hat = first_new / (1.0 - beta_one**STEP)
    second_hat = second_new / (1.0 - beta_two**STEP)
    weight_new = weight - learn_rate * (
        first_hat / (jnp.sqrt(second_hat) + adam_eps) + decay_rate * weight
    )
    return (weight_new, first_new, second_new)


def shards(
    x_in,
    vec_in,
    cot_x,
    cot_vec,
    mats,
    vecs,
    mats_first,
    mats_second,
    vecs_first,
    vecs_second,
    atom_count,
    neighbours,
    edge_mask,
    edge_vec,
    send_list,
):
    micro_total = x_in.shape[0]
    sum_mats = jnp.zeros(mats.shape, jnp.float32)
    sum_vecs = jnp.zeros(vecs.shape, jnp.float32)
    outs_x = []
    outs_vec = []
    grads_x = []
    grads_vec = []
    for micro_idx in range(micro_total):
        fetched = fetch_weights(mats, vecs)
        results = micro_step(
            x_in[micro_idx],
            vec_in[micro_idx],
            cot_x[micro_idx],
            cot_vec[micro_idx],
            fetched,
            atom_count[micro_idx],
            neighbours[micro_idx],
            edge_mask[micro_idx],
            edge_vec[micro_idx],
            send_list[micro_idx],
        )
        outs_x.append(results[0])
        outs_vec.append(results[1])
        grads_x.append(results[2])
        grads_vec.append(results[3])
        shard_mats, shard_vecs = reduce_grads(results[4], results[5])
        sum_mats = sum_mats + shard_mats
        sum_vecs = sum_vecs + shard_vecs
    new_mats, mats_one, mats_two = adam_update(mats, sum_mats, mats_first, mats_second)
    new_vecs, vecs_one, vecs_two = adam_update(vecs, sum_vecs, vecs_first, vecs_second)
    return (
        jnp.stack(outs_x),
        jnp.stack(outs_vec),
        jnp.stack(grads_x),
        jnp.stack(grads_vec),
        sum_mats,
        sum_vecs,
        new_mats,
        new_vecs,
        mats_one,
        mats_two,
        vecs_one,
        vecs_two,
    )


def solution(mesh):
    in_specs = (
        P(None, ("cells", "depth"), None),
        P(None, None, ("cells", "depth"), None),
        P(None, ("cells", "depth"), None),
        P(None, None, ("cells", "depth"), None),
        P("cells"),
        P("cells"),
        P("cells"),
        P("cells"),
        P("cells"),
        P("cells"),
        P(None, ("cells", "depth")),
        P(None, None, ("cells", "depth")),
        P(None, None, ("cells", "depth")),
        P(None, None, None, ("cells", "depth")),
        P(None, ("cells", "depth"), None),
    )
    out_specs = (
        P(None, ("cells", "depth"), None),
        P(None, None, ("cells", "depth"), None),
        P(None, ("cells", "depth"), None),
        P(None, None, ("cells", "depth"), None),
        P("cells"),
        P("cells"),
        P("cells"),
        P("cells"),
        P("cells"),
        P("cells"),
        P("cells"),
        P("cells"),
    )
    return jax.shard_map(shards, mesh=mesh, in_specs=in_specs, out_specs=out_specs, check_vma=False)
```

profile of v0, /device:TPU:0, one launch (start us, length us, event | category | flops | bytes accessed | tf_op | source)
XLA Modules:
  0.0 4338.4 jit_solution(1317066364797652104)
XLA Ops:
  12.0 23.4 all-reduce.18
  123.7 9.7 collective-permute-done
  138.4 22.8 collective-permute-done.2
  161.5 9.7 collective-permute-done.3
  198.4 319.0 %while.75 = (s32[]{:T(128)}, bf16[4,32,256]{2,1,0:T(8,128)(2,1)S(1)}, f32[4,3,32,256]{3,1,2,0:T(4,128)}, s32[4,64,32]{2,1,0:T(8,128)}, bf16[1664,768]{1,0:T(8,12...) while((s32[]{:T(128)}, ...), condition=%wide.region_17.19_spmd, body=%wide.region_13.18_spmd.sunk | while | flops 160481280 | bytes 70209824 | solution.py:225
  199.7 9.4 gather_fusion.3
  249.6 18.6 gather_fusion.5
  279.3 9.4 gather_fusion.3
  329.3 18.6 gather_fusion.5
  358.9 9.4 gather_fusion.3
  408.9 18.6 gather_fusion.5
  438.6 9.4 gather_fusion.3
  488.6 18.6 gather_fusion.5
  519.4 308.3 %while.74 = (s32[]{:T(128)}, bf16[4,32,256]{2,1,0:T(8,128)(2,1)}, f32[4,3,32,256]{3,1,2,0:T(4,128)}, s32[4,64,32]{2,1,0:T(8,128)}, bf16[1664,768]{1,0:T(8,128)(2...) while((s32[]{:T(128)}, bf16[4,32,256]{2,1,0:T(8,128)(2,1)}, ...), condition=%wide.region_8.10_spmd, body=%wide.region_4.9_spmd.sunk | while | flops 160481280 | bytes 83841360 | solution.py:225
  520.4 12.2 gather_fusion
  569.7 16.6 gather_fusion.2
  597.4 12.2 gather_fusion
  646.7 16.6 gather_fusion.2
  674.5 12.2 gather_fusion
  723.8 16.6 gather_fusion.2
  751.5 12.2 gather_fusion
  800.8 16.6 gather_fusion.2
  843.1 11.5 broadcast.786.clone
  854.7 11.4 broadcast.787.clone
  866.1 542.7 %while.76 = (s32[]{:T(128)}, f32[32,256]{1,0:T(8,128)}, f32[32,768]{1,0:T(8,128)}, f32[256]{0:T(256)}, f32[768]{0:T(1024)}, /*index=5*/bf16[4,32,256]{2,1,0:T(8,...) while((s32[]{:T(128)}, f32[32,256]{1,0:T(8,128)}, ...), condition=%wide.region_27.29_spmd.clone, body=%wide.region_19.28_spmd.clone.sunk | while | flops 343696384 | bytes 193636400 | solution.py:275
  908.1 18.5 gather_fusion.7
  926.6 15.4 fusion.306
  942.0 9.4 gather_fusion.8
  1043.5 18.5 gather_fusion.7
  1062.1 15.4 fusion.306
  1077.4 9.4 gather_fusion.8
  1179.1 18.5 gather_fusion.7
  1197.7 15.4 fusion.306
  1213.0 9.4 gather_fusion.8
  1314.7 18.5 gather_fusion.7
  1333.2 15.4 fusion.306
  1348.6 9.4 gather_fusion.8
  1412.4 45.0 %scatter_custom_fusion = f32[1664,256]{1,0:T(8,128)S(1)} fusion(s32[8192]{0:T(1024)} %reshape.1359, f32[8192,256]{1,0:T(8,128)} %bitcast.779, f32[]{:T(128)} %constant.177.clone.1), kind=kCustom, calls=%fused_computation.308 | custom fusion | flops 2097152 | bytes 1704448 | tf_op jit(solution)/shard_map/scatter-add | solution.py:279
  1471.9 11.5 broadcast.786.clone.1
  1483.4 11.4 broadcast.787.clone.1
  1494.8 543.4 %while.77 = (s32[]{:T(128)}, f32[32,256]{1,0:T(8,128)}, f32[32,768]{1,0:T(8,128)}, f32[256]{0:T(256)}, f32[768]{0:T(1024)}, /*index=5*/bf16[4,32,256]{2,1,0:T(8,...) while((s32[]{:T(128)}, f32[32,256]{1,0:T(8,128)}, ...), condition=%wide.region_48.50_spmd.clone, body=%wide.region_40.49_spmd.clone.sunk | while | flops 343696384 | bytes 193652832 | solution.py:275
  1536.7 18.6 gather_fusion.10
  1555.3 15.4 fusion.317
  1570.7 9.4 gather_fusion.11
  1580.2 9.1 convert_reduce_fusion.18
  1672.5 18.6 gather_fusion.10
  1691.1 15.4 fusion.317
  1706.5 9.4 gather_fusion.11
  1808.3 18.6 gather_fusion.10
  1826.9 15.4 fusion.317
  1842.3 9.4 gather_fusion.11
  1851.7 9.1 convert_reduce_fusion.18
  1944.0 18.6 gather_fusion.10
  1962.6 15.4 fusion.317
  1978.0 9.4 gather_fusion.11
  1987.4 9.1 convert_reduce_fusion.18
  2041.9 45.0 %scatter_custom_fusion.9 = f32[1664,256]{1,0:T(8,128)S(1)} fusion(s32[8192]{0:T(1024)} %reshape.1431, f32[8192,256]{1,0:T(8,128)} %bitcast.780, f32[]{:T(128)} %constant.177.clone.1), kind=kCustom, calls=%fused_computation.306 | custom fusion | flops 2097152 | bytes 1704448 | tf_op jit(solution)/shard_map/scatter-add | solution.py:279
  2094.8 56.2 %scatter_custom_fusion.1 = f32[1664,768]{1,0:T(8,128)} fusion(s32[8192]{0:T(1024)} %reshape.1359, f32[8192,768]{1,0:T(8,128)} %bitcast.777, f32[]{:T(128)} %constant.177.clone.1), kind=kCustom, calls=%fused_computation.264 | custom fusion | flops 6291456 | bytes 5112320 | tf_op jit(solution)/shard_map/scatter-add | solution.py:282
  2159.6 904.5 %scatter_fusion = f32[1664,3,256]{2,1,0:T(4,128)} fusion(f32[1664,3,256]{2,1,0:T(4,128)} %broadcast.789.clone, s32[8192]{0:T(1024)S(1)} %copy-done.165, f32[8192,3,256]{2,1,0:T(4,128)} %bitcast.761), kind=kCustom, calls=%fused_computation.26 | custom fusion | flops 6291456 | bytes 75530240 | tf_op jit(solution)/shard_map/scatter-add | solution.py:285
  3083.2 904.2 %scatter_fusion.7 = f32[1664,3,256]{2,1,0:T(4,128)} fusion(f32[1664,3,256]{2,1,0:T(4,128)} %broadcast.789.clone.1, s32[8192]{0:T(1024)S(1)} %copy-done.164, f32[8192,3,256]{2,1,0:T(4,128)} %bitcast.762), kind=kCustom, calls=%fused_computation.35 | custom fusion | flops 6291456 | bytes 75530240 | tf_op jit(solution)/shard_map/scatter-add | solution.py:285
  3993.7 56.3 %scatter_custom_fusion.10 = f32[1664,768]{1,0:T(8,128)} fusion(s32[8192]{0:T(1024)S(1)} %copy-done.164, f32[8192,768]{1,0:T(8,128)} %bitcast.778, f32[]{:T(128)} %constant.177.clone.1), kind=kCustom, calls=%fused_computation.262 | custom fusion | flops 6291456 | bytes 5112320 | tf_op jit(solution)/shard_map/scatter-add | solution.py:282
  4178.5 11.5 collective-permute-done.21
  4252.2 35.1 all-reduce.20
  4298.9 28.9 all-reduce.24.cloned.1.call-done
  (1618 shorter events, 1516.4 us)
Async XLA Ops:
  7.2 34.6 copy-start.194
  7.2 170.4 %all-gather.2.cloned.1.call-start = ((), (), s32[]{:S(2)}) async-start(), calls=%async_computation | async-start | bytes 1695744 | tf_op jit(solution)/shard_map/all_gather | solution.py:143
  8.9 4287.5 %all-reduce.26.cloned.1.call-start = ((), (), s32[]{:S(2)}) async-start(), calls=%async_computation.2 | async-start | bytes 6029312
  36.5 25.1 copy-start.118
  37.2 146.6 %copy-start.180 = (f32[256]{0:T(256)}, f32[256]{0:T(256)S(1)}, u32[]{:S(2)}) copy-start(f32[256]{0:T(256)S(1)} %get-tuple-element.1231) | copy-start | bytes 3076
  38.3 145.5 %copy-start.190 = (f32[128]{0:T(128)}, f32[128]{0:T(128)S(1)}, u32[]{:S(2)}) copy-start(f32[128]{0:T(128)S(1)} %broadcast_multiply_fusion.3) | copy-start | bytes 1540
  38.3 144.6 %copy-start.192 = (f32[128]{0:T(128)}, f32[128]{0:T(128)S(1)}, u32[]{:S(2)}) copy-start(f32[128]{0:T(128)S(1)} %broadcast_multiply_fusion.2) | copy-start | bytes 1540
  39.5 144.3 %copy-start.222 = (f32[128]{0:T(128)}, f32[128]{0:T(128)S(1)}, u32[]{:S(2)}) copy-start(f32[128]{0:T(128)S(1)} %fusion.170) | copy-start | bytes 1540
  40.7 21.0 copy-start.125
  40.8 19.3 copy-start.171
  40.8 19.3 copy-start.172
  40.8 19.5 copy-start.157
  41.8 18.3 copy-start.196
  41.8 18.3 copy-start.198
  41.9 20.8 copy-start.218
  41.9 20.8 copy-start.216
  41.9 25.8 copy-start.214
  41.9 32.1 copy-start.212
  41.9 32.1 copy-start.210
  41.9 32.1 copy-start.208
  43.9 63.1 %collective-permute-start.6 = (bf16[4,256,256]{2,0,1:T(4,128)(2,1)}, bf16[4,256,256]{2,0,1:T(4,128)(2,1)}, u32[]{:S(2)}, u32[]{:S(2)}) collective-permute-start(bf16[4,256,256]{2,0,1:T(4,128)(2,1)} %bitcast.75), channel_id=1, source_target_pairs={{0,4},{4,8},{8,12},{12,16},{16,20},{20,24},{24,28},{28,0},{1,5},{5... | collective-permute-start | bytes 1572872 | tf_op jit(solution)/shard_map/ppermute | solution.py:26
  45.8 64.4 %collective-permute-start.7 = (bf16[4,256,256]{2,0,1:T(4,128)(2,1)}, bf16[4,256,256]{2,0,1:T(4,128)(2,1)}, u32[]{:S(2)}, u32[]{:S(2)}) collective-permute-start(bf16[4,256,256]{2,0,1:T(4,128)(2,1)} %bitcast.78), channel_id=1, source_target_pairs={{0,28},{4,0},{8,4},{12,8},{16,12},{20,16},{24,20},{28,24},{1,29},{... | collective-permute-start | bytes 1572872 | tf_op jit(solution)/shard_map/ppermute | solution.py:26
  52.4 59.1 %collective-permute-start.8 = (bf16[4,256,256]{2,0,1:T(4,128)(2,1)}, bf16[4,256,256]{2,0,1:T(4,128)(2,1)}, u32[]{:S(2)}, u32[]{:S(2)}) collective-permute-start(bf16[4,256,256]{2,0,1:T(4,128)(2,1)} %bitcast.81), channel_id=1, source_target_pairs={{0,16},{4,20},{8,24},{12,28},{16,0},{20,4},{24,8},{28,12},{1,17},{... | collective-permute-start | bytes 1572872 | tf_op jit(solution)/shard_map/ppermute | solution.py:26
  54.4 63.2 %collective-permute-start.9 = (bf16[4,256,256]{2,0,1:T(4,128)(2,1)}, bf16[4,256,256]{2,0,1:T(4,128)(2,1)}, u32[]{:S(2)}, u32[]{:S(2)}) collective-permute-start(bf16[4,256,256]{2,0,1:T(4,128)(2,1)} %bitcast.84), channel_id=1, source_target_pairs={{0,16},{4,20},{8,24},{12,28},{16,0},{20,4},{24,8},{28,12},{1,17},{... | collective-permute-start | bytes 1572872 | tf_op jit(solution)/shard_map/ppermute | solution.py:26
  59.2 59.7 %collective-permute-start.10 = (bf16[4,256,256]{2,0,1:T(4,128)(2,1)}, bf16[4,256,256]{2,0,1:T(4,128)(2,1)}, u32[]{:S(2)}, u32[]{:S(2)}) collective-permute-start(bf16[4,256,256]{2,0,1:T(4,128)(2,1)} %bitcast.87), channel_id=1, source_target_pairs={{0,1},{1,2},{2,3},{3,0},{4,5},{5,6},{6,7},{7,4},{8,9},{9,10},{10,1... | collective-permute-start | bytes 1572872 | tf_op jit(solution)/shard_map/ppermute | solution.py:26
  63.0 29.4 copy-start.101
  76.6 28.4 copy-start.90
  107.0 16.2 collective-permute-start.11
  108.8 24.6 copy-start.129
  108.8 24.6 copy-start.42
  110.2 23.2 collective-permute-start
  111.5 26.7 collective-permute-start.1
  117.6 43.7 %collective-permute-start.2 = (bf16[4,256,256]{2,0,1:T(4,128)(2,1)S(1)}, bf16[4,256,256]{2,0,1:T(4,128)(2,1)S(1)}, u32[]{:S(2)}, u32[]{:S(2)}) collective-permute-start(bf16[4,256,256]{2,0,1:T(4,128)(2,1)S(1)} %bitcast.816), channel_id=1, source_target_pairs={{0,16},{4,20},{8,24},{12,28},{16,0},{20,4},{24,8},{28,12},{1,17},{... | collective-permute-start | bytes 1572872 | tf_op jit(solution)/shard_map/ppermute | solution.py:26
  118.9 52.2 %collective-permute-start.3 = (bf16[4,256,256]{2,0,1:T(4,128)(2,1)S(1)}, bf16[4,256,256]{2,0,1:T(4,128)(2,1)S(1)}, u32[]{:S(2)}, u32[]{:S(2)}) collective-permute-start(bf16[4,256,256]{2,0,1:T(4,128)(2,1)S(1)} %bitcast.815), channel_id=1, source_target_pairs={{0,16},{4,20},{8,24},{12,28},{16,0},{20,4},{24,8},{28,12},{1,17},{... | collective-permute-start | bytes 1572872 | tf_op jit(solution)/shard_map/ppermute | solution.py:26
  123.2 48.2 %collective-permute-start.4 = (bf16[4,256,256]{2,0,1:T(4,128)(2,1)S(1)}, bf16[4,256,256]{2,0,1:T(4,128)(2,1)S(1)}, u32[]{:S(2)}, u32[]{:S(2)}) collective-permute-start(bf16[4,256,256]{2,0,1:T(4,128)(2,1)S(1)} %bitcast.814), channel_id=1, source_target_pairs={{0,1},{1,2},{2,3},{3,0},{4,5},{5,6},{6,7},{7,4},{8,9},{9,10},{10,1... | collective-permute-start | bytes 1572872 | tf_op jit(solution)/shard_map/ppermute | solution.py:26
  133.4 38.3 collective-permute-start.5
  519.4 309.6 %copy-start.173 = (f32[768]{0:T(1024)S(1)}, f32[768]{0:T(1024)}, u32[]{:S(2)}) copy-start(f32[768]{0:T(1024)} %get-tuple-element.1224) | copy-start | bytes 9220
  1408.8 51.5 %copy-start.31 = (bf16[1,1664,256]{2,1,0:T(8,128)(2,1)S(1)}, bf16[1,1664,256]{2,1,0:T(8,128)(2,1)}, u32[]{:S(2)}) copy-start(bf16[1,1664,256]{2,1,0:T(8,128)(2,1)} %copy.409) | copy-start | bytes 2555908
  1495.0 85.2 %copy-start.142 = (f32[768]{0:T(1024)}, f32[768]{0:T(1024)S(1)}, u32[]{:S(2)}) copy-start(f32[768]{0:T(1024)S(1)} %get-tuple-element.2047) | copy-start | bytes 9220 | tf_op jit(solution)/shard_map/while
  1630.8 85.2 %copy-start.142 = (f32[768]{0:T(1024)}, f32[768]{0:T(1024)S(1)}, u32[]{:S(2)}) copy-start(f32[768]{0:T(1024)S(1)} %get-tuple-element.2047) | copy-start | bytes 9220 | tf_op jit(solution)/shard_map/while
  1766.5 85.2 %copy-start.142 = (f32[768]{0:T(1024)}, f32[768]{0:T(1024)S(1)}, u32[]{:S(2)}) copy-start(f32[768]{0:T(1024)S(1)} %get-tuple-element.2047) | copy-start | bytes 9220 | tf_op jit(solution)/shard_map/while
  1902.2 85.2 %copy-start.142 = (f32[768]{0:T(1024)}, f32[768]{0:T(1024)S(1)}, u32[]{:S(2)}) copy-start(f32[768]{0:T(1024)S(1)} %get-tuple-element.2047) | copy-start | bytes 9220 | tf_op jit(solution)/shard_map/while
  2038.2 51.4 %copy-start.29 = (bf16[1,1664,256]{2,1,0:T(8,128)(2,1)S(1)}, bf16[1,1664,256]{2,1,0:T(8,128)(2,1)}, u32[]{:S(2)}) copy-start(bf16[1,1664,256]{2,1,0:T(8,128)(2,1)} %copy-done.27) | copy-start | bytes 2555908
  2094.5 56.4 %copy-start.32 = (bf16[1,1664,256]{2,1,0:T(8,128)(2,1)S(1)}, bf16[1,1664,256]{2,1,0:T(8,128)(2,1)}, u32[]{:S(2)}) copy-start(bf16[1,1664,256]{2,1,0:T(8,128)(2,1)} %copy.409) | copy-start | bytes 2555908
  3074.8 1019.3 %collective-permute-start.12 = (bf16[4,256,256]{2,1,0:T(8,128)(2,1)}, bf16[4,256,256]{2,1,0:T(8,128)(2,1)}, u32[]{:S(2)}, u32[]{:S(2)}) collective-permute-start(bf16[4,256,256]{2,1,0:T(8,128)(2,1)} %get-tuple-element.1160), channel_id=1, source_target_pairs={{0,28},{4,0},{8,4},{12,8},{16,12},{20,16},{24,20},{28,24},{1,29},{... | collective-permute-start | bytes 1572872 | tf_op jit(solution)/shard_map/ppermute | solution.py:26
  3074.8 1022.3 %collective-permute-start.13 = (bf16[4,256,256]{2,1,0:T(8,128)(2,1)}, bf16[4,256,256]{2,1,0:T(8,128)(2,1)}, u32[]{:S(2)}, u32[]{:S(2)}) collective-permute-start(bf16[4,256,256]{2,1,0:T(8,128)(2,1)} %get-tuple-element.1159), channel_id=1, source_target_pairs={{0,4},{4,8},{8,12},{12,16},{16,20},{20,24},{24,28},{28,0},{1,5},{5... | collective-permute-start | bytes 1572872 | tf_op jit(solution)/shard_map/ppermute | solution.py:26
  3076.8 1024.7 %collective-permute-start.14 = (bf16[4,256,256]{2,1,0:T(8,128)(2,1)}, bf16[4,256,256]{2,1,0:T(8,128)(2,1)}, u32[]{:S(2)}, u32[]{:S(2)}) collective-permute-start(bf16[4,256,256]{2,1,0:T(8,128)(2,1)} %get-tuple-element.1158), channel_id=1, source_target_pairs={{0,16},{4,20},{8,24},{12,28},{16,0},{20,4},{24,8},{28,12},{1,17},{... | collective-permute-start | bytes 1572872 | tf_op jit(solution)/shard_map/ppermute | solution.py:26
  3076.8 1027.6 %collective-permute-start.15 = (bf16[4,256,256]{2,1,0:T(8,128)(2,1)}, bf16[4,256,256]{2,1,0:T(8,128)(2,1)}, u32[]{:S(2)}, u32[]{:S(2)}) collective-permute-start(bf16[4,256,256]{2,1,0:T(8,128)(2,1)} %get-tuple-element.1157), channel_id=1, source_target_pairs={{0,16},{4,20},{8,24},{12,28},{16,0},{20,4},{24,8},{28,12},{1,17},{... | collective-permute-start | bytes 1572872 | tf_op jit(solution)/shard_map/ppermute | solution.py:26
  3079.7 1027.5 %collective-permute-start.16 = (bf16[4,256,256]{2,1,0:T(8,128)(2,1)}, bf16[4,256,256]{2,1,0:T(8,128)(2,1)}, u32[]{:S(2)}, u32[]{:S(2)}) collective-permute-start(bf16[4,256,256]{2,1,0:T(8,128)(2,1)} %get-tuple-element.1156), channel_id=1, source_target_pairs={{0,3},{1,0},{2,1},{3,2},{4,7},{5,4},{6,5},{7,6},{8,11},{9,8},{10,9... | collective-permute-start | bytes 1572872 | tf_op jit(solution)/shard_map/ppermute | solution.py:26
  4090.5 237.3 %all-reduce.24.cloned.1.call-start = ((), (), s32[]{:S(2)}) async-start(), calls=%async_computation.1 | async-start | bytes 753664 | tf_op jit(solution)/shard_map/psum | solution.py:153
  4094.5 18.4 collective-permute-start.17
  4097.1 72.4 %collective-permute-start.18 = (bf16[4,256,256]{2,1,0:T(8,128)(2,1)}, bf16[4,256,256]{2,1,0:T(8,128)(2,1)}, u32[]{:S(2)}, u32[]{:S(2)}) collective-permute-start(bf16[4,256,256]{2,1,0:T(8,128)(2,1)} %get-tuple-element.1166), channel_id=1, source_target_pairs={{0,28},{4,0},{8,4},{12,8},{16,12},{20,16},{24,20},{28,24},{1,29},{... | collective-permute-start | bytes 1572872 | tf_op jit(solution)/shard_map/ppermute | solution.py:26
  4101.5 70.0 %collective-permute-start.19 = (bf16[4,256,256]{2,1,0:T(8,128)(2,1)}, bf16[4,256,256]{2,1,0:T(8,128)(2,1)}, u32[]{:S(2)}, u32[]{:S(2)}) collective-permute-start(bf16[4,256,256]{2,1,0:T(8,128)(2,1)} %get-tuple-element.1165), channel_id=1, source_target_pairs={{0,4},{4,8},{8,12},{12,16},{16,20},{20,24},{24,28},{28,0},{1,5},{5... | collective-permute-start | bytes 1572872 | tf_op jit(solution)/shard_map/ppermute | solution.py:26
  4104.5 71.2 %collective-permute-start.20 = (bf16[4,256,256]{2,1,0:T(8,128)(2,1)}, bf16[4,256,256]{2,1,0:T(8,128)(2,1)}, u32[]{:S(2)}, u32[]{:S(2)}) collective-permute-start(bf16[4,256,256]{2,1,0:T(8,128)(2,1)} %get-tuple-element.1164), channel_id=1, source_target_pairs={{0,16},{4,20},{8,24},{12,28},{16,0},{20,4},{24,8},{28,12},{1,17},{... | collective-permute-start | bytes 1572872 | tf_op jit(solution)/shard_map/ppermute | solution.py:26
  4107.2 82.7 %collective-permute-start.21 = (bf16[4,256,256]{2,1,0:T(8,128)(2,1)}, bf16[4,256,256]{2,1,0:T(8,128)(2,1)}, u32[]{:S(2)}, u32[]{:S(2)}) collective-permute-start(bf16[4,256,256]{2,1,0:T(8,128)(2,1)} %get-tuple-element.1163), channel_id=1, source_target_pairs={{0,16},{4,20},{8,24},{12,28},{16,0},{20,4},{24,8},{28,12},{1,17},{... | collective-permute-start | bytes 1572872 | tf_op jit(solution)/shard_map/ppermute | solution.py:26
  4112.9 79.8 %collective-permute-start.22 = (bf16[4,256,256]{2,1,0:T(8,128)(2,1)}, bf16[4,256,256]{2,1,0:T(8,128)(2,1)}, u32[]{:S(2)}, u32[]{:S(2)}) collective-permute-start(bf16[4,256,256]{2,1,0:T(8,128)(2,1)} %get-tuple-element.1162), channel_id=1, source_target_pairs={{0,3},{1,0},{2,1},{3,2},{4,7},{5,4},{6,5},{7,6},{8,11},{9,8},{10,9... | collective-permute-start | bytes 1572872 | tf_op jit(solution)/shard_map/ppermute | solution.py:26
  4169.5 26.0 collective-permute-start.23
  4241.9 52.9 %copy-start.40 = (f32[2,3,128,256]{3,2,1,0:T(8,128)S(1)}, f32[2,3,128,256]{3,2,1,0:T(8,128)}, u32[]{:S(2)}) copy-start(f32[2,3,128,256]{3,2,1,0:T(8,128)} %param.28) | copy-start | bytes 2359300
  4250.8 44.0 %copy-start.91 = (f32[3,128,256]{2,0,1:T(4,128)S(1)}, f32[3,128,256]{2,0,1:T(4,128)}, u32[]{:S(2)}) copy-start(f32[3,128,256]{2,0,1:T(4,128)} %slice.547) | copy-start | bytes 1179652
  4251.3 43.8 %copy-start.96 = (f32[3,128,256]{2,1,0:T(8,128)S(1)}, f32[3,128,256]{2,1,0:T(8,128)}, u32[]{:S(2)}) copy-start(f32[3,128,256]{2,1,0:T(8,128)} %get-tuple-element.1176) | copy-start | bytes 1179652
  4251.3 43.8 %copy-start.97 = (f32[3,128,256]{2,1,0:T(8,128)S(1)}, f32[3,128,256]{2,1,0:T(8,128)}, u32[]{:S(2)}) copy-start(f32[3,128,256]{2,1,0:T(8,128)} %get-tuple-element.1177) | copy-start | bytes 1179652
  4294.9 32.9 copy-start.98
  4295.1 32.7 copy-start.155
  4295.1 32.7 copy-start.156
  (382 other events, 2193.6 us)
Sparse Core Ops, SparseCore 0:
  10.8 81.9 all-gather.1
  4090.6 170.4 all-reduce.25
  4298.3 29.3 all-reduce.23
where the time goes:
time: 4400 us; the launch traced here: 4340 us
  other arithmetic  2680 us (61%)
  local copies, waits for them, and re-layouts  1190 us (27%)
  matrix products  271 us (6%)
  waiting for transfers between devices  84.9 us (2%)
  blocking collectives  64.1 us (1%)
    scatter-add x2, other arithmetic, micro_step(): jax.ops.segment_sum(vecedge_all.reshape(-1, 3, feat_width), flat_nbr, num...  1810 us
    gather x16, local copies, waits for them, and re-layouts, edge_inputs(): vec_edge = table_vec[:, nbr_blk].astype(f32)  289 us
    gather x16, local copies, waits for them, and re-layouts, edge_inputs(): value_edge = values[nbr_blk].astype(f32)  162 us
    gather x16, local copies, waits for them, and re-layouts, edge_inputs(): key_edge = keys[nbr_blk].astype(f32)  138 us
    dot_general x16, matrix products, edge_inputs(): jnp.einsum('kbr,rf->kbf', basis_blk, w_fvalue, preferred_element_type=f32)  126 us
    reduce_sum x8, other arithmetic, message_sum(): dir_gate[None] * unit_dir[..., None]  123 us
    scatter-add x2, other arithmetic, micro_step(): jax.ops.segment_sum(vedge_all.reshape(-1, 3 * feat_width), flat_nbr, num_...  112 us
    scatter-add x12, other arithmetic, micro_step(): returned = returned.at[:, send_rows[face_idx]].add(coming.astype(f32))  106 us
  transfers between devices with their start and end apart: 27, of which 6 were waited for; matrix products, arithmetic and copies ran while one was open for 28% of the time, Pallas kernels for 0%

commit v1 on v0

v1 whole, which is shorter than its diff:
```python
from functools import partial
import math

import jax
import jax.numpy as jnp
from jax import lax
from jax.experimental import pallas as pl
from jax.experimental.pallas import tpu as pltpu
from jax.sharding import PartitionSpec as P

HEADS = 8
NR = 32
FOLD = 4
STEP = 3

LANES = 128
ROWS = 256
UNIT = 256
BLOCK_SLOTS = 4
TILE = 128

norm_eps = 1e-05
cut_radius = 5.0
beta_one = 0.5
beta_two = 0.5
learn_rate = 0.05
decay_rate = 0.01
adam_eps = 1e-08

f32 = jnp.float32
bf16 = jnp.bfloat16
i32 = jnp.int32

VMEM_LIMIT = 60 * 1024 * 1024


def dot_nn(left, right):
    return lax.dot_general(left, right, (((1,), (0,)), ((), ())), preferred_element_type=f32)


def dot_nt(left, right):
    return lax.dot_general(left, right, (((1,), (1,)), ((), ())), preferred_element_type=f32)


def dot_tn(left, right):
    return lax.dot_general(left, right, (((0,), (0,)), ((), ())), preferred_element_type=f32)


def lane_mean(block):
    return jnp.sum(block, axis=-1, keepdims=True) * (1.0 / block.shape[-1])


def normalise(block):
    centered = block - lane_mean(block)
    spread = lax.rsqrt(lane_mean(centered * centered) + norm_eps)
    return centered * spread, spread


def norm_kernel(x_ref, vec_ref, *own_refs):
    for micro, own_ref in enumerate(own_refs):
        own_ref[0] = normalise(x_ref[micro])[0].astype(bf16)
        own_ref[1:] = vec_ref[micro].astype(bf16)


def prep_kernel(
    block_of,
    buckets,
    nbr_ref,
    mask_ref,
    geom_ref,
    list_ref,
    table_ref,
    units_ref,
    feat,
    place,
    count_vec,
    count_sc,
    packed,
    sem,
):
    micro = pl.program_id(0)
    slots, atoms = nbr_ref.shape[1], nbr_ref.shape[2]
    blocks = slots // BLOCK_SLOTS
    wide = BLOCK_SLOTS * atoms

    @pl.when(micro == 0)
    def _():
        feat[...] = jnp.zeros_like(feat)

    source = nbr_ref[0]
    live = mask_ref[0] > 0
    halo_at = source - atoms
    list_row = halo_at >> 7
    list_lane = halo_at & (LANES - 1)
    atom_in = source
    block_id = jnp.zeros_like(source)
    for row in range(list_ref.shape[1]):
        table = jnp.broadcast_to(list_ref[0, row : row + 1, :], (slots, atoms))
        picked = jnp.take_along_axis(table, list_lane, axis=1)
        here = list_row == row
        atom_in = jnp.where(here, picked, atom_in)
        block_id = jnp.where(here, block_of[row], block_id)
    entry = block_id * atoms + atom_in
    bucket = entry >> 8
    low = ((entry & (ROWS - 1)) + 1).astype(f32)
    atom_id = (lax.broadcasted_iota(i32, (slots, atoms), 1) + 1).astype(f32)
    live_float = live.astype(f32)

    comps = [geom_ref[0, axis] for axis in range(3)]
    radius = jnp.sqrt(comps[0] * comps[0] + comps[1] * comps[1] + comps[2] * comps[2])
    units = [comp / radius for comp in comps]
    cut = 0.5 * (jnp.cos(math.pi * radius / cut_radius) + 1.0) * live_float
    cut_high = cut.astype(bf16).astype(f32)
    cut_low = cut - cut_high
    decayed = jnp.exp(-(5.0 / cut_radius) * radius)
    start_value = math.exp(-cut_radius)
    ramp = lax.broadcasted_iota(i32, (NR, 1), 0).astype(f32) / float(NR - 1)
    centers = start_value * (1.0 - ramp) + ramp
    width_coef = (2.0 / NR * (1.0 - start_value)) ** (-2)
    extras = [live_float, low, atom_id, cut_high, cut_low] + units
    zeros = jnp.zeros((16 - len(extras), atoms), f32)
    for slot in range(slots):
        gap = decayed[slot : slot + 1, :] - centers
        basis = cut[slot : slot + 1, :] * jnp.exp(-width_coef * gap * gap)
        feat[slot, 0:NR, :] = basis.astype(bf16)
        rows = [extra[slot : slot + 1, :] for extra in extras] + [zeros]
        feat[slot, NR : NR + 16, :] = jnp.concatenate(rows, axis=0).astype(bf16)

    members = [jnp.where(live & (bucket == b), 1.0, 0.0) for b in range(buckets)]
    lane_from = lax.broadcasted_iota(i32, (atoms, 2 * atoms), 0)
    lane_to = lax.broadcasted_iota(i32, (atoms, 2 * atoms), 1)
    before = jnp.where((lane_from < lane_to) | (lane_to >= atoms), 1.0, 0.0).astype(bf16)
    slot_to = lax.broadcasted_iota(i32, (slots, slots), 0)
    slot_from = lax.broadcasted_iota(i32, (slots, slots), 1)
    same = (slot_to // BLOCK_SLOTS) == (slot_from // BLOCK_SLOTS)
    earlier = jnp.where(same & (slot_from < slot_to), 1.0, 0.0).astype(bf16)
    block_row = lax.broadcasted_iota(i32, (blocks, slots), 0)
    block_slot = lax.broadcasted_iota(i32, (blocks, slots), 1)
    gather_block = jnp.where(block_slot // BLOCK_SLOTS == block_row, 1.0, 0.0).astype(bf16)
    lane = lax.broadcasted_iota(i32, (blocks, LANES), 1)
    rank = jnp.zeros((slots, atoms), f32)
    counts = jnp.zeros((blocks, LANES), f32)
    for b in range(buckets):
        sums = dot_nn(members[b].astype(bf16), before)
        row_total = sums[:, atoms:].astype(bf16)
        offset = sums[:, :atoms] + dot_nn(earlier, row_total)
        rank = jnp.where(members[b] > 0.0, offset, rank)
        counts = jnp.where(lane == b, dot_nn(gather_block, row_total), counts)
    place[...] = jnp.where(live, bucket * 1024 + rank.astype(i32), -1)
    count_vec[...] = counts.astype(i32)
    copy = pltpu.make_async_copy(count_vec, count_sc, sem)
    copy.start()
    copy.wait()

    def block_body(b, block, at):
        number = count_sc[block, b]
        first = block * BLOCK_SLOTS
        places = jnp.concatenate(
            [place[pl.ds(first + t, 1), :] for t in range(BLOCK_SLOTS)], axis=1
        )

        def tile_body(tile, carry):
            feats = jnp.concatenate([feat[first + t] for t in range(BLOCK_SLOTS)], axis=1)
            wanted = lax.broadcasted_iota(i32, (TILE, wide), 0) + (b * 1024 + tile * TILE)
            pick = jnp.where(places == wanted, 1.0, 0.0).astype(bf16)
            packed[pl.ds(pl.multiple_of(at + tile * TILE, 8), TILE), :] = dot_nt(pick, feats)
            return carry

        lax.fori_loop(0, (number + (TILE - 1)) >> 7, tile_body, 0)
        return at + (((number + 7) >> 3) << 3)

    base = jnp.int32(0)
    for b in range(buckets):
        end = lax.fori_loop(0, blocks, partial(block_body, b), base)
        packed[pl.ds(pl.multiple_of(end, 8), UNIT), :] = jnp.zeros((UNIT, LANES), f32)
        held = (end - base + (UNIT - 1)) >> 8
        units_ref[micro, b] = held
        base = base + held * UNIT

    def cast_body(unit, carry):
        at = pl.ds(pl.multiple_of(unit * UNIT, UNIT), UNIT)
        table_ref[0, at, :] = packed[at, :].astype(bf16)
        return carry

    lax.fori_loop(0, base >> 8, cast_body, 0)


Q_AT, K_AT, V_AT, VEC_AT, O_AT, DK_AT, DV_AT = 0, 512, 1024, 2560, 4096, 5632, 5696
W_Q, W_K, W_V, W_VEC, W_O = 0, 1, 2, 5, 8


def edge_kernel(
    micro,
    domains,
    buckets,
    atoms,
    feat_width,
    has_prior,
    *refs,
):
    refs = list(refs)
    units_ref, count_ref, table_ref, x_ref, vec_ref, cotx_ref, cotv_ref, own_ref = refs[:8]
    halo_refs = refs[8 : 8 + domains - 1]
    at = 8 + domains - 1
    w_ref, v_ref = refs[at : at + 2]
    at += 2
    if has_prior:
        prior_m_ref, prior_v_ref = refs[at : at + 2]
        at += 2
    outx_ref, outv_ref, gown_ref = refs[at : at + 3]
    at += 3
    back_refs = refs[at : at + domains - 1]
    at += domains - 1
    gm_ref, gv_ref = refs[at : at + 2]
    at += 2
    (
        wide_w,
        wb,
        wd,
        norm_table,
        tab,
        acc,
        atom_tab,
        dir_tab,
        proj,
        go,
        agg,
        gwd,
        heads,
        hit,
        gath,
        per_atom,
        filt,
        cutb,
        pair,
        pair_sum,
        dedge,
        dfilt,
        msg,
    ) = refs[at:]

    def vector(index):
        both = [v_ref[2 * index + half : 2 * index + half + 1, :].astype(f32) for half in range(2)]
        return jnp.concatenate(both, axis=1)

    wide_w[...] = w_ref[...].astype(f32)

    def weight_block(first, stride, column, rows):
        halves = [
            wide_w[pl.ds(first + 2 * column + half, rows, stride=stride), :] for half in range(2)
        ]
        return jnp.concatenate(halves, axis=1)

    for slot, first, stride, count in (
        (W_Q, Q_AT, 2, 1),
        (W_K, K_AT, 2, 1),
        (W_V, V_AT, 6, 3),
        (W_VEC, VEC_AT, 6, 3),
        (W_O, O_AT, 6, 3),
    ):
        for column in range(count):
            wb[slot + column] = weight_block(first, stride, column, ROWS).astype(bf16)
    bias_row = lax.broadcasted_iota(i32, (LANES - NR, 1), 0) == 0
    for column in range(4):
        if column == 0:
            block = weight_block(DK_AT, 2, 0, NR)
        else:
            block = weight_block(DV_AT, 6, column - 1, NR)
        bias = jnp.where(bias_row, vector(10 + column), 0.0)
        cols = slice(column * ROWS, (column + 1) * ROWS)
        wd[:, cols] = (jnp.concatenate([block, bias], axis=0) * 0.5).astype(bf16)

    head_from = lax.broadcasted_iota(i32, (ROWS, ROWS), 0) // (feat_width // HEADS)
    head_to = lax.broadcasted_iota(i32, (ROWS, ROWS), 1) // (feat_width // HEADS)
    heads[...] = jnp.where(head_from == head_to, 0.5, 0.0).astype(bf16)

    gain = vector(0)
    shift = vector(1)
    own_hat, unused = normalise(x_ref[0])
    for domain in range(2 * buckets):
        rows = slice(domain * atoms, (domain + 1) * atoms)
        here = slice((domain % 2) * atoms, (domain % 2 + 1) * atoms)
        if domain == 0:
            norm_table[rows, :] = (own_hat * gain + shift).astype(bf16)
        elif domain < domains:
            hat = halo_refs[domain - 1][0].astype(f32)
            norm_table[rows, :] = (hat * gain + shift).astype(bf16)
        else:
            norm_table[rows, :] = jnp.zeros((atoms, feat_width), bf16)
        for axis in range(3):
            cols = slice((4 + axis) * ROWS, (5 + axis) * ROWS)
            if domain < domains:
                block = own_ref[1 + axis] if domain == 0 else halo_refs[domain - 1][1 + axis]
            else:
                block = jnp.zeros((atoms, feat_width), bf16)
            tab[domain // 2, here, cols] = block
    for b in range(buckets):
        rows = slice(b * ROWS, (b + 1) * ROWS)
        for column in range(4):
            cols = slice(column * ROWS, (column + 1) * ROWS)
            made = dot_nn(norm_table[rows, :], wb[W_K + column]) + vector(3 + column)
            tab[b, :, cols] = made.astype(bf16)

    live = (lax.broadcasted_iota(i32, (atoms, 1), 0) < count_ref[micro, 0]).astype(f32)
    query = dot_nn(norm_table[0:atoms, :], wb[W_Q]) + vector(2)
    atom_tab[:, 0:ROWS] = query.astype(bf16)
    vec_low = own_ref[1:].reshape(3 * atoms, feat_width)
    for part in range(3):
        proj[part] = dot_nn(vec_low, wb[W_VEC + part])
    parts = [slice(axis * atoms, (axis + 1) * atoms) for axis in range(3)]
    cot_x = cotx_ref[0] * live
    vec_dot = jnp.zeros((atoms, feat_width), f32)
    go_one = jnp.zeros((atoms, feat_width), f32)
    for axis in range(3):
        cot_v = cotv_ref[0, axis] * live
        vec_dot += proj[0, parts[axis], :] * proj[1, parts[axis], :]
        go_one += proj[2, parts[axis], :] * cot_v
        low = cot_v.astype(bf16)
        dir_tab[parts[axis], :] = low
        atom_tab[:, (2 + axis) * ROWS : (3 + axis) * ROWS] = low
    go[0] = go_one.astype(bf16)
    go[1] = (vec_dot * cot_x).astype(bf16)
    go[2] = cot_x.astype(bf16)
    g_agg = dot_nt(go[0], wb[W_O])
    for part in range(1, 3):
        g_agg += dot_nt(go[part], wb[W_O + part])
    atom_tab[:, ROWS : 2 * ROWS] = g_agg.astype(bf16)

    agg[...] = jnp.zeros_like(agg)
    gwd[...] = jnp.zeros_like(gwd)
    for b in range(buckets):
        acc[b] = jnp.zeros((ROWS, 7 * ROWS), f32)

    lane_row = lax.broadcasted_iota(i32, (UNIT, ROWS), 1).astype(f32) + 1.0
    lane_atom = lax.broadcasted_iota(i32, (UNIT, LANES), 1).astype(f32) + 1.0
    sub_row = lax.broadcasted_iota(i32, (ROWS, UNIT), 0).astype(f32) + 1.0
    sub_atom = lax.broadcasted_iota(i32, (atoms, UNIT), 0).astype(f32) + 1.0

    def unit_body(b, first, unit, carry):
        rows = pl.ds(pl.multiple_of((first + unit) * UNIT, UNIT), UNIT)
        low = table_ref[0, rows, :]
        full = low.astype(f32)
        turned = full.T

        def column(index):
            return full[:, NR + index : NR + index + 1]

        def across(index):
            return turned[NR + index : NR + index + 1, :]

        hit[...] = jnp.where(column(1) == lane_row, 1.0, 0.0).astype(bf16)
        cutb[...] = jnp.broadcast_to(column(3) + column(4), (UNIT, LANES))
        atom_hit = column(2) == lane_atom
        atom_one = jnp.where(atom_hit, 1.0, 0.0).astype(bf16)
        for block in range(7):
            cols = slice(block * ROWS, (block + 1) * ROWS)
            gath[:, cols] = dot_nn(hit[...], tab[b, :, cols])
        for block in range(5):
            cols = slice(block * ROWS, (block + 1) * ROWS)
            per_atom[:, cols] = dot_nn(atom_one, atom_tab[:, cols])
        along = jnp.concatenate(
            [jnp.where(atom_hit, column(5 + axis), 0.0).astype(bf16) for axis in range(3)],
            axis=1,
        )
        per_atom[:, 5 * ROWS :] = dot_nn(along, dir_tab[...])
        for block in range(4):
            cols = slice(block * ROWS, (block + 1) * ROWS)
            filt[:, cols] = dot_nn(low, wd[:, cols])

        def part(ref, block, here, half):
            start = block * ROWS + half * LANES
            return ref[here, start : start + LANES]

        def gate(here, block, half):
            value = part(filt, block, here, half)
            lift = 1.0 + jnp.tanh(value)
            return lift, value * lift

        def first_stage(step, carry):
            here = pl.ds(pl.multiple_of(step * 16, 16), 16)
            there = pl.ds(pl.multiple_of(UNIT + step * 16, 16), 16)
            for half in range(2):
                cols = slice(half * LANES, (half + 1) * LANES)
                silu_k = gate(here, 0, half)[1]
                silu_x = gate(here, 1, half)[1]
                score = part(per_atom, 0, here, half) * part(gath, 0, here, half) * silu_k
                back = part(per_atom, 1, here, half) * part(gath, 1, here, half) * silu_x
                pair[here, cols] = score.astype(bf16)
                pair[there, cols] = back.astype(bf16)
            return carry

        lax.fori_loop(0, UNIT // 16, first_stage, 0, unroll=2)
        pair_sum[...] = dot_nn(pair[...], heads[...])

        def second_stage(step, carry):
            here = pl.ds(pl.multiple_of(step * 16, 16), 16)
            there = pl.ds(pl.multiple_of(UNIT + step * 16, 16), 16)
            cut = cutb[here, :]
            for half in range(2):
                cols = slice(half * LANES, (half + 1) * LANES)

                def put(ref, block, value):
                    start = block * ROWS + half * LANES
                    ref[here, start : start + LANES] = value.astype(bf16)

                half_score = pair_sum[here, cols]
                lift = 1.0 + jnp.tanh(half_score)
                silu_s = half_score * lift
                attention = silu_s * cut
                dscore = pair_sum[there, cols] * cut * (lift + silu_s * (2.0 - lift))

                query_e = part(per_atom, 0, here, half)
                key_e = part(gath, 0, here, half)
                lift, silu = gate(here, 0, half)
                scaled = dscore * query_e
                put(dedge, 0, scaled * silu)
                put(dfilt, 0, scaled * key_e * (lift + silu * (2.0 - lift)))
                put(msg, 4, dscore * key_e * silu)

                value_e = part(gath, 1, here, half)
                lift, silu = gate(here, 1, half)
                down = part(per_atom, 1, here, half) * attention
                put(dedge, 1, down * silu)
                put(dfilt, 1, down * value_e * (lift + silu * (2.0 - lift)))
                put(msg, 0, value_e * silu * attention)

                value_e = part(gath, 2, here, half)
                lift, silu = gate(here, 2, half)
                gated = value_e * silu
                down = jnp.zeros_like(gated)
                for axis in range(3):
                    vec_e = part(gath, 4 + axis, here, half)
                    cot_e = part(per_atom, 2 + axis, here, half)
                    down += cot_e * vec_e
                    put(msg, 1 + axis, vec_e * gated)
                    put(dedge, 4 + axis, cot_e * gated)
                put(dedge, 2, down * silu)
                put(dfilt, 2, down * value_e * (lift + silu * (2.0 - lift)))

                value_e = part(gath, 3, here, half)
                lift, silu = gate(here, 3, half)
                down = part(per_atom, 5, here, half)
                put(dedge, 3, down * silu)
                put(dfilt, 3, down * value_e * (lift + silu * (2.0 - lift)))
                put(msg, 5, value_e * silu)
            return carry

        lax.fori_loop(0, UNIT // 16, second_stage, 0, unroll=2)

        hit_t = jnp.where(across(1) == sub_row, 1.0, 0.0).astype(bf16)
        for block in range(7):
            cols = slice(block * ROWS, (block + 1) * ROWS)
            acc[b, :, cols] += dot_nn(hit_t, dedge[:, cols])
        atom_hit_t = across(2) == sub_atom
        atom_one_t = jnp.where(atom_hit_t, 1.0, 0.0).astype(bf16)
        for block in (0, 4):
            cols = slice(block * ROWS, (block + 1) * ROWS)
            agg[:, cols] += dot_nn(atom_one_t, msg[:, cols])
        for axis in range(3):
            cols = slice((1 + axis) * ROWS, (2 + axis) * ROWS)
            along_t = jnp.where(atom_hit_t, across(5 + axis), 0.0).astype(bf16)
            agg[:, cols] += dot_nn(atom_one_t, msg[:, cols]) + dot_nn(
                along_t, msg[:, 5 * ROWS :]
            )
        feats_t = turned.astype(bf16)
        for block in range(4):
            cols = slice(block * ROWS, (block + 1) * ROWS)
            gwd[:, cols] += dot_nn(feats_t, dfilt[:, cols])
        return carry

    first = jnp.int32(0)
    for b in range(buckets):
        number = units_ref[micro, b]
        lax.fori_loop(0, number, partial(unit_body, b, first), 0)
        first = first + number

    agg_low = agg[:, 0:ROWS].astype(bf16)
    outs = [dot_nn(agg_low, wb[W_O + part]) + vector(7 + part) for part in range(3)]
    outx_ref[...] = x_ref[0] + (vec_dot * outs[1] + outs[2]) * live
    g_dot = cot_x * outs[1]
    for axis in range(3):
        rows = parts[axis]
        vec_agg = agg[:, (1 + axis) * ROWS : (2 + axis) * ROWS]
        outv_ref[axis] = vec_ref[0, axis] + (proj[2, rows, :] * outs[0] + vec_agg) * live
        proj[2, rows, :] = cotv_ref[0, axis] * live * outs[0]
        held = proj[0, rows, :]
        proj[0, rows, :] = g_dot * proj[1, rows, :]
        proj[1, rows, :] = g_dot * held

    def put_grad(first, stride, column, rows, value):
        for half in range(2):
            at = pl.ds(first + 2 * column + half, rows, stride=stride)
            gm_ref[at, :] = value[:, half * LANES : (half + 1) * LANES]

    def put_vector(index, value):
        for half in range(2):
            row = 2 * index + half
            gv_ref[row : row + 1, :] = value[:, half * LANES : (half + 1) * LANES]

    def column_sum(value):
        return jnp.sum(value.astype(f32), axis=0, keepdims=True)

    put_vector(0, jnp.zeros((1, ROWS), f32))
    put_vector(1, jnp.zeros((1, ROWS), f32))
    g_vec = jnp.zeros((3 * atoms, feat_width), f32)
    for part in range(3):
        put_grad(O_AT, 6, part, ROWS, dot_tn(agg_low, go[part]))
        put_vector(7 + part, column_sum(go[part]))
        gp = proj[part].astype(bf16)
        put_grad(VEC_AT, 6, part, ROWS, dot_tn(vec_low, gp))
        g_vec += dot_nt(gp, wb[W_VEC + part])

    g_query = agg[:, 4 * ROWS : 5 * ROWS].astype(bf16)
    put_grad(Q_AT, 2, 0, ROWS, dot_tn(norm_table[0:atoms, :], g_query))
    put_vector(2, column_sum(g_query))
    g_norm = dot_nt(g_query, wb[W_Q])

    sums = [jnp.zeros((ROWS, ROWS), f32) for column in range(4)]
    biases = [jnp.zeros((1, ROWS), f32) for column in range(4)]
    for b in range(buckets):
        rows = slice(b * ROWS, (b + 1) * ROWS)
        g_table = jnp.zeros((ROWS, ROWS), f32)
        for column in range(4):
            low = acc[b, :, column * ROWS : (column + 1) * ROWS].astype(bf16)
            sums[column] += dot_tn(norm_table[rows, :], low)
            biases[column] += column_sum(low)
            g_table += dot_nt(low, wb[W_K + column])
        for half in range(2):
            domain = 2 * b + half
            if domain >= domains:
                continue
            here = slice(half * atoms, (half + 1) * atoms)
            if domain == 0:
                gown_ref[0] = g_table[here, :] + g_norm
            else:
                back_refs[domain - 1][0] = g_table[here, :].astype(bf16)
            for axis in range(3):
                block = acc[b, here, (4 + axis) * ROWS : (5 + axis) * ROWS]
                if domain == 0:
                    gown_ref[1 + axis] = block + g_vec[parts[axis], :]
                else:
                    back_refs[domain - 1][1 + axis] = block.astype(bf16)
    for column in range(4):
        if column == 0:
            put_grad(K_AT, 2, 0, ROWS, sums[column])
        else:
            put_grad(V_AT, 6, column - 1, ROWS, sums[column])
        put_vector(3 + column, biases[column])
        cols = slice(column * ROWS, (column + 1) * ROWS)
        block = gwd[0:NR, cols] * 0.5
        if column == 0:
            put_grad(DK_AT, 2, 0, NR, block)
        else:
            put_grad(DV_AT, 6, column - 1, NR, block)
        put_vector(10 + column, gwd[NR : NR + 1, cols] * 0.5)
    if has_prior:
        gm_ref[...] += prior_m_ref[...]
        gv_ref[...] += prior_v_ref[...]


def close_kernel(domains, x_ref, cotx_ref, cotv_ref, gown_ref, *refs):
    back_refs = refs[: domains - 1]
    v_ref, gx_ref, gvec_ref, gln_ref = refs[domains - 1 :]
    total = [gown_ref[part] for part in range(4)]
    for back_ref in back_refs:
        for part in range(4):
            total[part] = total[part] + back_ref[part].astype(f32)
    gain = jnp.concatenate([v_ref[half : half + 1, :].astype(f32) for half in range(2)], axis=1)
    hat, spread = normalise(x_ref[0])
    for at, value in ((0, total[0] * hat), (2, total[0])):
        summed = jnp.sum(value, axis=0, keepdims=True)
        for half in range(2):
            gln_ref[at + half : at + half + 1, :] = summed[:, half * LANES : (half + 1) * LANES]
    g_hat = total[0] * gain
    g_x = spread * (g_hat - lane_mean(g_hat) - hat * lane_mean(g_hat * hat))
    gx_ref[...] = cotx_ref[0] + g_x
    for axis in range(3):
        gvec_ref[axis] = cotv_ref[0, axis] + total[1 + axis]


def adam_update(weight, grad, first, second):
    first_new = beta_one * first + (1.0 - beta_one) * grad
    second_new = beta_two * second + (1.0 - beta_two) * grad * grad
    first_hat = first_new / (1.0 - beta_one**STEP)
    second_hat = second_new / (1.0 - beta_two**STEP)
    weight_new = weight - learn_rate * (
        first_hat / (jnp.sqrt(second_hat) + adam_eps) + decay_rate * weight
    )
    return (weight_new, first_new, second_new)


def from_behind(shard, axis, by):
    length = lax.axis_size(axis)
    return lax.ppermute(shard, axis, [(i, (i + by) % length) for i in range(length)])


def micro_block(shape, micro):
    rest = tuple(shape[1:])
    zeros = (0,) * len(rest)
    return pl.BlockSpec((1,) + rest, lambda i: (micro,) + zeros)


def shards(
    x_in,
    vec_in,
    cot_x,
    cot_vec,
    mats,
    vecs,
    mats_first,
    mats_second,
    vecs_first,
    vecs_second,
    atom_count,
    neighbours,
    edge_mask,
    edge_vec,
    send_list,
):
    micros, atoms, width = x_in.shape
    slots = neighbours.shape[1]
    halo = send_list.shape[-1]
    per_face = halo // LANES
    cells, depth = lax.axis_size("cells"), lax.axis_size("depth")
    faces = [("cells", 1), ("cells", -1), ("cells", FOLD), ("cells", -FOLD), ("depth", 1), ("depth", -1)]
    sizes = {"cells": cells, "depth": depth}
    sources = []
    face_source = []
    for axis, by in faces:
        key = (axis, by % sizes[axis])
        if key not in sources:
            sources.append(key)
        face_source.append(sources.index(key))
    domains = 1 + len(sources)
    buckets = (domains * atoms + ROWS - 1) // ROWS
    block_of = [1 + face_source[row // per_face] for row in range(6 * per_face)]

    whole = pl.BlockSpec(memory_space=pltpu.VMEM)
    scalars = pl.BlockSpec(memory_space=pltpu.SMEM)

    lists = [None] * 6
    for index, (axis, by) in enumerate(sources):
        mine = [face for face in range(6) if face_source[face] == index]
        sent = jnp.stack([send_list[:, face] for face in mine], axis=1)
        got = from_behind(sent, axis, by)
        for order, face in enumerate(mine):
            lists[face] = got[:, order]
    list_rows = jnp.stack(lists, axis=1).reshape(micros, 6 * per_face, LANES)

    own = pl.pallas_call(
        norm_kernel,
        out_shape=tuple(
            jax.ShapeDtypeStruct((4, atoms, width), bf16) for micro in range(micros)
        ),
        in_specs=[whole] * 2,
        out_specs=[whole] * micros,
        name="norm",
    )(x_in, vec_in)

    halos = [[from_behind(own[micro], axis, by) for axis, by in sources] for micro in range(micros)]

    mats_rows = mats.reshape(-1, LANES)
    w_all = lax.all_gather(mats_rows.astype(bf16), "cells", axis=0, tiled=True)
    v_all = lax.all_gather(vecs.astype(bf16), "cells", axis=0, tiled=True).reshape(-1, LANES)
    w_rows, v_rows = w_all.shape[0], v_all.shape[0]

    limit = slots * atoms + buckets * (slots // BLOCK_SLOTS) * 8 + buckets * UNIT
    capacity = (limit + UNIT - 1) // UNIT * UNIT

    def by_micro(shape):
        zeros = (0,) * (len(shape) - 1)
        return pl.BlockSpec((1,) + tuple(shape[1:]), lambda i: (i,) + zeros)

    edge_table, units = pl.pallas_call(
        partial(prep_kernel, block_of, buckets),
        out_shape=(
            jax.ShapeDtypeStruct((micros, capacity, LANES), bf16),
            jax.ShapeDtypeStruct((micros, buckets), i32),
        ),
        grid=(micros,),
        in_specs=[
            by_micro(neighbours.shape),
            by_micro(edge_mask.shape),
            by_micro(edge_vec.shape),
            by_micro(list_rows.shape),
        ],
        out_specs=[by_micro((micros, capacity, LANES)), scalars],
        scratch_shapes=[
            pltpu.VMEM((slots, LANES, LANES), bf16),
            pltpu.VMEM((slots, atoms), i32),
            pltpu.VMEM((slots // BLOCK_SLOTS, LANES), i32),
            pltpu.SMEM((slots // BLOCK_SLOTS, LANES), i32),
            pltpu.VMEM((capacity + UNIT, LANES), f32),
            pltpu.SemaphoreType.DMA(()),
        ],
        compiler_params=pltpu.CompilerParams(vmem_limit_bytes=VMEM_LIMIT),
        name="prep",
    )(neighbours, edge_mask, edge_vec, list_rows)

    grads = []
    outs = []
    for micro in range(micros):
        prior = list(grads)
        operands = [
            units,
            atom_count,
            edge_table,
            x_in,
            vec_in,
            cot_x,
            cot_vec,
            own[micro],
            *halos[micro],
            w_all,
            v_all,
            *prior,
        ]
        specs = (
            [scalars, scalars]
            + [
                micro_block(array.shape, micro)
                for array in (edge_table, x_in, vec_in, cot_x, cot_vec)
            ]
            + [whole] * (1 + len(sources) + 2 + len(prior))
        )
        shapes = (
            [
                jax.ShapeDtypeStruct((atoms, width), f32),
                jax.ShapeDtypeStruct((3, atoms, width), f32),
                jax.ShapeDtypeStruct((4, atoms, width), f32),
            ]
            + [jax.ShapeDtypeStruct((4, atoms, width), bf16)] * len(sources)
            + [
                jax.ShapeDtypeStruct((w_rows, LANES), f32),
                jax.ShapeDtypeStruct((v_rows, LANES), f32),
            ]
        )
        results = pl.pallas_call(
            partial(edge_kernel, micro, domains, buckets, atoms, width, bool(prior)),
            out_shape=tuple(shapes),
            grid=(1,),
            in_specs=specs,
            out_specs=[whole] * len(shapes),
            scratch_shapes=[
                pltpu.VMEM((w_rows, LANES), f32),
                pltpu.VMEM((11, ROWS, ROWS), bf16),
                pltpu.VMEM((LANES, 4 * ROWS), bf16),
                pltpu.VMEM((buckets * ROWS, ROWS), bf16),
                pltpu.VMEM((buckets, ROWS, 7 * ROWS), bf16),
                pltpu.VMEM((buckets, ROWS, 7 * ROWS), f32),
                pltpu.VMEM((atoms, 5 * ROWS), bf16),
                pltpu.VMEM((3 * atoms, ROWS), bf16),
                pltpu.VMEM((3, 3 * atoms, ROWS), f32),
                pltpu.VMEM((3, atoms, ROWS), bf16),
                pltpu.VMEM((atoms, 5 * ROWS), f32),
                pltpu.VMEM((LANES, 4 * ROWS), f32),
                pltpu.VMEM((ROWS, ROWS), bf16),
                pltpu.VMEM((UNIT, ROWS), bf16),
                pltpu.VMEM((UNIT, 7 * ROWS), f32),
                pltpu.VMEM((UNIT, 6 * ROWS), f32),
                pltpu.VMEM((UNIT, 4 * ROWS), f32),
                pltpu.VMEM((UNIT, LANES), f32),
                pltpu.VMEM((2 * UNIT, ROWS), bf16),
                pltpu.VMEM((2 * UNIT, ROWS), f32),
                pltpu.VMEM((UNIT, 7 * ROWS), bf16),
                pltpu.VMEM((UNIT, 4 * ROWS), bf16),
                pltpu.VMEM((UNIT, 6 * ROWS), bf16),
            ],
            compiler_params=pltpu.CompilerParams(vmem_limit_bytes=VMEM_LIMIT),
            name="edges",
        )(*operands)
        outs.append(results)
        grads = list(results[-2:])

    closed = []
    for micro in range(micros):
        back = outs[micro][3 : 3 + len(sources)]
        returned = [
            from_behind(block, axis, -by) for block, (axis, by) in zip(back, sources)
        ]
        closed.append(
            pl.pallas_call(
                partial(close_kernel, domains),
                out_shape=(
                    jax.ShapeDtypeStruct((atoms, width), f32),
                    jax.ShapeDtypeStruct((3, atoms, width), f32),
                    jax.ShapeDtypeStruct((4, LANES), f32),
                ),
                grid=(1,),
                in_specs=[
                    micro_block(array.shape, micro) for array in (x_in, cot_x, cot_vec)
                ]
                + [whole] * (2 + len(sources)),
                out_specs=[whole] * 3,
                name="close",
            )(x_in, cot_x, cot_vec, outs[micro][2], *returned, v_all)
        )

    grad_m, grad_v = grads
    grad_norm = closed[0][2]
    for micro in range(1, micros):
        grad_norm = grad_norm + closed[micro][2]
    sum_mats = lax.psum_scatter(grad_m, "cells", scatter_dimension=0, tiled=True)
    sum_mats = lax.psum(sum_mats, "depth").reshape(-1)
    grad_v = jnp.concatenate([grad_norm, grad_v[4:]], axis=0)
    sum_vecs = lax.psum(grad_v, ("cells", "depth")).reshape(-1)
    sum_vecs = lax.dynamic_slice_in_dim(
        sum_vecs, lax.axis_index("cells") * vecs.shape[0], vecs.shape[0]
    )
    new_mats, mats_one, mats_two = adam_update(mats, sum_mats, mats_first, mats_second)
    new_vecs, vecs_one, vecs_two = adam_update(vecs, sum_vecs, vecs_first, vecs_second)
    return (
        jnp.stack([result[0] for result in outs]),
        jnp.stack([result[1] for result in outs]),
        jnp.stack([result[0] for result in closed]),
        jnp.stack([result[1] for result in closed]),
        sum_mats,
        sum_vecs,
        new_mats,
        new_vecs,
        mats_one,
        mats_two,
        vecs_one,
        vecs_two,
    )


def solution(mesh):
    by_atom = ("cells", "depth")
    shard = P("cells")
    in_specs = (
        P(None, by_atom, None),
        P(None, None, by_atom, None),
        P(None, by_atom, None),
        P(None, None, by_atom, None),
        shard,
        shard,
        shard,
        shard,
        shard,
        shard,
        P(None, by_atom),
        P(None, None, by_atom),
        P(None, None, by_atom),
        P(None, None, None, by_atom),
        P(None, by_atom, None),
    )
    out_specs = (
        P(None, by_atom, None),
        P(None, None, by_atom, None),
        P(None, by_atom, None),
        P(None, None, by_atom, None),
    ) + (shard,) * 8
    return jax.shard_map(shards, mesh=mesh, in_specs=in_specs, out_specs=out_specs, check_vma=False)
```

time: 4400 us -> 366 us (0.08); the launches traced: 4340 us -> 368 us
  other arithmetic: 2680 us -> 9.97 us
  local copies, waits for them, and re-layouts: 1190 us -> 8.61 us
  matrix products: 271 us -> 0 us
  Pallas kernels: 0 us -> 143 us
    scatter-add x18 -> x0, other arithmetic: 2120 us -> none  [the longest x2 1810 us: micro_step(): jax.ops.segment_sum(vecedge_all.reshape(-1, 3, feat_width), flat_nbr, num...]
    gather x60 -> x0, local copies, waits for them, and re-layouts: 612 us -> none  [the longest x16 289 us: edge_inputs(): vec_edge = table_vec[:, nbr_blk].astype(f32)]
    reduce_sum x64 -> x0, other arithmetic: 309 us -> none  [the longest x8 123 us: message_sum(): dir_gate[None] * unit_dir[..., None]]
    dot_general x78 -> x0, matrix products: 271 us -> none  [the longest x16 126 us: edge_inputs(): jnp.einsum('kbr,rf->kbf', basis_blk, w_fvalue, preferred_element_type=f32)]
    mul x98 -> x0, local copies, waits for them, and re-layouts: 220 us -> none  [the longest x32 104 us: message_sum(): x_part.reshape(head_shape) * attention[..., None]]
    pallas_call x0 -> x6, Pallas kernels: none -> 143 us  [the longest x2 108 us: shards(): pl.pallas_call(partial(edge_kernel, micro, domains, buckets, atoms, width...]
    dynamic_update_slice x24 -> x0, other arithmetic: 103 us -> none  [micro_step(): lax.scan(backward_block, start_carry, back_items)]
    slice x39 -> x2, local copies, waits for them, and re-layouts: 68.2 us -> 0.74 us  [the longest x1 0.73 us: shards(): sent = jnp.stack([send_list[:, face] for face in mine], axis=1)]
  transfers between devices with their start and end apart: 27 -> 28, of which waited for: 6 -> 4; matrix products, arithmetic and copies ran while one was open for 28% -> 3% of each run, Pallas kernels for 0% -> 24%
where the time goes in v1:
time: 366 us; the launch traced here: 368 us
  Pallas kernels  143 us (39%)
  blocking collectives  82.1 us (22%)
  starting transfers between devices  59.3 us (16%)
  waiting for transfers between devices  49.9 us (14%)
  between operations  14.9 us (4%)
  other arithmetic  9.97 us (3%)
  local copies, waits for them, and re-layouts  8.61 us (2%)
    pallas_call x2, Pallas kernels, shards(): pl.pallas_call(partial(edge_kernel, micro, domains, buckets, atoms, width...  108 us
    ppermute x25, starting transfers between devices, from_behind(): lax.ppermute(shard, axis, [(i, (i + by) % length) for i in range(length)])  59.2 us
    psum x1, blocking collectives, shards(): sum_vecs = lax.psum(grad_v, ('cells', 'depth')).reshape(-1)  58.6 us
    psum x1, waiting for transfers between devices, shards(): sum_mats = lax.psum(sum_mats, 'depth').reshape(-1)  32.3 us
    pallas_call x1, Pallas kernels, shards(): pl.pallas_call(partial(prep_kernel, block_of, buckets), out_shape=(jax.Sh...  27.7 us
    unnamed x1, blocking collectives  23.5 us
    ppermute x25, waiting for transfers between devices, from_behind(): lax.ppermute(shard, axis, [(i, (i + by) % length) for i in range(length)])  17.5 us
  transfers between devices with their start and end apart: 28, of which 4 were waited for; matrix products, arithmetic and copies ran while one was open for 3% of the time, Pallas kernels for 24%

profile of v1, /device:TPU:0, one launch (start us, length us, event | category | flops | bytes accessed | tf_op | source)
XLA Modules:
  0.0 368.3 jit_solution(5705836817704067575)
XLA Ops:
  7.2 0.0 all-gather.2.cloned.1.call-start
  7.2 1.7 convert_bitcast_fusion
  8.9 0.0 all-gather.2.cloned.1.call-update
  8.9 0.0 reduce-scatter.2.cloned.1.call-start
  9.0 0.7 stack.43
  9.7 4.0 %collective-permute-start.2 = (s32[2,2,256]{2,0,1:T(2,128)S(1)}, s32[2,2,256]{2,0,1:T(2,128)S(1)}, u32[]{:S(2)}, u32[]{:S(2)}) collective-permute-start(s32[2,2,256]{2,0,1:T(2,128)S(1)} %stack.43), channel_id=1, source_target_pairs={{0,16},{4,20},{8,24},{12,28},{16,0},{20,4},{24,8},{28,12},{1,17},{... | collective-permute-start | bytes 12296 | tf_op jit(solution)/shard_map/ppermute | solution.py:594
  13.7 0.7 fusion.4
  14.4 1.5 collective-permute-start
  16.0 3.2 collective-permute-start.1
  19.2 1.7 collective-permute-start.4
  20.9 2.2 norm.1
  23.1 4.7 %collective-permute-start.6 = (bf16[4,128,256]{2,1,0:T(8,128)(2,1)}, bf16[4,128,256]{2,1,0:T(8,128)(2,1)S(1)}, u32[]{:S(2)}, u32[]{:S(2)}) collective-permute-start(bf16[4,128,256]{2,1,0:T(8,128)(2,1)} %get-tuple-element.44.refs_7_), channel_id=1, source_target_pairs={{0,28},{4,0},{8,4},{12,8},{16,12},{20,16},{24,20},{28,24},{1,29},{... | collective-permute-start | bytes 786440 | tf_op jit(solution)/shard_map/ppermute | solution.py:594
  27.9 0.1 collective-permute-start.8
  27.9 1.7 collective-permute-start.9
  29.7 0.7 convert_element_type.11
  30.3 1.3 copy.31.refs_1_
  31.6 1.2 dynamic-slice
  33.5 0.3 dynamic-update-slice
  33.8 23.5 %all-reduce = bf16[3584]{0:T(1024)(128)(2,1)} all-reduce(bf16[3584]{0:T(1024)(128)(2,1)S(1)} %dynamic-update-slice), channel_id=1, replica_groups=mesh['cells'=8,'depth'=4] {'cells'}, use_global_device_ids=true, to_apply=%add | all-reduce | flops 3584 | bytes 14336
  57.3 0.1 collective-permute-start.10
  57.4 4.7 %collective-permute-start.11 = (bf16[4,128,256]{2,1,0:T(8,128)(2,1)}, bf16[4,128,256]{2,1,0:T(8,128)(2,1)S(1)}, u32[]{:S(2)}, u32[]{:S(2)}) collective-permute-start(bf16[4,128,256]{2,1,0:T(8,128)(2,1)} %get-tuple-element.46.refs_7_), channel_id=1, source_target_pairs={{0,28},{4,0},{8,4},{12,8},{16,12},{20,16},{24,20},{28,24},{1,29},{... | collective-permute-start | bytes 786440 | tf_op jit(solution)/shard_map/ppermute | solution.py:594
  62.1 1.2 collective-permute-start.12
  63.3 1.7 collective-permute-start.14
  65.1 0.6 reshape.38.list_ref
  65.7 27.7 %prep.1 = (bf16[2,9472,128]{2,1,0:T(8,128)(2,1)}, s32[2,3]{1,0:T(2,128)}) custom-call(s32[2,64,128]{2,1,0:T(8,128)} %nbr_ref.1, s32[2,64,128]{2,1,0:T(8,128)} %mask_ref.1, f32[2,3,64,128]{3,2,1,0:T(8,128)} %geom_ref.1, s32[2,12,128]{2,1,0:T(8,128)} %reshape.38.list_ref), custom_call_target="tpu_custom_call" | custom-call | tf_op jit(solution)/shard_map/prep/pallas_call | solution.py:674
  93.4 0.0 all-gather.2.cloned.1.call-done.refs_13_
  93.5 52.0 %edges.2 = (f32[128,256]{1,0:T(8,128)}, f32[3,128,256]{2,1,0:T(8,128)}, f32[4,128,256]{2,1,0:T(8,128)}, bf16[4,128,256]{2,1,0:T(8,128)(2,1)}, bf16[4,128,256]{2,...) custom-call(s32[2,3]{1,0:T(2,128)} %get-tuple-element.42.refs_0_, ...), custom_call_target="tpu_custom_call" | custom-call | tf_op jit(solution)/shard_map/edges/pallas_call | solution.py:738
  145.5 0.0 copy-start.11
  145.5 0.0 copy-start.12
  145.6 0.0 copy-start.18
  145.6 0.6 copy-done.11
  146.2 0.1 copy-done.12
  146.3 0.1 copy-done.14
  146.4 0.1 copy-done.18
  146.5 0.1 copy-done.22
  146.6 55.8 %edges.3 = (f32[128,256]{1,0:T(8,128)}, f32[3,128,256]{2,1,0:T(8,128)}, f32[4,128,256]{2,1,0:T(8,128)}, bf16[4,128,256]{2,1,0:T(8,128)(2,1)}, bf16[4,128,256]{2,...) custom-call(s32[2,3]{1,0:T(2,128)} %get-tuple-element.42.refs_0_, ...), custom_call_target="tpu_custom_call" | custom-call | tf_op jit(solution)/shard_map/edges/pallas_call | solution.py:738
  202.4 0.0 reduce-scatter.2.cloned.1.call-update
  202.4 0.0 all-reduce.3.cloned.1.call-start
  202.5 0.8 copy-done.37
  203.3 0.1 copy-done.36
  203.4 1.9 collective-permute-start.16
  205.3 14.4 %collective-permute-start.17 = (bf16[4,128,256]{2,1,0:T(8,128)(2,1)S(1)}, bf16[4,128,256]{2,1,0:T(8,128)(2,1)S(1)}, u32[]{:S(2)}, u32[]{:S(2)}) collective-permute-start(bf16[4,128,256]{2,1,0:T(8,128)(2,1)S(1)} %copy-done.35), channel_id=1, source_target_pairs={{0,16},{4,20},{8,24},{12,28},{16,0},{20,4},{24,8},{28,12},{1,17},{... | collective-permute-start | bytes 786440 | tf_op jit(solution)/shard_map/ppermute | solution.py:594
  219.8 3.6 collective-permute-start.19
  223.4 5.6 %collective-permute-start.20 = (bf16[4,128,256]{2,1,0:T(8,128)(2,1)}, bf16[4,128,256]{2,1,0:T(8,128)(2,1)S(1)}, u32[]{:S(2)}, u32[]{:S(2)}) collective-permute-start(bf16[4,128,256]{2,1,0:T(8,128)(2,1)} %get-tuple-element.60), channel_id=1, source_target_pairs={{0,28},{4,0},{8,4},{12,8},{16,12},{20,16},{24,20},{28,24},{1,29},{... | collective-permute-start | bytes 786440 | tf_op jit(solution)/shard_map/ppermute | solution.py:594
  229.0 0.0 copy-start.19
  229.0 0.6 collective-permute-start.22
  229.7 7.5 %collective-permute-start.23 = (bf16[4,128,256]{2,1,0:T(8,128)(2,1)}, bf16[4,128,256]{2,1,0:T(8,128)(2,1)S(1)}, u32[]{:S(2)}, u32[]{:S(2)}) collective-permute-start(bf16[4,128,256]{2,1,0:T(8,128)(2,1)} %get-tuple-element.63), channel_id=1, source_target_pairs={{0,3},{1,0},{2,1},{3,2},{4,7},{5,4},{6,5},{7,6},{8,11},{9,8},{10,9... | collective-permute-start | bytes 786440 | tf_op jit(solution)/shard_map/ppermute | solution.py:594
  237.2 0.5 collective-permute-done.19.refs_4_
  237.6 0.7 collective-permute-start.24
  238.4 3.0 close.2
  241.4 0.0 copy-start.13
  241.4 0.0 copy-start.16
  241.4 13.4 %collective-permute-done.22.refs_2_ = bf16[4,128,256]{2,1,0:T(8,128)(2,1)S(1)} collective-permute-done((bf16[4,128,256]{2,1,0:T(8,128)(2,1)}, bf16[4,128,256]{2,1,0:T(8,128)(2,1)S(1)}, u32[]{:S(2)}, u32[]{:S(2)}) %collective-permute-start.22) | collective-permute-done | bytes 262176 | tf_op jit(solution)/shard_map/ppermute | solution.py:594
  254.8 3.7 collective-permute-done.24.refs_4_
  258.5 2.8 close.3
  261.4 0.8 add.42
  262.2 58.6 %psum.15 = f32[3584]{0:T(1024)S(1)} all-reduce(f32[3584]{0:T(1024)S(1)} %maximum_bitcast_fusion), channel_id=1, replica_groups=mesh['cells'=8,'depth'=4] {'cells','depth'}, use_global_device_ids=true, to_apply=%region_2.0 | all-reduce | flops 3584 | bytes 28672 | tf_op jit(solution)/shard_map/psum | solution.py:806
  320.8 1.7 pad_maximum_fusion.2
  322.5 2.2 pad_maximum_fusion
  324.8 0.0 all-reduce.3.cloned.1.call-update
  324.8 0.7 multiply_subtract_fusion.1
  325.5 32.3 %all-reduce.3.cloned.1.call-done = f32[94208]{0:T(1024)} async-done(((f32[94208]{0:T(1024)}), f32[94208]{0:T(1024)}) %all-reduce.3.cloned.1.call-update) | async-done | bytes 376848 | tf_op jit(solution)/shard_map/psum | solution.py:804
  357.8 2.2 multiply_subtract_fusion
  360.0 1.8 copy.39
  (102 shorter events, 0.3 us)
Async XLA Ops:
  7.2 86.3 %all-gather.2.cloned.1.call-start = ((), (), s32[]{:S(2)}) async-start(), calls=%async_computation.1 | async-start | bytes 1695744 | tf_op jit(solution)/shard_map/all_gather | solution.py:663
  8.9 315.8 %reduce-scatter.2.cloned.1.call-start = ((), (), s32[]{:S(2)}) async-start(), calls=%async_computation.2 | async-start | bytes 3391488 | tf_op jit(solution)/shard_map/reduce_scatter | solution.py:803
  9.7 18.3 %collective-permute-start.2 = (s32[2,2,256]{2,0,1:T(2,128)S(1)}, s32[2,2,256]{2,0,1:T(2,128)S(1)}, u32[]{:S(2)}, u32[]{:S(2)}) collective-permute-start(s32[2,2,256]{2,0,1:T(2,128)S(1)} %stack.43), channel_id=1, source_target_pairs={{0,16},{4,20},{8,24},{12,28},{16,0},{20,4},{24,8},{28,12},{1,17},{... | collective-permute-start | bytes 12296 | tf_op jit(solution)/shard_map/ppermute | solution.py:594
  14.4 8.7 %collective-permute-start = (s32[2,1,256]{2,0,1:T(2,128)S(1)}, s32[2,1,256]{2,0,1:T(2,128)S(1)}, u32[]{:S(2)}, u32[]{:S(2)}) collective-permute-start(s32[2,1,256]{2,0,1:T(2,128)S(1)} %get-tuple-element.81), channel_id=1, source_target_pairs={{0,4},{4,8},{8,12},{12,16},{16,20},{20,24},{24,28},{28,0},{1,5},{5... | collective-permute-start | bytes 6152 | tf_op jit(solution)/shard_map/ppermute | solution.py:594
  16.0 7.2 %collective-permute-start.1 = (s32[2,1,256]{2,0,1:T(2,128)S(1)}, s32[2,1,256]{2,0,1:T(2,128)S(1)}, u32[]{:S(2)}, u32[]{:S(2)}) collective-permute-start(s32[2,1,256]{2,0,1:T(2,128)S(1)} %get-tuple-element.80), channel_id=1, source_target_pairs={{0,28},{4,0},{8,4},{12,8},{16,12},{20,16},{24,20},{28,24},{1,29},{... | collective-permute-start | bytes 6152 | tf_op jit(solution)/shard_map/ppermute | solution.py:594
  19.2 8.7 %collective-permute-start.3 = (s32[2,1,256]{2,0,1:T(2,128)S(1)}, s32[2,1,256]{2,0,1:T(2,128)S(1)}, u32[]{:S(2)}, u32[]{:S(2)}) collective-permute-start(s32[2,1,256]{2,0,1:T(2,128)S(1)} %get-tuple-element.82), channel_id=1, source_target_pairs={{0,1},{1,2},{2,3},{3,0},{4,5},{5,6},{6,7},{7,4},{8,9},{9,10},{10,1... | collective-permute-start | bytes 6152 | tf_op jit(solution)/shard_map/ppermute | solution.py:594
  19.2 8.7 %collective-permute-start.4 = (s32[2,1,256]{2,0,1:T(2,128)S(1)}, s32[2,1,256]{2,0,1:T(2,128)S(1)}, u32[]{:S(2)}, u32[]{:S(2)}) collective-permute-start(s32[2,1,256]{2,0,1:T(2,128)S(1)} %get-tuple-element.79), channel_id=1, source_target_pairs={{0,3},{1,0},{2,1},{3,2},{4,7},{5,4},{6,5},{7,6},{8,11},{9,8},{10,9... | collective-permute-start | bytes 6152 | tf_op jit(solution)/shard_map/ppermute | solution.py:594
  23.1 34.2 %collective-permute-start.5 = (bf16[4,128,256]{2,1,0:T(8,128)(2,1)}, bf16[4,128,256]{2,1,0:T(8,128)(2,1)S(1)}, u32[]{:S(2)}, u32[]{:S(2)}) collective-permute-start(bf16[4,128,256]{2,1,0:T(8,128)(2,1)} %get-tuple-element.44.refs_7_), channel_id=1, source_target_pairs={{0,4},{4,8},{8,12},{12,16},{16,20},{20,24},{24,28},{28,0},{1,5},{5... | collective-permute-start | bytes 786440 | tf_op jit(solution)/shard_map/ppermute | solution.py:594
  23.1 34.3 %collective-permute-start.6 = (bf16[4,128,256]{2,1,0:T(8,128)(2,1)}, bf16[4,128,256]{2,1,0:T(8,128)(2,1)S(1)}, u32[]{:S(2)}, u32[]{:S(2)}) collective-permute-start(bf16[4,128,256]{2,1,0:T(8,128)(2,1)} %get-tuple-element.44.refs_7_), channel_id=1, source_target_pairs={{0,28},{4,0},{8,4},{12,8},{16,12},{20,16},{24,20},{28,24},{1,29},{... | collective-permute-start | bytes 786440 | tf_op jit(solution)/shard_map/ppermute | solution.py:594
  27.8 34.2 %collective-permute-start.7 = (bf16[4,128,256]{2,1,0:T(8,128)(2,1)}, bf16[4,128,256]{2,1,0:T(8,128)(2,1)S(1)}, u32[]{:S(2)}, u32[]{:S(2)}) collective-permute-start(bf16[4,128,256]{2,1,0:T(8,128)(2,1)} %get-tuple-element.44.refs_7_), channel_id=1, source_target_pairs={{0,16},{4,20},{8,24},{12,28},{16,0},{20,4},{24,8},{28,12},{1,17},{... | collective-permute-start | bytes 786440 | tf_op jit(solution)/shard_map/ppermute | solution.py:594
  27.9 35.4 %collective-permute-start.8 = (bf16[4,128,256]{2,1,0:T(8,128)(2,1)}, bf16[4,128,256]{2,1,0:T(8,128)(2,1)S(1)}, u32[]{:S(2)}, u32[]{:S(2)}) collective-permute-start(bf16[4,128,256]{2,1,0:T(8,128)(2,1)} %get-tuple-element.44.refs_7_), channel_id=1, source_target_pairs={{0,1},{1,2},{2,3},{3,0},{4,5},{5,6},{6,7},{7,4},{8,9},{9,10},{10,1... | collective-permute-start | bytes 786440 | tf_op jit(solution)/shard_map/ppermute | solution.py:594
  27.9 35.4 %collective-permute-start.9 = (bf16[4,128,256]{2,1,0:T(8,128)(2,1)}, bf16[4,128,256]{2,1,0:T(8,128)(2,1)S(1)}, u32[]{:S(2)}, u32[]{:S(2)}) collective-permute-start(bf16[4,128,256]{2,1,0:T(8,128)(2,1)} %get-tuple-element.44.refs_7_), channel_id=1, source_target_pairs={{0,3},{1,0},{2,1},{3,2},{4,7},{5,4},{6,5},{7,6},{8,11},{9,8},{10,9... | collective-permute-start | bytes 786440 | tf_op jit(solution)/shard_map/ppermute | solution.py:594
  57.3 36.2 %copy-start.6 = (bf16[4,128,256]{2,1,0:T(8,128)(2,1)}, bf16[4,128,256]{2,1,0:T(8,128)(2,1)S(1)}, u32[]{:S(2)}) copy-start(bf16[4,128,256]{2,1,0:T(8,128)(2,1)S(1)} %collective-permute-done.5.refs_8_) | copy-start | bytes 786436
  57.3 88.2 %collective-permute-start.10 = (bf16[4,128,256]{2,1,0:T(8,128)(2,1)}, bf16[4,128,256]{2,1,0:T(8,128)(2,1)S(1)}, u32[]{:S(2)}, u32[]{:S(2)}) collective-permute-start(bf16[4,128,256]{2,1,0:T(8,128)(2,1)} %get-tuple-element.46.refs_7_), channel_id=1, source_target_pairs={{0,4},{4,8},{8,12},{12,16},{16,20},{20,24},{24,28},{28,0},{1,5},{5... | collective-permute-start | bytes 786440 | tf_op jit(solution)/shard_map/ppermute | solution.py:594
  57.4 36.1 %copy-start.7 = (bf16[4,128,256]{2,1,0:T(8,128)(2,1)}, bf16[4,128,256]{2,1,0:T(8,128)(2,1)S(1)}, u32[]{:S(2)}) copy-start(bf16[4,128,256]{2,1,0:T(8,128)(2,1)S(1)} %collective-permute-done.6.refs_9_) | copy-start | bytes 786436
  57.4 88.1 %collective-permute-start.11 = (bf16[4,128,256]{2,1,0:T(8,128)(2,1)}, bf16[4,128,256]{2,1,0:T(8,128)(2,1)S(1)}, u32[]{:S(2)}, u32[]{:S(2)}) collective-permute-start(bf16[4,128,256]{2,1,0:T(8,128)(2,1)} %get-tuple-element.46.refs_7_), channel_id=1, source_target_pairs={{0,28},{4,0},{8,4},{12,8},{16,12},{20,16},{24,20},{28,24},{1,29},{... | collective-permute-start | bytes 786440 | tf_op jit(solution)/shard_map/ppermute | solution.py:594
  62.1 31.4 %copy-start.8 = (bf16[4,128,256]{2,1,0:T(8,128)(2,1)}, bf16[4,128,256]{2,1,0:T(8,128)(2,1)S(1)}, u32[]{:S(2)}) copy-start(bf16[4,128,256]{2,1,0:T(8,128)(2,1)S(1)} %collective-permute-done.7.refs_10_) | copy-start | bytes 786436
  62.1 83.5 %collective-permute-start.12 = (bf16[4,128,256]{2,1,0:T(8,128)(2,1)}, bf16[4,128,256]{2,1,0:T(8,128)(2,1)S(1)}, u32[]{:S(2)}, u32[]{:S(2)}) collective-permute-start(bf16[4,128,256]{2,1,0:T(8,128)(2,1)} %get-tuple-element.46.refs_7_), channel_id=1, source_target_pairs={{0,16},{4,20},{8,24},{12,28},{16,0},{20,4},{24,8},{28,12},{1,17},{... | collective-permute-start | bytes 786440 | tf_op jit(solution)/shard_map/ppermute | solution.py:594
  63.3 30.2 %copy-start.9 = (bf16[4,128,256]{2,1,0:T(8,128)(2,1)}, bf16[4,128,256]{2,1,0:T(8,128)(2,1)S(1)}, u32[]{:S(2)}) copy-start(bf16[4,128,256]{2,1,0:T(8,128)(2,1)S(1)} %collective-permute-done.8.refs_11_) | copy-start | bytes 786436
  63.3 82.3 %collective-permute-start.13 = (bf16[4,128,256]{2,1,0:T(8,128)(2,1)}, bf16[4,128,256]{2,1,0:T(8,128)(2,1)S(1)}, u32[]{:S(2)}, u32[]{:S(2)}) collective-permute-start(bf16[4,128,256]{2,1,0:T(8,128)(2,1)} %get-tuple-element.46.refs_7_), channel_id=1, source_target_pairs={{0,1},{1,2},{2,3},{3,0},{4,5},{5,6},{6,7},{7,4},{8,9},{9,10},{10,1... | collective-permute-start | bytes 786440 | tf_op jit(solution)/shard_map/ppermute | solution.py:594
  63.3 30.2 %copy-start.10 = (bf16[4,128,256]{2,1,0:T(8,128)(2,1)}, bf16[4,128,256]{2,1,0:T(8,128)(2,1)S(1)}, u32[]{:S(2)}) copy-start(bf16[4,128,256]{2,1,0:T(8,128)(2,1)S(1)} %collective-permute-done.9.refs_12_) | copy-start | bytes 786436
  63.3 82.3 %collective-permute-start.14 = (bf16[4,128,256]{2,1,0:T(8,128)(2,1)}, bf16[4,128,256]{2,1,0:T(8,128)(2,1)S(1)}, u32[]{:S(2)}, u32[]{:S(2)}) collective-permute-start(bf16[4,128,256]{2,1,0:T(8,128)(2,1)} %get-tuple-element.46.refs_7_), channel_id=1, source_target_pairs={{0,3},{1,0},{2,1},{3,2},{4,7},{5,4},{6,5},{7,6},{8,11},{9,8},{10,9... | collective-permute-start | bytes 786440 | tf_op jit(solution)/shard_map/ppermute | solution.py:594
  145.5 0.8 copy-start.12
  145.6 0.8 copy-start.14
  145.6 0.9 copy-start.18
  145.6 1.0 copy-start.22
  202.4 1.0 copy-start.37
  202.4 1.0 copy-start.36
  202.4 3.0 copy-start.35
  202.4 17.4 %copy-start.34 = (bf16[4,128,256]{2,1,0:T(8,128)(2,1)S(1)}, bf16[4,128,256]{2,1,0:T(8,128)(2,1)}, u32[]{:S(2)}) copy-start(bf16[4,128,256]{2,1,0:T(8,128)(2,1)} %get-tuple-element.56) | copy-start | bytes 786436
  202.4 17.4 %copy-start.33 = (bf16[4,128,256]{2,1,0:T(8,128)(2,1)S(1)}, bf16[4,128,256]{2,1,0:T(8,128)(2,1)}, u32[]{:S(2)}) copy-start(bf16[4,128,256]{2,1,0:T(8,128)(2,1)} %get-tuple-element.57) | copy-start | bytes 786436
  202.4 35.9 %copy-start.28 = (f32[28,128]{1,0:T(8,128)S(1)}, f32[28,128]{1,0:T(8,128)}, u32[]{:S(2)}) copy-start(f32[28,128]{1,0:T(8,128)} %get-tuple-element.71) | copy-start | bytes 43012
  202.4 155.4 %all-reduce.3.cloned.1.call-start = ((), (), s32[]{:S(2)}) async-start(), calls=%async_computation.3 | async-start | bytes 753664 | tf_op jit(solution)/shard_map/psum | solution.py:804
  203.3 20.1 %collective-permute-start.15 = (bf16[4,128,256]{2,1,0:T(8,128)(2,1)S(1)}, bf16[4,128,256]{2,1,0:T(8,128)(2,1)S(1)}, u32[]{:S(2)}, u32[]{:S(2)}) collective-permute-start(bf16[4,128,256]{2,1,0:T(8,128)(2,1)S(1)} %copy-done.37), channel_id=1, source_target_pairs={{0,28},{4,0},{8,4},{12,8},{16,12},{20,16},{24,20},{28,24},{1,29},{... | collective-permute-start | bytes 786440 | tf_op jit(solution)/shard_map/ppermute | solution.py:594
  203.4 25.6 %collective-permute-start.16 = (bf16[4,128,256]{2,1,0:T(8,128)(2,1)S(1)}, bf16[4,128,256]{2,1,0:T(8,128)(2,1)S(1)}, u32[]{:S(2)}, u32[]{:S(2)}) collective-permute-start(bf16[4,128,256]{2,1,0:T(8,128)(2,1)S(1)} %copy-done.36), channel_id=1, source_target_pairs={{0,4},{4,8},{8,12},{12,16},{16,20},{20,24},{24,28},{28,0},{1,5},{5... | collective-permute-start | bytes 786440 | tf_op jit(solution)/shard_map/ppermute | solution.py:594
  205.3 23.7 %collective-permute-start.17 = (bf16[4,128,256]{2,1,0:T(8,128)(2,1)S(1)}, bf16[4,128,256]{2,1,0:T(8,128)(2,1)S(1)}, u32[]{:S(2)}, u32[]{:S(2)}) collective-permute-start(bf16[4,128,256]{2,1,0:T(8,128)(2,1)S(1)} %copy-done.35), channel_id=1, source_target_pairs={{0,16},{4,20},{8,24},{12,28},{16,0},{20,4},{24,8},{28,12},{1,17},{... | collective-permute-start | bytes 786440 | tf_op jit(solution)/shard_map/ppermute | solution.py:594
  219.8 9.9 %collective-permute-start.18 = (bf16[4,128,256]{2,1,0:T(8,128)(2,1)S(1)}, bf16[4,128,256]{2,1,0:T(8,128)(2,1)S(1)}, u32[]{:S(2)}, u32[]{:S(2)}) collective-permute-start(bf16[4,128,256]{2,1,0:T(8,128)(2,1)S(1)} %copy-done.34), channel_id=1, source_target_pairs={{0,3},{1,0},{2,1},{3,2},{4,7},{5,4},{6,5},{7,6},{8,11},{9,8},{10,9... | collective-permute-start | bytes 786440 | tf_op jit(solution)/shard_map/ppermute | solution.py:594
  219.8 17.9 %collective-permute-start.19 = (bf16[4,128,256]{2,1,0:T(8,128)(2,1)S(1)}, bf16[4,128,256]{2,1,0:T(8,128)(2,1)S(1)}, u32[]{:S(2)}, u32[]{:S(2)}) collective-permute-start(bf16[4,128,256]{2,1,0:T(8,128)(2,1)S(1)} %copy-done.33), channel_id=1, source_target_pairs={{0,1},{1,2},{2,3},{3,0},{4,5},{5,6},{6,7},{7,4},{8,9},{9,10},{10,1... | collective-permute-start | bytes 786440 | tf_op jit(solution)/shard_map/ppermute | solution.py:594
  223.4 14.9 %copy-start.15 = (bf16[4,128,256]{2,1,0:T(8,128)(2,1)}, bf16[4,128,256]{2,1,0:T(8,128)(2,1)S(1)}, u32[]{:S(2)}) copy-start(bf16[4,128,256]{2,1,0:T(8,128)(2,1)S(1)} %collective-permute-done.15.refs_0_) | copy-start | bytes 786436
  223.4 18.0 %collective-permute-start.20 = (bf16[4,128,256]{2,1,0:T(8,128)(2,1)}, bf16[4,128,256]{2,1,0:T(8,128)(2,1)S(1)}, u32[]{:S(2)}, u32[]{:S(2)}) collective-permute-start(bf16[4,128,256]{2,1,0:T(8,128)(2,1)} %get-tuple-element.60), channel_id=1, source_target_pairs={{0,28},{4,0},{8,4},{12,8},{16,12},{20,16},{24,20},{28,24},{1,29},{... | collective-permute-start | bytes 786440 | tf_op jit(solution)/shard_map/ppermute | solution.py:594
  229.0 9.4 %copy-start.17 = (bf16[4,128,256]{2,1,0:T(8,128)(2,1)}, bf16[4,128,256]{2,1,0:T(8,128)(2,1)S(1)}, u32[]{:S(2)}) copy-start(bf16[4,128,256]{2,1,0:T(8,128)(2,1)S(1)} %collective-permute-done.16.refs_1_) | copy-start | bytes 786436
  229.0 12.4 %collective-permute-start.21 = (bf16[4,128,256]{2,1,0:T(8,128)(2,1)}, bf16[4,128,256]{2,1,0:T(8,128)(2,1)S(1)}, u32[]{:S(2)}, u32[]{:S(2)}) collective-permute-start(bf16[4,128,256]{2,1,0:T(8,128)(2,1)} %get-tuple-element.61), channel_id=1, source_target_pairs={{0,4},{4,8},{8,12},{12,16},{16,20},{20,24},{24,28},{28,0},{1,5},{5... | collective-permute-start | bytes 786440 | tf_op jit(solution)/shard_map/ppermute | solution.py:594
  229.0 9.4 %copy-start.19 = (bf16[4,128,256]{2,1,0:T(8,128)(2,1)}, bf16[4,128,256]{2,1,0:T(8,128)(2,1)S(1)}, u32[]{:S(2)}) copy-start(bf16[4,128,256]{2,1,0:T(8,128)(2,1)S(1)} %collective-permute-done.17.refs_2_) | copy-start | bytes 786436
  229.0 25.8 %collective-permute-start.22 = (bf16[4,128,256]{2,1,0:T(8,128)(2,1)}, bf16[4,128,256]{2,1,0:T(8,128)(2,1)S(1)}, u32[]{:S(2)}, u32[]{:S(2)}) collective-permute-start(bf16[4,128,256]{2,1,0:T(8,128)(2,1)} %get-tuple-element.62), channel_id=1, source_target_pairs={{0,16},{4,20},{8,24},{12,28},{16,0},{20,4},{24,8},{28,12},{1,17},{... | collective-permute-start | bytes 786440 | tf_op jit(solution)/shard_map/ppermute | solution.py:594
  229.7 8.7 %copy-start.21 = (bf16[4,128,256]{2,1,0:T(8,128)(2,1)}, bf16[4,128,256]{2,1,0:T(8,128)(2,1)S(1)}, u32[]{:S(2)}) copy-start(bf16[4,128,256]{2,1,0:T(8,128)(2,1)S(1)} %collective-permute-done.18.refs_3_) | copy-start | bytes 786436
  229.7 25.2 %collective-permute-start.23 = (bf16[4,128,256]{2,1,0:T(8,128)(2,1)}, bf16[4,128,256]{2,1,0:T(8,128)(2,1)S(1)}, u32[]{:S(2)}, u32[]{:S(2)}) collective-permute-start(bf16[4,128,256]{2,1,0:T(8,128)(2,1)} %get-tuple-element.63), channel_id=1, source_target_pairs={{0,3},{1,0},{2,1},{3,2},{4,7},{5,4},{6,5},{7,6},{8,11},{9,8},{10,9... | collective-permute-start | bytes 786440 | tf_op jit(solution)/shard_map/ppermute | solution.py:594
  237.6 20.8 %collective-permute-start.24 = (bf16[4,128,256]{2,1,0:T(8,128)(2,1)}, bf16[4,128,256]{2,1,0:T(8,128)(2,1)}, u32[]{:S(2)}, u32[]{:S(2)}) collective-permute-start(bf16[4,128,256]{2,1,0:T(8,128)(2,1)} %get-tuple-element.64), channel_id=1, source_target_pairs={{0,1},{1,2},{2,3},{3,0},{4,5},{5,6},{6,7},{7,4},{8,9},{9,10},{10,1... | collective-permute-start | bytes 786440 | tf_op jit(solution)/shard_map/ppermute | solution.py:594
  238.4 82.4 %copy-start.25 = (f32[128,256]{1,0:T(8,128)S(1)}, f32[128,256]{1,0:T(8,128)}, u32[]{:S(2)}) copy-start(f32[128,256]{1,0:T(8,128)} %get-tuple-element.45) | copy-start | bytes 393220
  238.4 84.1 %copy-start.1 = (f32[3,128,256]{2,1,0:T(8,128)S(1)}, f32[3,128,256]{2,1,0:T(8,128)}, u32[]{:S(2)}) copy-start(f32[3,128,256]{2,1,0:T(8,128)} %get-tuple-element.50) | copy-start | bytes 1179652
  238.4 84.1 %copy-start.2 = (f32[3,128,256]{2,1,0:T(8,128)S(1)}, f32[3,128,256]{2,1,0:T(8,128)}, u32[]{:S(2)}) copy-start(f32[3,128,256]{2,1,0:T(8,128)} %get-tuple-element.51) | copy-start | bytes 1179652
  241.4 20.0 %copy-start.32 = (f32[4,128]{1,0:T(4,128)S(1)}, f32[4,128]{1,0:T(4,128)}, u32[]{:S(2)}) copy-start(f32[4,128]{1,0:T(4,128)} %get-tuple-element.69) | copy-start | bytes 6148
  241.4 79.4 %copy-start.26 = (f32[128,256]{1,0:T(8,128)S(1)}, f32[128,256]{1,0:T(8,128)}, u32[]{:S(2)}) copy-start(f32[128,256]{1,0:T(8,128)} %get-tuple-element.49) | copy-start | bytes 393220
  241.4 79.4 %copy-start.27 = (f32[128,256]{1,0:T(8,128)S(1)}, f32[128,256]{1,0:T(8,128)}, u32[]{:S(2)}) copy-start(f32[128,256]{1,0:T(8,128)} %get-tuple-element.58) | copy-start | bytes 393220
  241.4 81.1 %copy-start.3 = (f32[3,128,256]{2,1,0:T(8,128)S(1)}, f32[3,128,256]{2,1,0:T(8,128)}, u32[]{:S(2)}) copy-start(f32[3,128,256]{2,1,0:T(8,128)} %get-tuple-element.66) | copy-start | bytes 1179652
  241.4 17.1 %copy-start.13 = (bf16[4,128,256]{2,1,0:T(8,128)(2,1)}, bf16[4,128,256]{2,1,0:T(8,128)(2,1)S(1)}, u32[]{:S(2)}) copy-start(bf16[4,128,256]{2,1,0:T(8,128)(2,1)S(1)} %collective-permute-done.20.refs_0_) | copy-start | bytes 786436
  241.4 17.0 %copy-start.16 = (bf16[4,128,256]{2,1,0:T(8,128)(2,1)}, bf16[4,128,256]{2,1,0:T(8,128)(2,1)S(1)}, u32[]{:S(2)}) copy-start(bf16[4,128,256]{2,1,0:T(8,128)(2,1)S(1)} %collective-permute-done.21.refs_1_) | copy-start | bytes 786436
  254.8 3.7 copy-start.20
  254.8 3.7 copy-start.24
  261.3 63.5 %copy-start.29 = (f32[448]{0:T(512)S(1)}, f32[448]{0:T(512)}, u32[]{:S(2)}) copy-start(f32[448]{0:T(512)} %param.20) | copy-start | bytes 5380
  261.3 63.5 %copy-start.30 = (f32[448]{0:T(512)S(1)}, f32[448]{0:T(512)}, u32[]{:S(2)}) copy-start(f32[448]{0:T(512)} %param.23) | copy-start | bytes 5380
  261.3 63.5 %copy-start.31 = (f32[448]{0:T(512)S(1)}, f32[448]{0:T(512)}, u32[]{:S(2)}) copy-start(f32[448]{0:T(512)} %param.24) | copy-start | bytes 5380
  261.3 96.5 %copy-start = (f32[94208]{0:T(1024)S(1)}, f32[94208]{0:T(1024)}, u32[]{:S(2)}) copy-start(f32[94208]{0:T(1024)} %param.19) | copy-start | bytes 1130500
  261.3 96.5 %copy-start.4 = (f32[94208]{0:T(1024)S(1)}, f32[94208]{0:T(1024)}, u32[]{:S(2)}) copy-start(f32[94208]{0:T(1024)} %param.21) | copy-start | bytes 1130500
  261.3 96.5 %copy-start.5 = (f32[94208]{0:T(1024)S(1)}, f32[94208]{0:T(1024)}, u32[]{:S(2)}) copy-start(f32[94208]{0:T(1024)} %param.22) | copy-start | bytes 1130500
  (2 other events, 1.4 us)
Sparse Core Ops, SparseCore 0:
  10.8 70.1 all-gather.1
  202.6 118.7 reduce-scatter.1
  324.9 32.8 all-reduce.2

commit v2 on v1

--- a/solution.py
+++ b/solution.py
@@ -56,7 +56,11 @@
     return centered * spread, spread
 
 
-def norm_kernel(x_ref, vec_ref, *own_refs):
+def norm_kernel(x_ref, vec_ref, mats_ref, *refs):
+    *own_refs, low_ref = refs
+    quarter = low_ref.shape[1]
+    for part in range(low_ref.shape[0]):
+        low_ref[part] = mats_ref[part * quarter : (part + 1) * quarter, :].astype(bf16)
     for micro, own_ref in enumerate(own_refs):
         own_ref[0] = normalise(x_ref[micro])[0].astype(bf16)
         own_ref[1:] = vec_ref[micro].astype(bf16)
@@ -243,7 +247,11 @@
         both = [v_ref[2 * index + half : 2 * index + half + 1, :].astype(f32) for half in range(2)]
         return jnp.concatenate(both, axis=1)
 
-    wide_w[...] = w_ref[...].astype(f32)
+    cells, parts_w, quarter = w_ref.shape[0], w_ref.shape[1], w_ref.shape[2]
+    for cell in range(cells):
+        for part in range(parts_w):
+            start = (cell * parts_w + part) * quarter
+            wide_w[start : start + quarter, :] = w_ref[cell, part].astype(f32)
 
     def weight_block(first, stride, column, rows):
         halves = [
@@ -487,10 +495,12 @@
         proj[0, rows, :] = g_dot * proj[1, rows, :]
         proj[1, rows, :] = g_dot * held
 
+    gm_sum = wide_w if has_prior else gm_ref
+
     def put_grad(first, stride, column, rows, value):
         for half in range(2):
             at = pl.ds(first + 2 * column + half, rows, stride=stride)
-            gm_ref[at, :] = value[:, half * LANES : (half + 1) * LANES]
+            gm_sum[at, :] = value[:, half * LANES : (half + 1) * LANES]
 
     def put_vector(index, value):
         for half in range(2):
@@ -554,28 +564,261 @@
             put_grad(DV_AT, 6, column - 1, NR, block)
         put_vector(10 + column, gwd[NR : NR + 1, cols] * 0.5)
     if has_prior:
-        gm_ref[...] += prior_m_ref[...]
+        for cell in range(cells):
+            for part in range(parts_w):
+                start = (cell * parts_w + part) * quarter
+                rows = slice(start, start + quarter)
+                gm_ref[part, cell] = (gm_sum[rows, :] + prior_m_ref[rows, :]).astype(bf16)
         gv_ref[...] += prior_v_ref[...]
 
 
-def close_kernel(domains, x_ref, cotx_ref, cotv_ref, gown_ref, *refs):
-    back_refs = refs[: domains - 1]
-    v_ref, gx_ref, gvec_ref, gln_ref = refs[domains - 1 :]
-    total = [gown_ref[part] for part in range(4)]
-    for back_ref in back_refs:
-        for part in range(4):
-            total[part] = total[part] + back_ref[part].astype(f32)
-    gain = jnp.concatenate([v_ref[half : half + 1, :].astype(f32) for half in range(2)], axis=1)
-    hat, spread = normalise(x_ref[0])
-    for at, value in ((0, total[0] * hat), (2, total[0])):
-        summed = jnp.sum(value, axis=0, keepdims=True)
+def core_mate(depth_at):
+    return depth_at + 1 - 2 * (depth_at % 2)
+
+
+def chip_mate(depth_at):
+    return (depth_at + 2) % 4
+
+
+def greet(cells, depth):
+    barrier = pltpu.get_barrier_semaphore()
+    cell_at, depth_at = lax.axis_index("cells"), lax.axis_index("depth")
+    for by in range(1, cells):
+        pl.semaphore_signal(barrier, inc=1, device_id={"cells": (cell_at + by) % cells})
+    for by in range(1, depth):
+        pl.semaphore_signal(barrier, inc=1, device_id={"depth": (depth_at + by) % depth})
+    pl.semaphore_wait(barrier, cells + depth - 2)
+
+
+def remote(source, target, send, receive, device):
+    return pltpu.make_async_remote_copy(
+        src_ref=source, dst_ref=target, send_sem=send, recv_sem=receive, device_id=device
+    )
+
+
+def fetch_kernel(cells, depth, micros, sources, faces, *refs):
+    own_refs = refs[:micros]
+    lists_ref, w_ref, v_ref = refs[micros : micros + 3]
+    refs = refs[micros + 3 :]
+    halo_refs = refs[: micros * len(sources)]
+    got_lists, got_w, got_v = refs[micros * len(sources) : micros * len(sources) + 3]
+    halo_send, halo_recv, list_send, list_recv, v_send, v_recv, w_send, w_recv = refs[
+        micros * len(sources) + 3 :
+    ]
+    cell_at, depth_at = lax.axis_index("cells"), lax.axis_index("depth")
+    sizes = {"cells": cells, "depth": depth}
+    places = {"cells": cell_at, "depth": depth_at}
+    got_w[cell_at] = w_ref[...]
+    got_v[cell_at] = v_ref[...]
+    greet(cells, depth)
+
+    def ahead(axis, by):
+        return {axis: (places[axis] + by) % sizes[axis]}
+
+    started = []
+
+    def start(*args):
+        copy = remote(*args)
+        copy.start()
+        started.append(copy)
+        return copy
+
+    first = []
+    for by in range(1, cells):
+        there = ahead("cells", by)
+        first.append(
+            start(
+                w_ref.at[depth_at],
+                got_w.at[cell_at, depth_at],
+                w_send.at[0, by],
+                w_recv.at[0, by],
+                there,
+            )
+        )
+    lists = [
+        start(
+            lists_ref.at[face],
+            got_lists.at[face],
+            list_send.at[face],
+            list_recv.at[face],
+            ahead(axis, by),
+        )
+        for face, (axis, by) in enumerate(faces)
+    ]
+    vectors = [
+        start(v_ref, got_v.at[cell_at], v_send.at[by], v_recv.at[by], ahead("cells", by))
+        for by in range(1, cells)
+    ]
+    halos = []
+    for micro in range(micros):
+        for index, (axis, by) in enumerate(sources):
+            halos.append(
+                start(
+                    own_refs[micro],
+                    halo_refs[micro * len(sources) + index],
+                    halo_send.at[micro, index],
+                    halo_recv.at[micro, index],
+                    ahead(axis, by),
+                )
+            )
+    mate, other = core_mate(depth_at), chip_mate(depth_at)
+    across = []
+    last = []
+    for by in range(1, cells):
+        first[by - 1].wait_recv()
+        piece = got_w.at[(cell_at + cells - by) % cells, depth_at]
+        across.append(
+            start(piece, piece, w_send.at[1, by], w_recv.at[1, by], {"depth": other})
+        )
+        last.append(start(piece, piece, w_send.at[2, by], w_recv.at[2, by], {"depth": mate}))
+    for by in range(1, cells):
+        across[by - 1].wait_recv()
+        piece = got_w.at[(cell_at + cells - by) % cells, other]
+        last.append(start(piece, piece, w_send.at[3, by], w_recv.at[3, by], {"depth": mate}))
+    for copy in lists + vectors + last + halos:
+        copy.wait_recv()
+    for copy in started:
+        copy.wait_send()
+
+
+def close_kernel(cells, depth, micros, sources, *refs):
+    x_ref, cotx_ref, cotv_ref, gain_ref, gvec_in, part_ref = refs[:6]
+    refs = refs[6:]
+    gown_refs = refs[:micros]
+    back_refs = refs[micros : micros + micros * len(sources)]
+    refs = refs[micros + micros * len(sources) :]
+    gx_ref, gvec_ref, summ_ref, sumv_ref = refs[:4]
+    came, one_in, two_out, two_in, three_out, three_in, held, quad, octo = refs[4:13]
+    halo_send, halo_recv, m_send, m_recv, c_send, c_recv, d_send, d_recv, e_send, e_recv, f_send, f_recv = refs[13:]
+    cell_at, depth_at = lax.axis_index("cells"), lax.axis_index("depth")
+    sizes = {"cells": cells, "depth": depth}
+    places = {"cells": cell_at, "depth": depth_at}
+    greet(cells, depth)
+
+    def ahead(axis, by):
+        return {axis: (places[axis] + by) % sizes[axis]}
+
+    started = []
+
+    def start(*args):
+        copy = remote(*args)
+        copy.start()
+        started.append(copy)
+        return copy
+
+    mate, other = core_mate(depth_at), chip_mate(depth_at)
+    mate_other = chip_mate(mate)
+    one_far = start(
+        part_ref.at[mate_other], one_in.at[1], m_send.at[0], m_recv.at[0], {"depth": mate}
+    )
+    one_near = start(part_ref.at[mate], one_in.at[0], m_send.at[1], m_recv.at[1], {"depth": mate})
+    halos = []
+    for micro in range(micros):
+        for index, (axis, by) in enumerate(sources):
+            halos.append(
+                start(
+                    back_refs[micro * len(sources) + index],
+                    came.at[micro, index],
+                    halo_send.at[micro, index],
+                    halo_recv.at[micro, index],
+                    ahead(axis, -by),
+                )
+            )
+    one_far.wait_recv()
+    two_out[...] = (part_ref[other].astype(f32) + one_in[1].astype(f32)).astype(bf16)
+    two = start(two_out, two_in, m_send.at[2], m_recv.at[2], {"depth": other})
+    one_near.wait_recv()
+    two.wait_recv()
+    for cell in range(cells):
+        total = (
+            part_ref[depth_at, cell].astype(f32)
+            + one_in[0, cell].astype(f32)
+            + two_in[cell].astype(f32)
+        )
+        three_out[cell] = total.astype(bf16)
+    three = []
+    for by in range(1, cells):
+        there = (cell_at + by) % cells
+        three.append(
+            start(
+                three_out.at[there],
+                three_in.at[by],
+                c_send.at[by],
+                c_recv.at[by],
+                {"cells": there},
+            )
+        )
+
+    for copy in halos:
+        copy.wait_recv()
+    gain = jnp.concatenate([gain_ref[half : half + 1, :].astype(f32) for half in range(2)], axis=1)
+    norm_grads = [jnp.zeros((1, gain.shape[1]), f32) for part in range(2)]
+    for micro in range(micros):
+        total = [gown_refs[micro][part] for part in range(4)]
+        for index in range(len(sources)):
+            for part in range(4):
+                total[part] = total[part] + came[micro, index, part].astype(f32)
+        hat, spread = normalise(x_ref[micro])
+        norm_grads[0] += jnp.sum(total[0] * hat, axis=0, keepdims=True)
+        norm_grads[1] += jnp.sum(total[0], axis=0, keepdims=True)
+        g_hat = total[0] * gain
+        g_x = spread * (g_hat - lane_mean(g_hat) - hat * lane_mean(g_hat * hat))
+        gx_ref[micro] = cotx_ref[micro] + g_x
+        for axis in range(3):
+            gvec_ref[micro, axis] = cotv_ref[micro, axis] + total[1 + axis]
+    held[...] = gvec_in[...]
+    for part in range(2):
         for half in range(2):
-            gln_ref[at + half : at + half + 1, :] = summed[:, half * LANES : (half + 1) * LANES]
-    g_hat = total[0] * gain
-    g_x = spread * (g_hat - lane_mean(g_hat) - hat * lane_mean(g_hat * hat))
-    gx_ref[...] = cotx_ref[0] + g_x
-    for axis in range(3):
-        gvec_ref[axis] = cotv_ref[0, axis] + total[1 + axis]
+            row = 2 * part + half
+            held[row : row + 1, :] = norm_grads[part][:, half * LANES : (half + 1) * LANES]
+    quad[depth_at] = held[...]
+    four = [
+        start(held, quad.at[depth_at], d_send.at[by], d_recv.at[by], ahead("depth", by))
+        for by in range(1, depth)
+    ]
+
+    for copy in three:
+        copy.wait_recv()
+    final = three_out[cell_at].astype(f32)
+    for by in range(1, cells):
+        final = final + three_in[by].astype(f32)
+    summ_ref[depth_at] = final
+    share = [
+        start(
+            summ_ref.at[depth_at],
+            summ_ref.at[depth_at],
+            e_send.at[by],
+            e_recv.at[by],
+            ahead("depth", by),
+        )
+        for by in range(1, depth)
+    ]
+    for copy in four:
+        copy.wait_recv()
+    total = quad[0]
+    for at in range(1, depth):
+        total = total + quad[at]
+    octo[cell_at] = total
+    eight = [
+        start(
+            octo.at[cell_at],
+            octo.at[cell_at],
+            f_send.at[by],
+            f_recv.at[by],
+            ahead("cells", by),
+        )
+        for by in range(1, cells)
+    ]
+    for copy in eight:
+        copy.wait_recv()
+    total = octo[0]
+    for cell in range(1, cells):
+        total = total + octo[cell]
+    sumv_ref[...] = total
+    for copy in share:
+        copy.wait_recv()
+    for copy in started:
+        copy.wait_send()
 
 
 def adam_update(weight, grad, first, second):
@@ -587,11 +830,6 @@
         first_hat / (jnp.sqrt(second_hat) + adam_eps) + decay_rate * weight
     )
     return (weight_new, first_new, second_new)
-
-
-def from_behind(shard, axis, by):
-    length = lax.axis_size(axis)
-    return lax.ppermute(shard, axis, [(i, (i + by) % length) for i in range(length)])
 
 
 def micro_block(shape, micro):
@@ -638,31 +876,61 @@
     whole = pl.BlockSpec(memory_space=pltpu.VMEM)
     scalars = pl.BlockSpec(memory_space=pltpu.SMEM)
 
-    lists = [None] * 6
-    for index, (axis, by) in enumerate(sources):
-        mine = [face for face in range(6) if face_source[face] == index]
-        sent = jnp.stack([send_list[:, face] for face in mine], axis=1)
-        got = from_behind(sent, axis, by)
-        for order, face in enumerate(mine):
-            lists[face] = got[:, order]
-    list_rows = jnp.stack(lists, axis=1).reshape(micros, 6 * per_face, LANES)
-
-    own = pl.pallas_call(
+    any_space = pl.BlockSpec(memory_space=pl.ANY)
+    count = len(sources)
+    quarter = mats.shape[0] // LANES // depth
+    v_rows = -(-vecs.shape[0] // LANES)
+    v_low = jnp.pad(vecs.astype(bf16), (0, v_rows * LANES - vecs.shape[0])).reshape(v_rows, LANES)
+    faces_first = jnp.moveaxis(
+        send_list.reshape(micros, 6, per_face, LANES), 1, 0
+    ).reshape(6, micros * per_face, LANES)
+
+    *own, w_low = pl.pallas_call(
         norm_kernel,
         out_shape=tuple(
             jax.ShapeDtypeStruct((4, atoms, width), bf16) for micro in range(micros)
+        )
+        + (jax.ShapeDtypeStruct((depth, quarter, LANES), bf16),),
+        in_specs=[whole] * 3,
+        out_specs=[whole] * (micros + 1),
+        name="norm",
+    )(x_in, vec_in, mats.reshape(-1, LANES))
+
+    dma = pltpu.SemaphoreType.DMA
+    fetched = pl.pallas_call(
+        partial(fetch_kernel, cells, depth, micros, sources, faces),
+        out_shape=tuple(
+            [jax.ShapeDtypeStruct((4, atoms, width), bf16)] * (micros * count)
+            + [
+                jax.ShapeDtypeStruct(faces_first.shape, i32),
+                jax.ShapeDtypeStruct((cells, depth, quarter, LANES), bf16),
+                jax.ShapeDtypeStruct((cells, v_rows, LANES), bf16),
+            ]
         ),
-        in_specs=[whole] * 2,
-        out_specs=[whole] * micros,
-        name="norm",
-    )(x_in, vec_in)
-
-    halos = [[from_behind(own[micro], axis, by) for axis, by in sources] for micro in range(micros)]
-
-    mats_rows = mats.reshape(-1, LANES)
-    w_all = lax.all_gather(mats_rows.astype(bf16), "cells", axis=0, tiled=True)
-    v_all = lax.all_gather(vecs.astype(bf16), "cells", axis=0, tiled=True).reshape(-1, LANES)
-    w_rows, v_rows = w_all.shape[0], v_all.shape[0]
+        in_specs=[any_space] * micros + [whole] * 3,
+        out_specs=[any_space] * (micros * count) + [whole] * 3,
+        scratch_shapes=[
+            dma((micros, count)),
+            dma((micros, count)),
+            dma((6,)),
+            dma((6,)),
+            dma((cells,)),
+            dma((cells,)),
+            dma((4, cells)),
+            dma((4, cells)),
+        ],
+        compiler_params=pltpu.CompilerParams(
+            collective_id=0, has_side_effects=True, vmem_limit_bytes=VMEM_LIMIT
+        ),
+        name="fetch",
+    )(*own, faces_first, w_low, v_low)
+    halos = [fetched[micro * count : (micro + 1) * count] for micro in range(micros)]
+    got_lists, w_all, v_all = fetched[micros * count :]
+    list_rows = jnp.moveaxis(
+        got_lists.reshape(6, micros, per_face, LANES), 1, 0
+    ).reshape(micros, 6 * per_face, LANES)
+    v_all = v_all.reshape(cells, v_rows * LANES)[:, : vecs.shape[0]].reshape(-1, LANES)
+    w_rows, v_rows = cells * depth * quarter, v_all.shape[0]
 
     limit = slots * atoms + buckets * (slots // BLOCK_SLOTS) * 8 + buckets * UNIT
     capacity = (limit + UNIT - 1) // UNIT * UNIT
@@ -731,7 +999,9 @@
             ]
             + [jax.ShapeDtypeStruct((4, atoms, width), bf16)] * len(sources)
             + [
-                jax.ShapeDtypeStruct((w_rows, LANES), f32),
+                jax.ShapeDtypeStruct((depth, cells, quarter, LANES), bf16)
+                if prior
+                else jax.ShapeDtypeStruct((w_rows, LANES), f32),
                 jax.ShapeDtypeStruct((v_rows, LANES), f32),
             ]
         )
@@ -772,48 +1042,65 @@
         outs.append(results)
         grads = list(results[-2:])
 
-    closed = []
-    for micro in range(micros):
-        back = outs[micro][3 : 3 + len(sources)]
-        returned = [
-            from_behind(block, axis, -by) for block, (axis, by) in zip(back, sources)
-        ]
-        closed.append(
-            pl.pallas_call(
-                partial(close_kernel, domains),
-                out_shape=(
-                    jax.ShapeDtypeStruct((atoms, width), f32),
-                    jax.ShapeDtypeStruct((3, atoms, width), f32),
-                    jax.ShapeDtypeStruct((4, LANES), f32),
-                ),
-                grid=(1,),
-                in_specs=[
-                    micro_block(array.shape, micro) for array in (x_in, cot_x, cot_vec)
-                ]
-                + [whole] * (2 + len(sources)),
-                out_specs=[whole] * 3,
-                name="close",
-            )(x_in, cot_x, cot_vec, outs[micro][2], *returned, v_all)
-        )
-
-    grad_m, grad_v = grads
-    grad_norm = closed[0][2]
-    for micro in range(1, micros):
-        grad_norm = grad_norm + closed[micro][2]
-    sum_mats = lax.psum_scatter(grad_m, "cells", scatter_dimension=0, tiled=True)
-    sum_mats = lax.psum(sum_mats, "depth").reshape(-1)
-    grad_v = jnp.concatenate([grad_norm, grad_v[4:]], axis=0)
-    sum_vecs = lax.psum(grad_v, ("cells", "depth")).reshape(-1)
+    part_m, part_v = grads
+    grad_x, grad_vec, sum_mats, sum_vecs = pl.pallas_call(
+        partial(close_kernel, cells, depth, micros, sources),
+        out_shape=(
+            jax.ShapeDtypeStruct(x_in.shape, f32),
+            jax.ShapeDtypeStruct(vec_in.shape, f32),
+            jax.ShapeDtypeStruct((depth, quarter, LANES), f32),
+            jax.ShapeDtypeStruct((v_rows, LANES), f32),
+        ),
+        in_specs=[whole] * (6 + micros) + [any_space] * (micros * count),
+        out_specs=[whole] * 4,
+        scratch_shapes=[
+            pltpu.VMEM((micros, count, 4, atoms, width), bf16),
+            pltpu.VMEM((2, cells, quarter, LANES), bf16),
+            pltpu.VMEM((cells, quarter, LANES), bf16),
+            pltpu.VMEM((cells, quarter, LANES), bf16),
+            pltpu.VMEM((cells, quarter, LANES), bf16),
+            pltpu.VMEM((cells, quarter, LANES), bf16),
+            pltpu.VMEM((v_rows, LANES), f32),
+            pltpu.VMEM((depth, v_rows, LANES), f32),
+            pltpu.VMEM((cells, v_rows, LANES), f32),
+            dma((micros, count)),
+            dma((micros, count)),
+            dma((3,)),
+            dma((3,)),
+            dma((cells,)),
+            dma((cells,)),
+            dma((depth,)),
+            dma((depth,)),
+            dma((depth,)),
+            dma((depth,)),
+            dma((cells,)),
+            dma((cells,)),
+        ],
+        compiler_params=pltpu.CompilerParams(
+            collective_id=1, has_side_effects=True, vmem_limit_bytes=VMEM_LIMIT
+        ),
+        name="close",
+    )(
+        x_in,
+        cot_x,
+        cot_vec,
+        v_all,
+        part_v,
+        part_m,
+        *[result[2] for result in outs],
+        *[block for result in outs for block in result[3 : 3 + count]],
+    )
+    sum_mats = sum_mats.reshape(-1)
     sum_vecs = lax.dynamic_slice_in_dim(
-        sum_vecs, lax.axis_index("cells") * vecs.shape[0], vecs.shape[0]
+        sum_vecs.reshape(-1), lax.axis_index("cells") * vecs.shape[0], vecs.shape[0]
     )
     new_mats, mats_one, mats_two = adam_update(mats, sum_mats, mats_first, mats_second)
     new_vecs, vecs_one, vecs_two = adam_update(vecs, sum_vecs, vecs_first, vecs_second)
     return (
         jnp.stack([result[0] for result in outs]),
         jnp.stack([result[1] for result in outs]),
-        jnp.stack([result[0] for result in closed]),
-        jnp.stack([result[1] for result in closed]),
+        grad_x,
+        grad_vec,
         sum_mats,
         sum_vecs,
         new_mats,

time: 366 us -> 276 us (0.75); the launches traced: 368 us -> 272 us
  Pallas kernels: 143 us -> 257 us
  blocking collectives: 82.1 us -> 0 us
  starting transfers between devices: 59.3 us -> 0 us
  waiting for transfers between devices: 49.9 us -> 0 us
  between operations: 14.9 us -> 0.81 us
  other arithmetic: 9.97 us -> 6.03 us
    pallas_call x2, Pallas kernels: 5.78 us -> 129 us  [the longest x1 76.7 us: shards(): pl.pallas_call(partial(close_kernel, cells, depth, micros, sources), out_...]
    ppermute x25 -> x0, starting transfers between devices: 59.2 us -> none  [from_behind(): lax.ppermute(shard, axis, [(i, (i + by) % length) for i in range(length)])]
    psum x1 -> x0, blocking collectives: 58.6 us -> none  [shards(): sum_vecs = lax.psum(grad_v, ('cells', 'depth')).reshape(-1)]
    psum x1 -> x0, waiting for transfers between devices: 32.3 us -> none  [shards(): sum_mats = lax.psum(sum_mats, 'depth').reshape(-1)]
    unnamed x1 -> x0, blocking collectives: 23.5 us -> none
    ppermute x25 -> x0, waiting for transfers between devices: 17.5 us -> none  [from_behind(): lax.ppermute(shard, axis, [(i, (i + by) % length) for i in range(length)])]
    pallas_call x2, Pallas kernels: 108 us -> 98.8 us  [shards(): pl.pallas_call(partial(edge_kernel, micro, domains, buckets, atoms, width...]
  transfers between devices with their start and end apart: 28 -> 0, of which waited for: 4 -> 0; matrix products, arithmetic and copies ran while one was open for 3% -> 0% of each run, Pallas kernels for 24% -> 0%
where the time goes in v2:
time: 276 us; the launch traced here: 272 us
  Pallas kernels  257 us (93%)
  local copies, waits for them, and re-layouts  8.31 us (3%)
  other arithmetic  6.03 us (2%)
    pallas_call x2, Pallas kernels, shards(): pl.pallas_call(partial(edge_kernel, micro, domains, buckets, atoms, width...  98.8 us
    pallas_call x1, Pallas kernels, shards(): pl.pallas_call(partial(close_kernel, cells, depth, micros, sources), out_...  76.7 us
    pallas_call x1, Pallas kernels, shards(): pl.pallas_call(partial(fetch_kernel, cells, depth, micros, sources, faces...  52.6 us
    pallas_call x1, Pallas kernels, shards(): pl.pallas_call(partial(prep_kernel, block_of, buckets), out_shape=(jax.Sh...  26.8 us

profile of v2, /device:TPU:0, one launch (start us, length us, event | category | flops | bytes accessed | tf_op | source)
XLA Modules:
  0.0 272.3 jit_solution(340644213800892223)
XLA Ops:
  0.6 2.3 norm.1
  3.0 1.3 reshape.55
  4.3 0.7 convert_element_type.5
  5.0 0.6 pad_bitcast_fusion.refs_4_
  5.6 52.6 %fetch.1 = (bf16[4,128,256]{2,1,0:T(8,128)(2,1)}, bf16[4,128,256]{2,1,0:T(8,128)(2,1)}, bf16[4,128,256]{2,1,0:T(8,128)(2,1)}, bf16[4,128,256]{2,1,0:T(8,128)(2,1...) custom-call(bf16[4,128,256]{2,1,0:T(8,128)(2,1)} %get-tuple-element., ...), custom_call_target="tpu_custom_call" | custom-call | tf_op jit(solution)/shard_map/fetch/pallas_call | solution.py:900
  58.2 0.7 copy.30
  58.9 0.6 copy.31.list_ref
  59.5 26.8 %prep.1 = (bf16[2,9472,128]{2,1,0:T(8,128)(2,1)}, s32[2,3]{1,0:T(2,128)}) custom-call(s32[2,64,128]{2,1,0:T(8,128)} %nbr_ref.1, s32[2,64,128]{2,1,0:T(8,128)} %mask_ref.1, f32[2,3,64,128]{3,2,1,0:T(8,128)} %geom_ref.1, s32[2,12,128]{2,1,0:T(8,128)} %copy.31.list_ref), custom_call_target="tpu_custom_call" | custom-call | tf_op jit(solution)/shard_map/prep/pallas_call | solution.py:942
  86.3 0.7 copy.36
  87.0 0.7 reshape.61.refs_14_.refs_3_
  87.6 1.3 copy.32.refs_1_
  88.9 46.2 %edges.2 = (f32[128,256]{1,0:T(8,128)}, f32[3,128,256]{2,1,0:T(8,128)}, f32[4,128,256]{2,1,0:T(8,128)}, bf16[4,128,256]{2,1,0:T(8,128)(2,1)}, bf16[4,128,256]{2,...) custom-call(s32[2,3]{1,0:T(2,128)} %get-tuple-element.58.refs_0_, ...), custom_call_target="tpu_custom_call" | custom-call | tf_op jit(solution)/shard_map/edges/pallas_call | solution.py:1008
  135.1 52.6 %edges.3 = (f32[128,256]{1,0:T(8,128)}, f32[3,128,256]{2,1,0:T(8,128)}, f32[4,128,256]{2,1,0:T(8,128)}, bf16[4,128,256]{2,1,0:T(8,128)(2,1)}, bf16[4,128,256]{2,...) custom-call(s32[2,3]{1,0:T(2,128)} %get-tuple-element.58.refs_0_, ...), custom_call_target="tpu_custom_call" | custom-call | tf_op jit(solution)/shard_map/edges/pallas_call | solution.py:1008
  187.7 0.0 copy-start
  187.7 0.0 copy-start.5
  187.7 0.0 copy-start.6
  187.7 0.0 copy-start.10
  187.7 0.0 copy-start.11
  187.8 0.0 copy-start.12
  187.8 0.0 copy-start.3
  187.8 0.0 copy-start.4
  187.8 76.7 %close.1 = (f32[2,128,256]{2,1,0:T(8,128)}, f32[2,3,128,256]{3,2,1,0:T(8,128)}, f32[4,184,128]{2,1,0:T(8,128)}, f32[28,128]{1,0:T(8,128)}) custom-call(f32[2,128,256]{2,1,0:T(8,128)} %refs_0_.1, f32[2,128,256]{2,1,0:T(8,128)} %refs_1_.3, f32[2,3,128,256]{3,2,1,0:T(8,128)} %refs_2_.1, bf16[28,128]{1,0:T(8,128)(2,1)} %reshape.61.refs_14_.refs_3_, ...), custom_call_target="tpu_custom_call" | custom-call | tf_op jit(solution)/shard_map/close/pallas_call | solution.py:1046
  264.5 0.0 copy-start.8
  264.5 0.0 copy-start.9
  264.5 0.0 copy-start.7
  264.5 0.0 copy-start.2
  264.5 0.0 copy-done
  264.5 0.0 copy-done.5
  264.6 0.0 copy-done.6
  264.6 0.0 copy-start.1
  264.6 2.3 multiply_subtract_fusion
  266.9 0.0 copy-done.10
  266.9 0.0 copy-done.11
  266.9 0.0 copy-done.12
  266.9 1.4 multiply_subtract_fusion.1
  268.2 0.0 copy-done.3
  268.3 0.0 copy-done.4
  268.3 1.0 pad_maximum_fusion
  269.2 0.0 copy-done.8
  269.2 0.0 copy-done.9
  269.2 0.7 pad_maximum_fusion.1
  269.9 0.0 copy-done.7
  269.9 0.7 copy.40
  270.7 0.0 copy-done.2
  270.7 0.9 copy.41
  271.5 0.0 copy-done.1
  271.5 0.8 copy.42
Async XLA Ops:
  187.7 76.8 %copy-start = (f32[94208]{0:T(1024)S(1)}, f32[94208]{0:T(1024)}, u32[]{:S(2)}) copy-start(f32[94208]{0:T(1024)} %param.19) | copy-start | bytes 1130500
  187.7 76.8 %copy-start.5 = (f32[94208]{0:T(1024)S(1)}, f32[94208]{0:T(1024)}, u32[]{:S(2)}) copy-start(f32[94208]{0:T(1024)} %param.21) | copy-start | bytes 1130500
  187.7 76.8 %copy-start.6 = (f32[94208]{0:T(1024)S(1)}, f32[94208]{0:T(1024)}, u32[]{:S(2)}) copy-start(f32[94208]{0:T(1024)} %param.22) | copy-start | bytes 1130500
  187.7 79.1 %copy-start.10 = (f32[448]{0:T(512)S(1)}, f32[448]{0:T(512)}, u32[]{:S(2)}) copy-start(f32[448]{0:T(512)} %param.20) | copy-start | bytes 5380
  187.7 79.1 %copy-start.11 = (f32[448]{0:T(512)S(1)}, f32[448]{0:T(512)}, u32[]{:S(2)}) copy-start(f32[448]{0:T(512)} %param.23) | copy-start | bytes 5380
  187.8 79.1 %copy-start.12 = (f32[448]{0:T(512)S(1)}, f32[448]{0:T(512)}, u32[]{:S(2)}) copy-start(f32[448]{0:T(512)} %param.24) | copy-start | bytes 5380
  187.8 80.5 %copy-start.3 = (f32[3,128,256]{2,1,0:T(8,128)S(1)}, f32[3,128,256]{2,1,0:T(8,128)}, u32[]{:S(2)}) copy-start(f32[3,128,256]{2,1,0:T(8,128)} %get-tuple-element.76) | copy-start | bytes 1179652
  187.8 80.5 %copy-start.4 = (f32[3,128,256]{2,1,0:T(8,128)S(1)}, f32[3,128,256]{2,1,0:T(8,128)}, u32[]{:S(2)}) copy-start(f32[3,128,256]{2,1,0:T(8,128)} %get-tuple-element.77) | copy-start | bytes 1179652
  264.5 4.7 %copy-start.8 = (f32[128,256]{1,0:T(8,128)S(1)}, f32[128,256]{1,0:T(8,128)}, u32[]{:S(2)}) copy-start(f32[128,256]{1,0:T(8,128)} %get-tuple-element.67) | copy-start | bytes 393220
  264.5 4.7 %copy-start.9 = (f32[128,256]{1,0:T(8,128)S(1)}, f32[128,256]{1,0:T(8,128)}, u32[]{:S(2)}) copy-start(f32[128,256]{1,0:T(8,128)} %get-tuple-element.75) | copy-start | bytes 393220
  264.5 5.4 %copy-start.7 = (f32[2,128,256]{2,1,0:T(8,128)S(1)}, f32[2,128,256]{2,1,0:T(8,128)}, u32[]{:S(2)}) copy-start(f32[2,128,256]{2,1,0:T(8,128)} %get-tuple-element.117) | copy-start | bytes 786436
  264.5 6.1 %copy-start.2 = (f32[2,3,128,256]{3,2,1,0:T(8,128)S(1)}, f32[2,3,128,256]{3,2,1,0:T(8,128)}, u32[]{:S(2)}) copy-start(f32[2,3,128,256]{3,2,1,0:T(8,128)} %get-tuple-element.118) | copy-start | bytes 2359300
  264.6 7.0 %copy-start.1 = (f32[4,184,128]{2,1,0:T(8,128)S(1)}, f32[4,184,128]{2,1,0:T(8,128)}, u32[]{:S(2)}) copy-start(f32[4,184,128]{2,1,0:T(8,128)} %get-tuple-element.94) | copy-start | bytes 1130500

commit v3 on v2

v3 whole, which is shorter than its diff:
```python
from functools import partial
import math

import jax
import jax.numpy as jnp
from jax import lax
from jax.experimental import pallas as pl
from jax.experimental.pallas import tpu as pltpu
from jax.sharding import PartitionSpec as P

HEADS = 8
NR = 32
FOLD = 4
STEP = 3

LANES = 128
ROWS = 256
UNIT = 256
BLOCK_SLOTS = 4
TILE = 192

norm_eps = 1e-05
cut_radius = 5.0
beta_one = 0.5
beta_two = 0.5
learn_rate = 0.05
decay_rate = 0.01
adam_eps = 1e-08

f32 = jnp.float32
bf16 = jnp.bfloat16
i32 = jnp.int32

VMEM_LIMIT = 60 * 1024 * 1024


def dot_nn(left, right):
    return lax.dot_general(left, right, (((1,), (0,)), ((), ())), preferred_element_type=f32)


def dot_nt(left, right):
    return lax.dot_general(left, right, (((1,), (1,)), ((), ())), preferred_element_type=f32)


def dot_tn(left, right):
    return lax.dot_general(left, right, (((0,), (0,)), ((), ())), preferred_element_type=f32)


def lane_mean(block):
    return jnp.sum(block, axis=-1, keepdims=True) * (1.0 / block.shape[-1])


def normalise(block):
    centered = block - lane_mean(block)
    spread = lax.rsqrt(lane_mean(centered * centered) + norm_eps)
    return centered * spread, spread


def norm_kernel(x_ref, vec_ref, mats_ref, own_ref, low_ref):
    quarter = low_ref.shape[1]
    for part in range(low_ref.shape[0]):
        low_ref[part] = mats_ref[part * quarter : (part + 1) * quarter, :].astype(bf16)
    for micro in range(x_ref.shape[0]):
        own_ref[micro, 0] = normalise(x_ref[micro])[0].astype(bf16)
        own_ref[micro, 1:] = vec_ref[micro].astype(bf16)


Q_AT, K_AT, V_AT, VEC_AT, O_AT, DK_AT, DV_AT = 0, 512, 1024, 2560, 4096, 5632, 5696
W_Q, W_K, W_V, W_VEC, W_O = 0, 1, 2, 5, 8
FEATS = 48
CHUNK = 16
GATH, PER_ATOM, FILT, SUMS, KEPT, WORK = 0, 7, 12, 16, 18, 24


def edge_features(nbr, mask, geom, lists, block_of, buckets, feat, place, count_vec):
    slots, atoms = nbr.shape
    blocks = slots // BLOCK_SLOTS
    live = mask > 0
    halo_at = nbr - atoms
    list_row = halo_at >> 7
    list_lane = halo_at & (LANES - 1)
    atom_in = nbr
    block_id = jnp.zeros_like(nbr)
    for row in range(lists.shape[0]):
        table = jnp.broadcast_to(lists[row : row + 1, :], (slots, atoms))
        picked = jnp.take_along_axis(table, list_lane, axis=1)
        here = list_row == row
        atom_in = jnp.where(here, picked, atom_in)
        block_id = jnp.where(here, block_of[row], block_id)
    entry = block_id * atoms + atom_in
    bucket = entry >> 8
    low = ((entry & (ROWS - 1)) + 1).astype(f32)
    atom_id = (lax.broadcasted_iota(i32, (slots, atoms), 1) + 1).astype(f32)
    live_float = live.astype(f32)

    radius = jnp.sqrt(geom[0] * geom[0] + geom[1] * geom[1] + geom[2] * geom[2])
    units = [comp / radius for comp in geom]
    cut = 0.5 * (jnp.cos(math.pi * radius / cut_radius) + 1.0) * live_float
    cut_high = cut.astype(bf16).astype(f32)
    cut_low = cut - cut_high
    decayed = jnp.exp(-(5.0 / cut_radius) * radius)
    start_value = math.exp(-cut_radius)
    ramp = lax.broadcasted_iota(i32, (NR, 1), 0).astype(f32) / float(NR - 1)
    centers = start_value * (1.0 - ramp) + ramp
    width_coef = (2.0 / NR * (1.0 - start_value)) ** (-2)
    extras = [live_float, low, atom_id, cut_high, cut_low] + units
    zeros = jnp.zeros((16 - len(extras), atoms), f32)
    for slot in range(slots):
        gap = decayed[slot : slot + 1, :] - centers
        basis = cut[slot : slot + 1, :] * jnp.exp(-width_coef * gap * gap)
        feat[slot, 0:NR, :] = basis.astype(bf16)
        rows = [extra[slot : slot + 1, :] for extra in extras] + [zeros]
        feat[slot, NR : NR + 16, :] = jnp.concatenate(rows, axis=0).astype(bf16)

    members = [jnp.where(live & (bucket == b), 1.0, 0.0) for b in range(buckets)]
    lane_from = lax.broadcasted_iota(i32, (atoms, 2 * atoms), 0)
    lane_to = lax.broadcasted_iota(i32, (atoms, 2 * atoms), 1)
    before = jnp.where((lane_from < lane_to) | (lane_to >= atoms), 1.0, 0.0).astype(bf16)
    slot_to = lax.broadcasted_iota(i32, (slots, slots), 0)
    slot_from = lax.broadcasted_iota(i32, (slots, slots), 1)
    same = (slot_to // BLOCK_SLOTS) == (slot_from // BLOCK_SLOTS)
    earlier = jnp.where(same & (slot_from < slot_to), 1.0, 0.0).astype(bf16)
    block_row = lax.broadcasted_iota(i32, (blocks, slots), 0)
    block_slot = lax.broadcasted_iota(i32, (blocks, slots), 1)
    gather_block = jnp.where(block_slot // BLOCK_SLOTS == block_row, 1.0, 0.0).astype(bf16)
    lane = lax.broadcasted_iota(i32, (blocks, LANES), 1)
    rank = jnp.zeros((slots, atoms), f32)
    counts = jnp.zeros((blocks, LANES), f32)
    for b in range(buckets):
        sums = dot_nn(members[b].astype(bf16), before)
        row_total = sums[:, atoms:].astype(bf16)
        offset = sums[:, :atoms] + dot_nn(earlier, row_total)
        rank = jnp.where(members[b] > 0.0, offset, rank)
        counts = jnp.where(lane == b, dot_nn(gather_block, row_total), counts)
    place[...] = jnp.where(live, bucket * 1024 + rank.astype(i32), -1)
    count_vec[...] = counts.astype(i32)


def pack_edges(blocks, atoms, buckets, feat, place, count_sc, packed):
    wide = BLOCK_SLOTS * atoms

    def total_body(block, totals):
        return tuple(
            total + (((count_sc[block, b] + 7) >> 3) << 3) for b, total in enumerate(totals)
        )

    totals = lax.fori_loop(0, blocks, total_body, (jnp.int32(0),) * buckets)
    held = [(total + (UNIT - 1)) >> 8 for total in totals]
    bases = [jnp.int32(UNIT)]
    for total in totals:
        bases.append(bases[-1] + (((total + (2 * UNIT - 1)) >> 8) << 8))

    def picks(places, b, first):
        wanted = lax.broadcasted_iota(i32, (TILE, wide), 0) + (b * 1024 + first)
        return jnp.where(places == wanted, 1.0, 0.0).astype(bf16)

    def block_body(block, at):
        first = block * BLOCK_SLOTS
        places = jnp.concatenate(
            [place[pl.ds(first + t, 1), :] for t in range(BLOCK_SLOTS)], axis=1
        )
        feats = jnp.concatenate([feat[first + t] for t in range(BLOCK_SLOTS)], axis=1)
        following = []
        for b in range(buckets):
            number = count_sc[block, b]
            packed[pl.ds(pl.multiple_of(at[b], 8), TILE), :] = dot_nt(picks(places, b, 0), feats)

            @pl.when(number > TILE)
            def _(b=b, number=number):
                def tile_body(tile, carry):
                    feats = jnp.concatenate([feat[first + t] for t in range(BLOCK_SLOTS)], axis=1)
                    pick = picks(places, b, tile * TILE)
                    start = pl.multiple_of(at[b] + tile * TILE, 8)
                    packed[pl.ds(start, TILE), :] = dot_nt(pick, feats)
                    return carry

                lax.fori_loop(1, (number + (TILE - 1)) // TILE, tile_body, 0)

            following.append(at[b] + (((number + 7) >> 3) << 3))
        return tuple(following)

    ends = lax.fori_loop(0, blocks, block_body, tuple(bases[:buckets]))
    zeros = jnp.zeros((UNIT, LANES), f32)
    for end in ends:
        packed[pl.ds(pl.multiple_of(end, 8), UNIT), :] = zeros
    packed[0:UNIT, :] = zeros
    return held, bases


def edge_kernel(domains, buckets, block_of, *refs):
    refs = list(refs)
    count_ref, nbr_ref, mask_ref, geom_ref, list_ref, x_ref, vec_ref, cotx_ref, cotv_ref = refs[:9]
    halo_refs = refs[9 : 9 + domains - 1]
    at = 9 + domains - 1
    w_ref, v_ref = refs[at : at + 2]
    at += 2
    outx_ref, outv_ref, gown_ref = refs[at : at + 3]
    at += 3
    back_refs = refs[at : at + domains - 1]
    at += domains - 1
    gm_ref, gv_ref = refs[at : at + 2]
    at += 2
    (
        feat,
        place,
        count_vec,
        count_sc,
        packed,
        sem,
        wide_w,
        wb,
        wd,
        norm_table,
        tab,
        acc,
        atom_tab,
        proj,
        go,
        agg,
        gwd,
        heads,
    ) = refs[at : at + 18]
    rest = refs[at + 18 :]
    sides = [tuple(rest[side::2]) for side in range(2)]
    micro = pl.program_id(0)
    slots, atoms = nbr_ref.shape[1:]
    feat_width = x_ref.shape[2]
    cells, parts_w, quarter = w_ref.shape[:3]
    parts = [slice(axis * atoms, (axis + 1) * atoms) for axis in range(3)]

    def vector(index):
        both = [v_ref[2 * index + half : 2 * index + half + 1, :].astype(f32) for half in range(2)]
        return jnp.concatenate(both, axis=1)

    @pl.when(micro == 0)
    def _():
        feat[...] = jnp.zeros_like(feat)
        for ref in sides[1][6:]:
            ref[...] = jnp.zeros_like(ref)
        gwd[...] = jnp.zeros_like(gwd)
        for cell in range(cells):
            for part in range(parts_w):
                start = (cell * parts_w + part) * quarter
                wide_w[start : start + quarter, :] = w_ref[cell, part].astype(f32)

        def weight_block(first, stride, column, rows):
            halves = [
                wide_w[pl.ds(first + 2 * column + half, rows, stride=stride), :]
                for half in range(2)
            ]
            return jnp.concatenate(halves, axis=1)

        for slot, first, stride, count in (
            (W_Q, Q_AT, 2, 1),
            (W_K, K_AT, 2, 1),
            (W_V, V_AT, 6, 3),
            (W_VEC, VEC_AT, 6, 3),
            (W_O, O_AT, 6, 3),
        ):
            for column in range(count):
                wb[slot + column] = weight_block(first, stride, column, ROWS).astype(bf16)
        bias_row = lax.broadcasted_iota(i32, (LANES - NR, 1), 0) == 0
        for column in range(4):
            if column == 0:
                block = weight_block(DK_AT, 2, 0, NR)
            else:
                block = weight_block(DV_AT, 6, column - 1, NR)
            bias = jnp.where(bias_row, vector(10 + column), 0.0)
            cols = slice(column * ROWS, (column + 1) * ROWS)
            wd[:, cols] = (jnp.concatenate([block, bias], axis=0) * 0.5).astype(bf16)
        head_from = lax.broadcasted_iota(i32, (ROWS, ROWS), 0) // (feat_width // HEADS)
        head_to = lax.broadcasted_iota(i32, (ROWS, ROWS), 1) // (feat_width // HEADS)
        heads[...] = jnp.where(head_from == head_to, 0.5, 0.0).astype(bf16)

    geom = [geom_ref[0, axis] for axis in range(3)]
    edge_features(
        nbr_ref[0], mask_ref[0], geom, list_ref[0], block_of, buckets, feat, place, count_vec
    )
    copy = pltpu.make_async_copy(count_vec, count_sc, sem)
    copy.start()

    gain = vector(0)
    shift = vector(1)
    own_hat, unused = normalise(x_ref[0])
    vec_low = vec_ref[0].astype(bf16)
    for domain in range(2 * buckets):
        rows = slice(domain * atoms, (domain + 1) * atoms)
        here = slice((domain % 2) * atoms, (domain % 2 + 1) * atoms)
        if domain == 0:
            norm_table[rows, :] = (own_hat * gain + shift).astype(bf16)
        elif domain < domains:
            hat = halo_refs[domain - 1][0, 0].astype(f32)
            norm_table[rows, :] = (hat * gain + shift).astype(bf16)
        else:
            norm_table[rows, :] = jnp.zeros((atoms, feat_width), bf16)
        for axis in range(3):
            cols = slice((4 + axis) * ROWS, (5 + axis) * ROWS)
            if domain < domains:
                block = vec_low[axis] if domain == 0 else halo_refs[domain - 1][0, 1 + axis]
            else:
                block = jnp.zeros((atoms, feat_width), bf16)
            tab[domain // 2, here, cols] = block
    for b in range(buckets):
        rows = slice(b * ROWS, (b + 1) * ROWS)
        for column in range(4):
            cols = slice(column * ROWS, (column + 1) * ROWS)
            made = dot_nn(norm_table[rows, :], wb[W_K + column]) + vector(3 + column)
            tab[b, :, cols] = made.astype(bf16)

    live = (lax.broadcasted_iota(i32, (atoms, 1), 0) < count_ref[micro, 0]).astype(f32)
    query = dot_nn(norm_table[0:atoms, :], wb[W_Q]) + vector(2)
    atom_tab[:, 0:ROWS] = query.astype(bf16)
    vec_rows = vec_low.reshape(3 * atoms, feat_width)
    for part in range(3):
        proj[part] = dot_nn(vec_rows, wb[W_VEC + part])
    cot_x = cotx_ref[0] * live
    vec_dot = jnp.zeros((atoms, feat_width), f32)
    go_one = jnp.zeros((atoms, feat_width), f32)
    for axis in range(3):
        cot_v = cotv_ref[0, axis] * live
        vec_dot += proj[0, parts[axis], :] * proj[1, parts[axis], :]
        go_one += proj[2, parts[axis], :] * cot_v
        atom_tab[:, (2 + axis) * ROWS : (3 + axis) * ROWS] = cot_v.astype(bf16)
    go[0] = go_one.astype(bf16)
    go[1] = (vec_dot * cot_x).astype(bf16)
    go[2] = cot_x.astype(bf16)
    g_agg = dot_nt(go[0], wb[W_O])
    for part in range(1, 3):
        g_agg += dot_nt(go[part], wb[W_O + part])
    atom_tab[:, ROWS : 2 * ROWS] = g_agg.astype(bf16)
    agg[...] = jnp.zeros_like(agg)
    for b in range(buckets):
        acc[b] = jnp.zeros((ROWS, 7 * ROWS), f32)

    copy.wait()
    held, bases = pack_edges(
        slots // BLOCK_SLOTS, atoms, buckets, feat, place, count_sc, packed
    )
    firsts = [jnp.int32(0)]
    for number in held:
        firsts.append(firsts[-1] + number)
    total_units = firsts[-1]

    def bucket_of(unit):
        b = jnp.int32(0)
        for at in range(1, buckets):
            b = b + jnp.where(unit >= firsts[at], 1, 0)
        return b

    def rows_of(unit):
        start = jnp.int32(0)
        for at in range(buckets):
            inside = (unit >= firsts[at]) & (unit < firsts[at + 1])
            start = jnp.where(inside, bases[at] + (unit - firsts[at]) * UNIT, start)
        return pl.ds(pl.multiple_of(start, UNIT), UNIT)

    def block_cols(block):
        return slice(block * ROWS, (block + 1) * ROWS)

    def hits(side, rows):
        hit, atom_one = side[:2]
        full = packed[rows, :]
        lane_row = lax.broadcasted_iota(i32, (UNIT, ROWS), 1).astype(f32) + 1.0
        lane_atom = lax.broadcasted_iota(i32, (UNIT, LANES), 1).astype(f32) + 1.0
        hit[...] = jnp.where(full[:, NR + 1 : NR + 2] == lane_row, 1.0, 0.0).astype(bf16)
        atom_one[...] = jnp.where(full[:, NR + 2 : NR + 3] == lane_atom, 1.0, 0.0).astype(bf16)

    def spread(side, rows):
        cutb, dirs = side[3:5]
        full = packed[rows, :]
        for axis in range(3):
            column = full[:, NR + 5 + axis : NR + 6 + axis]
            dirs[axis] = jnp.broadcast_to(column, (UNIT, LANES))
        column = full[:, NR + 3 : NR + 4] + full[:, NR + 4 : NR + 5]
        cutb[...] = jnp.broadcast_to(column, (UNIT, LANES))

    def gather_steps(side, unit):
        hit, atom_one, work = side[:3]
        b = jnp.minimum(bucket_of(unit), buckets - 1)
        rows = rows_of(unit)

        def gather_table(block):
            work[:, block_cols(GATH + block)] = dot_nn(hit[...], tab[b, :, block_cols(block)])

        def gather_atom(block):
            made = dot_nn(atom_one[...], atom_tab[:, block_cols(block)])
            work[:, block_cols(PER_ATOM + block)] = made

        def filters(block):
            low = packed[rows, :].astype(bf16)
            work[:, block_cols(FILT + block)] = dot_nn(low, wd[:, block_cols(block)])

        return (
            [partial(gather_table, block) for block in range(7)]
            + [partial(gather_atom, block) for block in range(5)]
            + [partial(filters, block) for block in range(4)]
        )

    def mix(first, second):
        done = 0
        for at, step in enumerate(first):
            step()
            until = (at + 1) * len(second) // len(first)
            for other in second[done:until]:
                other()
            done = until

    chunks = [
        (slice(start, start + CHUNK), half)
        for start in range(0, UNIT, CHUNK)
        for half in range(2)
    ]

    def put(ref, block, here, half, value):
        ref[2 * block + half, here, :] = value.astype(bf16)

    def reader(work):
        def part(block, here, half):
            start = block * ROWS + half * LANES
            return work[here, start : start + LANES]

        def gate(here, block, half):
            value = part(FILT + block, here, half)
            turn = jnp.tanh(value)
            lift = 1.0 + turn
            silu = value * lift
            return silu, lift + silu * (1.0 - turn)

        return part, gate

    def heads_stage(side, here, half):
        work, pair = side[2], side[5]
        part, gate = reader(work)

        def keep(block, value):
            start = (KEPT + block) * ROWS + half * LANES
            work[here, start : start + LANES] = value

        there = slice(UNIT + here.start, UNIT + here.stop)
        silu, slope = gate(here, 0, half)
        query_e = part(PER_ATOM, here, half)
        key_e = part(GATH, here, half)
        gated = query_e * silu
        keep(0, gated)
        keep(1, query_e * key_e * slope)
        keep(2, key_e * silu)
        pair[half, here, :] = (gated * key_e).astype(bf16)
        silu, slope = gate(here, 1, half)
        cot_e = part(PER_ATOM + 1, here, half)
        value_e = part(GATH + 1, here, half)
        gated = value_e * silu
        keep(3, cot_e * silu)
        keep(4, cot_e * value_e * slope)
        keep(5, gated)
        pair[half, there, :] = (cot_e * gated).astype(bf16)

    def head_sums(side):
        work, pair = side[2], side[5]
        for at in range(2):
            rows = slice(at * UNIT, (at + 1) * UNIT)
            both = jnp.concatenate([pair[0, rows, :], pair[1, rows, :]], axis=1)
            work[:, block_cols(SUMS + at)] = dot_nn(both, heads[...])

    def vector_stage(side, here, half):
        dirs, dedge, dfilt, msg = side[4], *side[6:]
        part, gate = reader(side[2])
        cots = [part(PER_ATOM + 2 + axis, here, half) for axis in range(3)]
        vecs = [part(GATH + 4 + axis, here, half) for axis in range(3)]
        turns = [dirs[axis, here, :] for axis in range(3)]
        silu, slope = gate(here, 2, half)
        value_e = part(GATH + 2, here, half)
        gated = value_e * silu
        down = cots[0] * vecs[0] + cots[1] * vecs[1] + cots[2] * vecs[2]
        for axis in range(3):
            put(msg, 1 + axis, here, half, vecs[axis] * gated)
            put(dedge, 4 + axis, here, half, cots[axis] * gated)
        put(dedge, 2, here, half, down * silu)
        put(dfilt, 2, here, half, down * value_e * slope)
        silu, slope = gate(here, 3, half)
        value_e = part(GATH + 3, here, half)
        down = cots[0] * turns[0] + cots[1] * turns[1] + cots[2] * turns[2]
        put(dedge, 3, here, half, down * silu)
        put(dfilt, 3, here, half, down * value_e * slope)
        put(msg, 5, here, half, value_e * silu)

    def score_stage(side, here, half):
        cutb, dedge, dfilt, msg = side[3], *side[6:]
        part, unused = reader(side[2])
        cut = cutb[here, :]
        score = part(SUMS, here, half)
        turn = jnp.tanh(score)
        lift = 1.0 + turn
        silu = score * lift
        attention = silu * cut
        dscore = part(SUMS + 1, here, half) * cut * (lift + silu * (1.0 - turn))
        put(dedge, 0, here, half, dscore * part(KEPT, here, half))
        put(dfilt, 0, here, half, dscore * part(KEPT + 1, here, half))
        put(msg, 4, here, half, dscore * part(KEPT + 2, here, half))
        put(dedge, 1, here, half, attention * part(KEPT + 3, here, half))
        put(dfilt, 1, here, half, attention * part(KEPT + 4, here, half))
        put(msg, 0, here, half, attention * part(KEPT + 5, here, half))

    def both_halves(ref, block):
        return jnp.concatenate([ref[2 * block], ref[2 * block + 1]], axis=1)

    def scatter_steps(side, unit):
        dedge, dfilt, msg = side[6:]
        b = jnp.minimum(bucket_of(unit), buckets - 1)
        turned = packed[rows_of(unit), :].T

        def across(index):
            return turned[NR + index : NR + index + 1, :]

        sub_row = lax.broadcasted_iota(i32, (ROWS, UNIT), 0).astype(f32) + 1.0
        sub_atom = lax.broadcasted_iota(i32, (atoms, UNIT), 0).astype(f32) + 1.0
        hit_t = jnp.where(across(1) == sub_row, 1.0, 0.0).astype(bf16)
        atom_hit = across(2) == sub_atom
        atom_t = jnp.where(atom_hit, 1.0, 0.0).astype(bf16)
        feats_t = turned[0:FEATS, :].astype(bf16)
        turn = both_halves(msg, 5)

        def add_vector(axis):
            along = jnp.where(atom_hit, across(5 + axis), 0.0).astype(bf16)
            agg[:, block_cols(1 + axis)] += dot_nn(
                jnp.concatenate([atom_t, along], axis=1),
                jnp.concatenate([both_halves(msg, 1 + axis), turn], axis=0),
            )

        def add_table(block):
            acc[b, :, block_cols(block)] += dot_nn(hit_t, both_halves(dedge, block))

        def add_filter(block):
            gwd[:, block_cols(block)] += dot_nn(feats_t, both_halves(dfilt, block))

        def add_atom(block):
            agg[:, block_cols(block)] += dot_nn(atom_t, both_halves(msg, block))

        return (
            [partial(add_vector, axis) for axis in range(3)]
            + [partial(add_table, block) for block in (2, 3, 4, 5, 6, 0, 1)]
            + [partial(add_filter, block) for block in (2, 3, 0, 1)]
            + [partial(add_atom, block) for block in (0, 4)]
        )

    def on_chunks(stage, side):
        return [partial(stage, side, here, half) for here, half in chunks]

    hits(sides[0], rows_of(jnp.int32(0)))
    mix(gather_steps(sides[0], jnp.int32(0)), [])

    def pair_body(step, carry):
        for at in range(2):
            unit = 2 * step + at
            mine, other = sides[at], sides[1 - at]

            @pl.when(count_sc[0, 0] >= 0)
            def _(unit=unit, mine=mine, other=other):
                spread(mine, rows_of(unit))
                hits(other, rows_of(unit + 1))
                mix(scatter_steps(other, unit - 1), on_chunks(heads_stage, mine))

            @pl.when(count_sc[0, 0] >= 0)
            def _(unit=unit, mine=mine, other=other):
                head_sums(mine)
                mix(
                    gather_steps(other, unit + 1),
                    [step for two in zip(on_chunks(vector_stage, mine), on_chunks(score_stage, mine)) for step in two],
                )

        return carry

    steps = (total_units + 1) // 2
    lax.fori_loop(0, steps, pair_body, 0)
    mix(scatter_steps(sides[1], 2 * steps - 1), [])

    agg_low = agg[:, 0:ROWS].astype(bf16)
    outs = [dot_nn(agg_low, wb[W_O + part]) + vector(7 + part) for part in range(3)]
    outx_ref[0] = x_ref[0] + (vec_dot * outs[1] + outs[2]) * live
    g_dot = cot_x * outs[1]
    for axis in range(3):
        rows = parts[axis]
        vec_agg = agg[:, block_cols(1 + axis)]
        outv_ref[0, axis] = vec_ref[0, axis] + (proj[2, rows, :] * outs[0] + vec_agg) * live
        proj[2, rows, :] = cotv_ref[0, axis] * live * outs[0]
        first_part = proj[0, rows, :]
        proj[0, rows, :] = g_dot * proj[1, rows, :]
        proj[1, rows, :] = g_dot * first_part

    later = micro > 0

    def put_grad(first, stride, column, rows, value):
        for half in range(2):
            at = pl.ds(first + 2 * column + half, rows, stride=stride)
            before = jnp.where(later, wide_w[at, :], 0.0)
            wide_w[at, :] = value[:, half * LANES : (half + 1) * LANES] + before

    def put_vector(index, value):
        for half in range(2):
            row = slice(2 * index + half, 2 * index + half + 1)
            before = jnp.where(later, gv_ref[row, :], 0.0)
            gv_ref[row, :] = value[:, half * LANES : (half + 1) * LANES] + before

    def column_sum(value):
        return jnp.sum(value.astype(f32), axis=0, keepdims=True)

    put_vector(0, jnp.zeros((1, ROWS), f32))
    put_vector(1, jnp.zeros((1, ROWS), f32))
    g_vec = jnp.zeros((3 * atoms, feat_width), f32)
    for part_at in range(3):
        put_grad(O_AT, 6, part_at, ROWS, dot_tn(agg_low, go[part_at]))
        put_vector(7 + part_at, column_sum(go[part_at]))
        gp = proj[part_at].astype(bf16)
        put_grad(VEC_AT, 6, part_at, ROWS, dot_tn(vec_rows, gp))
        g_vec += dot_nt(gp, wb[W_VEC + part_at])

    g_query = agg[:, block_cols(4)].astype(bf16)
    put_grad(Q_AT, 2, 0, ROWS, dot_tn(norm_table[0:atoms, :], g_query))
    put_vector(2, column_sum(g_query))
    g_norm = dot_nt(g_query, wb[W_Q])

    sums = [jnp.zeros((ROWS, ROWS), f32) for column in range(4)]
    biases = [jnp.zeros((1, ROWS), f32) for column in range(4)]
    for b in range(buckets):
        rows = slice(b * ROWS, (b + 1) * ROWS)
        g_table = jnp.zeros((ROWS, ROWS), f32)
        for column in range(4):
            low = acc[b, :, block_cols(column)].astype(bf16)
            sums[column] += dot_tn(norm_table[rows, :], low)
            biases[column] += column_sum(low)
            g_table += dot_nt(low, wb[W_K + column])
        for half in range(2):
            domain = 2 * b + half
            if domain >= domains:
                continue
            here = slice(half * atoms, (half + 1) * atoms)
            if domain == 0:
                gown_ref[0, 0] = g_table[here, :] + g_norm
            else:
                back_refs[domain - 1][0, 0] = g_table[here, :].astype(bf16)
            for axis in range(3):
                block = acc[b, here, block_cols(4 + axis)]
                if domain == 0:
                    gown_ref[0, 1 + axis] = block + g_vec[parts[axis], :]
                else:
                    back_refs[domain - 1][0, 1 + axis] = block.astype(bf16)
    for column in range(4):
        if column == 0:
            put_grad(K_AT, 2, 0, ROWS, sums[column])
        else:
            put_grad(V_AT, 6, column - 1, ROWS, sums[column])
        put_vector(3 + column, biases[column])

    @pl.when(micro == pl.num_programs(0) - 1)
    def _():
        for column in range(4):
            block = gwd[0:NR, block_cols(column)] * 0.5
            first, stride, at = (DK_AT, 2, 0) if column == 0 else (DV_AT, 6, column - 1)
            for half in range(2):
                cols = slice(half * LANES, (half + 1) * LANES)
                wide_w[pl.ds(first + 2 * at + half, NR, stride=stride), :] = block[:, cols]
                row = 2 * (10 + column) + half
                bias = gwd[NR : NR + 1, column * ROWS + half * LANES :][:, :LANES]
                gv_ref[row : row + 1, :] = bias * 0.5
        for cell in range(cells):
            for part_at in range(parts_w):
                start = (cell * parts_w + part_at) * quarter
                gm_ref[part_at, cell] = wide_w[start : start + quarter, :].astype(bf16)


def core_mate(depth_at):
    return depth_at + 1 - 2 * (depth_at % 2)


def chip_mate(depth_at):
    return (depth_at + 2) % 4


def greet(cells, depth):
    barrier = pltpu.get_barrier_semaphore()
    cell_at, depth_at = lax.axis_index("cells"), lax.axis_index("depth")
    for by in range(1, cells):
        pl.semaphore_signal(barrier, inc=1, device_id={"cells": (cell_at + by) % cells})
    for by in range(1, depth):
        pl.semaphore_signal(barrier, inc=1, device_id={"depth": (depth_at + by) % depth})
    pl.semaphore_wait(barrier, cells + depth - 2)


def remote(source, target, send, receive, device):
    return pltpu.make_async_remote_copy(
        src_ref=source, dst_ref=target, send_sem=send, recv_sem=receive, device_id=device
    )


def fetch_kernel(cells, depth, micros, sources, faces, *refs):
    own_ref, lists_ref, w_ref, v_ref = refs[:4]
    halo_refs = refs[4 : 4 + len(sources)]
    got_lists, got_w, got_v = refs[4 + len(sources) : 7 + len(sources)]
    halo_send, halo_recv, list_send, list_recv, v_send, v_recv, w_send, w_recv = refs[
        7 + len(sources) :
    ]
    cell_at, depth_at = lax.axis_index("cells"), lax.axis_index("depth")
    sizes = {"cells": cells, "depth": depth}
    places = {"cells": cell_at, "depth": depth_at}
    got_w[cell_at] = w_ref[...]
    got_v[cell_at] = v_ref[...]
    greet(cells, depth)

    def ahead(axis, by):
        return {axis: (places[axis] + by) % sizes[axis]}

    started = []

    def start(*args):
        copy = remote(*args)
        copy.start()
        started.append(copy)
        return copy

    first = []
    for by in range(1, cells):
        there = ahead("cells", by)
        first.append(
            start(
                w_ref.at[depth_at],
                got_w.at[cell_at, depth_at],
                w_send.at[0, by],
                w_recv.at[0, by],
                there,
            )
        )
    lists = [
        start(
            lists_ref.at[face],
            got_lists.at[face],
            list_send.at[face],
            list_recv.at[face],
            ahead(axis, by),
        )
        for face, (axis, by) in enumerate(faces)
    ]
    vectors = [
        start(v_ref, got_v.at[cell_at], v_send.at[by], v_recv.at[by], ahead("cells", by))
        for by in range(1, cells)
    ]
    halos = []
    for micro in range(micros):
        for index, (axis, by) in enumerate(sources):
            halos.append(
                start(
                    own_ref.at[micro],
                    halo_refs[index].at[micro],
                    halo_send.at[micro, index],
                    halo_recv.at[micro, index],
                    ahead(axis, by),
                )
            )
    mate, other = core_mate(depth_at), chip_mate(depth_at)
    across = []
    last = []
    for by in range(1, cells):
        first[by - 1].wait_recv()
        piece = got_w.at[(cell_at + cells - by) % cells, depth_at]
        across.append(
            start(piece, piece, w_send.at[1, by], w_recv.at[1, by], {"depth": other})
        )
        last.append(start(piece, piece, w_send.at[2, by], w_recv.at[2, by], {"depth": mate}))
    for by in range(1, cells):
        across[by - 1].wait_recv()
        piece = got_w.at[(cell_at + cells - by) % cells, other]
        last.append(start(piece, piece, w_send.at[3, by], w_recv.at[3, by], {"depth": mate}))
    for copy in lists + vectors + last + halos:
        copy.wait_recv()
    for copy in started:
        copy.wait_send()


def close_kernel(cells, depth, micros, sources, *refs):
    x_ref, cotx_ref, cotv_ref, gain_ref, gvec_in, part_ref = refs[:6]
    refs = refs[6:]
    gown_ref = refs[0]
    back_refs = refs[1 : 1 + len(sources)]
    refs = refs[1 + len(sources) :]
    gx_ref, gvec_ref, summ_ref, sumv_ref = refs[:4]
    came, one_in, two_out, two_in, three_out, three_in, held, quad, octo = refs[4:13]
    halo_send, halo_recv, m_send, m_recv, c_send, c_recv, d_send, d_recv, e_send, e_recv, f_send, f_recv = refs[13:]
    cell_at, depth_at = lax.axis_index("cells"), lax.axis_index("depth")
    sizes = {"cells": cells, "depth": depth}
    places = {"cells": cell_at, "depth": depth_at}
    greet(cells, depth)

    def ahead(axis, by):
        return {axis: (places[axis] + by) % sizes[axis]}

    started = []

    def start(*args):
        copy = remote(*args)
        copy.start()
        started.append(copy)
        return copy

    mate, other = core_mate(depth_at), chip_mate(depth_at)
    mate_other = chip_mate(mate)
    one_far = start(
        part_ref.at[mate_other], one_in.at[1], m_send.at[0], m_recv.at[0], {"depth": mate}
    )
    one_near = start(part_ref.at[mate], one_in.at[0], m_send.at[1], m_recv.at[1], {"depth": mate})
    halos = []
    for micro in range(micros):
        for index, (axis, by) in enumerate(sources):
            halos.append(
                start(
                    back_refs[index].at[micro],
                    came.at[micro, index],
                    halo_send.at[micro, index],
                    halo_recv.at[micro, index],
                    ahead(axis, -by),
                )
            )
    one_far.wait_recv()
    two_out[...] = (part_ref[other].astype(f32) + one_in[1].astype(f32)).astype(bf16)
    two = start(two_out, two_in, m_send.at[2], m_recv.at[2], {"depth": other})
    one_near.wait_recv()
    two.wait_recv()
    for cell in range(cells):
        total = (
            part_ref[depth_at, cell].astype(f32)
            + one_in[0, cell].astype(f32)
            + two_in[cell].astype(f32)
        )
        three_out[cell] = total.astype(bf16)
    three = []
    for by in range(1, cells):
        there = (cell_at + by) % cells
        three.append(
            start(
                three_out.at[there],
                three_in.at[by],
                c_send.at[by],
                c_recv.at[by],
                {"cells": there},
            )
        )

    for copy in halos:
        copy.wait_recv()
    gain = jnp.concatenate([gain_ref[half : half + 1, :].astype(f32) for half in range(2)], axis=1)
    norm_grads = [jnp.zeros((1, gain.shape[1]), f32) for part in range(2)]
    for micro in range(micros):
        total = [gown_ref[micro, part] for part in range(4)]
        for index in range(len(sources)):
            for part in range(4):
                total[part] = total[part] + came[micro, index, part].astype(f32)
        hat, spread = normalise(x_ref[micro])
        norm_grads[0] += jnp.sum(total[0] * hat, axis=0, keepdims=True)
        norm_grads[1] += jnp.sum(total[0], axis=0, keepdims=True)
        g_hat = total[0] * gain
        g_x = spread * (g_hat - lane_mean(g_hat) - hat * lane_mean(g_hat * hat))
        gx_ref[micro] = cotx_ref[micro] + g_x
        for axis in range(3):
            gvec_ref[micro, axis] = cotv_ref[micro, axis] + total[1 + axis]
    held[...] = gvec_in[...]
    for part in range(2):
        for half in range(2):
            row = 2 * part + half
            held[row : row + 1, :] = norm_grads[part][:, half * LANES : (half + 1) * LANES]
    quad[depth_at] = held[...]
    four = [
        start(held, quad.at[depth_at], d_send.at[by], d_recv.at[by], ahead("depth", by))
        for by in range(1, depth)
    ]

    for copy in three:
        copy.wait_recv()
    final = three_out[cell_at].astype(f32)
    for by in range(1, cells):
        final = final + three_in[by].astype(f32)
    summ_ref[depth_at] = final
    share = [
        start(
            summ_ref.at[depth_at],
            summ_ref.at[depth_at],
            e_send.at[by],
            e_recv.at[by],
            ahead("depth", by),
        )
        for by in range(1, depth)
    ]
    for copy in four:
        copy.wait_recv()
    total = quad[0]
    for at in range(1, depth):
        total = total + quad[at]
    octo[cell_at] = total
    eight = [
        start(
            octo.at[cell_at],
            octo.at[cell_at],
            f_send.at[by],
            f_recv.at[by],
            ahead("cells", by),
        )
        for by in range(1, cells)
    ]
    for copy in eight:
        copy.wait_recv()
    total = octo[0]
    for cell in range(1, cells):
        total = total + octo[cell]
    sumv_ref[...] = total
    for copy in share:
        copy.wait_recv()
    for copy in started:
        copy.wait_send()


def adam_update(weight, grad, first, second):
    first_new = beta_one * first + (1.0 - beta_one) * grad
    second_new = beta_two * second + (1.0 - beta_two) * grad * grad
    first_hat = first_new / (1.0 - beta_one**STEP)
    second_hat = second_new / (1.0 - beta_two**STEP)
    weight_new = weight - learn_rate * (
        first_hat / (jnp.sqrt(second_hat) + adam_eps) + decay_rate * weight
    )
    return (weight_new, first_new, second_new)


def shards(
    x_in,
    vec_in,
    cot_x,
    cot_vec,
    mats,
    vecs,
    mats_first,
    mats_second,
    vecs_first,
    vecs_second,
    atom_count,
    neighbours,
    edge_mask,
    edge_vec,
    send_list,
):
    micros, atoms, width = x_in.shape
    slots = neighbours.shape[1]
    halo = send_list.shape[-1]
    per_face = halo // LANES
    cells, depth = lax.axis_size("cells"), lax.axis_size("depth")
    faces = [("cells", 1), ("cells", -1), ("cells", FOLD), ("cells", -FOLD), ("depth", 1), ("depth", -1)]
    sizes = {"cells": cells, "depth": depth}
    sources = []
    face_source = []
    for axis, by in faces:
        key = (axis, by % sizes[axis])
        if key not in sources:
            sources.append(key)
        face_source.append(sources.index(key))
    domains = 1 + len(sources)
    buckets = (domains * atoms + ROWS - 1) // ROWS
    block_of = [1 + face_source[row // per_face] for row in range(6 * per_face)]

    whole = pl.BlockSpec(memory_space=pltpu.VMEM)
    scalars = pl.BlockSpec(memory_space=pltpu.SMEM)

    any_space = pl.BlockSpec(memory_space=pl.ANY)
    count = len(sources)
    quarter = mats.shape[0] // LANES // depth
    v_rows = -(-vecs.shape[0] // LANES)
    v_low = jnp.pad(vecs.astype(bf16), (0, v_rows * LANES - vecs.shape[0])).reshape(v_rows, LANES)
    faces_first = jnp.moveaxis(
        send_list.reshape(micros, 6, per_face, LANES), 1, 0
    ).reshape(6, micros * per_face, LANES)

    own, w_low = pl.pallas_call(
        norm_kernel,
        out_shape=(
            jax.ShapeDtypeStruct((micros, 4, atoms, width), bf16),
            jax.ShapeDtypeStruct((depth, quarter, LANES), bf16),
        ),
        in_specs=[whole] * 3,
        out_specs=[whole] * 2,
        name="norm",
    )(x_in, vec_in, mats.reshape(-1, LANES))

    dma = pltpu.SemaphoreType.DMA
    fetched = pl.pallas_call(
        partial(fetch_kernel, cells, depth, micros, sources, faces),
        out_shape=tuple(
            [jax.ShapeDtypeStruct((micros, 4, atoms, width), bf16)] * count
            + [
                jax.ShapeDtypeStruct(faces_first.shape, i32),
                jax.ShapeDtypeStruct((cells, depth, quarter, LANES), bf16),
                jax.ShapeDtypeStruct((cells, v_rows, LANES), bf16),
            ]
        ),
        in_specs=[any_space] + [whole] * 3,
        out_specs=[any_space] * count + [whole] * 3,
        scratch_shapes=[
            dma((micros, count)),
            dma((micros, count)),
            dma((6,)),
            dma((6,)),
            dma((cells,)),
            dma((cells,)),
            dma((4, cells)),
            dma((4, cells)),
        ],
        compiler_params=pltpu.CompilerParams(
            collective_id=0, has_side_effects=True, vmem_limit_bytes=VMEM_LIMIT
        ),
        name="fetch",
    )(own, faces_first, w_low, v_low)
    halos = fetched[:count]
    got_lists, w_all, v_all = fetched[count:]
    list_rows = jnp.moveaxis(
        got_lists.reshape(6, micros, per_face, LANES), 1, 0
    ).reshape(micros, 6 * per_face, LANES)
    v_all = v_all.reshape(cells, v_rows * LANES)[:, : vecs.shape[0]].reshape(-1, LANES)
    w_rows, v_rows = cells * depth * quarter, v_all.shape[0]

    limit = slots * atoms + buckets * (slots // BLOCK_SLOTS) * 8 + buckets * 2 * UNIT
    capacity = (limit + UNIT - 1) // UNIT * UNIT + 4 * UNIT

    def by_micro(array):
        zeros = (0,) * (len(array.shape) - 1)
        return pl.BlockSpec((1,) + tuple(array.shape[1:]), lambda i: (i,) + zeros)

    per_micro = [neighbours, edge_mask, edge_vec, list_rows, x_in, vec_in, cot_x, cot_vec, *halos]
    out_blocks = [
        jax.ShapeDtypeStruct((micros, atoms, width), f32),
        jax.ShapeDtypeStruct((micros, 3, atoms, width), f32),
        jax.ShapeDtypeStruct((micros, 4, atoms, width), f32),
    ] + [jax.ShapeDtypeStruct((micros, 4, atoms, width), bf16)] * count
    results = pl.pallas_call(
        partial(edge_kernel, domains, buckets, block_of),
        out_shape=tuple(
            out_blocks
            + [
                jax.ShapeDtypeStruct((depth, cells, quarter, LANES), bf16),
                jax.ShapeDtypeStruct((v_rows, LANES), f32),
            ]
        ),
        grid=(micros,),
        in_specs=[scalars] + [by_micro(array) for array in per_micro] + [whole] * 2,
        out_specs=[by_micro(block) for block in out_blocks] + [whole] * 2,
        scratch_shapes=[
            pltpu.VMEM((slots, LANES, LANES), bf16),
            pltpu.VMEM((slots, atoms), i32),
            pltpu.VMEM((slots // BLOCK_SLOTS, LANES), i32),
            pltpu.SMEM((slots // BLOCK_SLOTS, LANES), i32),
            pltpu.VMEM((capacity, LANES), f32),
            pltpu.SemaphoreType.DMA(()),
            pltpu.VMEM((w_rows, LANES), f32),
            pltpu.VMEM((11, ROWS, ROWS), bf16),
            pltpu.VMEM((LANES, 4 * ROWS), bf16),
            pltpu.VMEM((buckets * ROWS, ROWS), bf16),
            pltpu.VMEM((buckets, ROWS, 7 * ROWS), bf16),
            pltpu.VMEM((buckets, ROWS, 7 * ROWS), f32),
            pltpu.VMEM((atoms, 5 * ROWS), bf16),
            pltpu.VMEM((3, 3 * atoms, ROWS), f32),
            pltpu.VMEM((3, atoms, ROWS), bf16),
            pltpu.VMEM((atoms, 5 * ROWS), f32),
            pltpu.VMEM((FEATS, 4 * ROWS), f32),
            pltpu.VMEM((ROWS, ROWS), bf16),
        ]
        + [
            scratch
            for scratch in (
                pltpu.VMEM((UNIT, ROWS), bf16),
                pltpu.VMEM((UNIT, LANES), bf16),
                pltpu.VMEM((UNIT, WORK * ROWS), f32),
                pltpu.VMEM((UNIT, LANES), f32),
                pltpu.VMEM((3, UNIT, LANES), f32),
                pltpu.VMEM((2, 2 * UNIT, LANES), bf16),
                pltpu.VMEM((14, UNIT, LANES), bf16),
                pltpu.VMEM((8, UNIT, LANES), bf16),
                pltpu.VMEM((12, UNIT, LANES), bf16),
            )
            for side in range(2)
        ],
        compiler_params=pltpu.CompilerParams(vmem_limit_bytes=VMEM_LIMIT),
        name="edges",
    )(atom_count, *per_micro, w_all, v_all)
    out_x, out_vec, g_own = results[:3]
    backs = results[3 : 3 + count]
    part_m, part_v = results[3 + count :]
    grad_x, grad_vec, sum_mats, sum_vecs = pl.pallas_call(
        partial(close_kernel, cells, depth, micros, sources),
        out_shape=(
            jax.ShapeDtypeStruct(x_in.shape, f32),
            jax.ShapeDtypeStruct(vec_in.shape, f32),
            jax.ShapeDtypeStruct((depth, quarter, LANES), f32),
            jax.ShapeDtypeStruct((v_rows, LANES), f32),
        ),
        in_specs=[whole] * 7 + [any_space] * count,
        out_specs=[whole] * 4,
        scratch_shapes=[
            pltpu.VMEM((micros, count, 4, atoms, width), bf16),
            pltpu.VMEM((2, cells, quarter, LANES), bf16),
            pltpu.VMEM((cells, quarter, LANES), bf16),
            pltpu.VMEM((cells, quarter, LANES), bf16),
            pltpu.VMEM((cells, quarter, LANES), bf16),
            pltpu.VMEM((cells, quarter, LANES), bf16),
            pltpu.VMEM((v_rows, LANES), f32),
            pltpu.VMEM((depth, v_rows, LANES), f32),
            pltpu.VMEM((cells, v_rows, LANES), f32),
            dma((micros, count)),
            dma((micros, count)),
            dma((3,)),
            dma((3,)),
            dma((cells,)),
            dma((cells,)),
            dma((depth,)),
            dma((depth,)),
            dma((depth,)),
            dma((depth,)),
            dma((cells,)),
            dma((cells,)),
        ],
        compiler_params=pltpu.CompilerParams(
            collective_id=1, has_side_effects=True, vmem_limit_bytes=VMEM_LIMIT
        ),
        name="close",
    )(
        x_in,
        cot_x,
        cot_vec,
        v_all,
        part_v,
        part_m,
        g_own,
        *backs,
    )
    sum_mats = sum_mats.reshape(-1)
    sum_vecs = lax.dynamic_slice_in_dim(
        sum_vecs.reshape(-1), lax.axis_index("cells") * vecs.shape[0], vecs.shape[0]
    )
    new_mats, mats_one, mats_two = adam_update(mats, sum_mats, mats_first, mats_second)
    new_vecs, vecs_one, vecs_two = adam_update(vecs, sum_vecs, vecs_first, vecs_second)
    return (
        out_x,
        out_vec,
        grad_x,
        grad_vec,
        sum_mats,
        sum_vecs,
        new_mats,
        new_vecs,
        mats_one,
        mats_two,
        vecs_one,
        vecs_two,
    )


def solution(mesh):
    by_atom = ("cells", "depth")
    shard = P("cells")
    in_specs = (
        P(None, by_atom, None),
        P(None, None, by_atom, None),
        P(None, by_atom, None),
        P(None, None, by_atom, None),
        shard,
        shard,
        shard,
        shard,
        shard,
        shard,
        P(None, by_atom),
        P(None, None, by_atom),
        P(None, None, by_atom),
        P(None, None, None, by_atom),
        P(None, by_atom, None),
    )
    out_specs = (
        P(None, by_atom, None),
        P(None, None, by_atom, None),
        P(None, by_atom, None),
        P(None, None, by_atom, None),
    ) + (shard,) * 8
    return jax.shard_map(shards, mesh=mesh, in_specs=in_specs, out_specs=out_specs, check_vma=False)
```

time: 276 us -> 230 us (0.83); the launches traced: 272 us -> 231 us
  Pallas kernels: 257 us -> 218 us
    pallas_call x4 -> x2, Pallas kernels: 128 us -> 108 us  [the longest x1 105 us: shards(): pl.pallas_call(partial(edge_kernel, domains, buckets, block_of), out_shap...]
    pallas_call x1, Pallas kernels: 76.7 us -> 57.9 us  [shards(): pl.pallas_call(partial(close_kernel, cells, depth, micros, sources), out_...]
where the time goes in v3:
time: 230 us; the launch traced here: 231 us
  Pallas kernels  218 us (95%)
  local copies, waits for them, and re-layouts  7.65 us (3%)
  other arithmetic  4.36 us (2%)
    pallas_call x1, Pallas kernels, shards(): pl.pallas_call(partial(edge_kernel, domains, buckets, block_of), out_shap...  105 us
    pallas_call x1, Pallas kernels, shards(): pl.pallas_call(partial(close_kernel, cells, depth, micros, sources), out_...  57.9 us
    pallas_call x1, Pallas kernels, shards(): pl.pallas_call(partial(fetch_kernel, cells, depth, micros, sources, faces...  52.5 us

profile of v3, /device:TPU:0, one launch (start us, length us, event | category | flops | bytes accessed | tf_op | source)
XLA Modules:
  0.0 230.9 jit_solution(15700983250995003403)
XLA Ops:
  0.6 0.0 copy-start.9
  0.7 2.4 %norm.1 = (bf16[2,4,128,256]{3,2,1,0:T(8,128)(2,1)}, bf16[4,184,128]{2,1,0:T(8,128)(2,1)}) custom-call(f32[2,128,256]{2,1,0:T(8,128)} %refs_0_.2, f32[2,3,128,256]{3,2,1,0:T(8,128)} %refs_6_.1, f32[736,128]{1,0:T(8,128)} %bitcast.19), custom_call_target="tpu_custom_call" | custom-call | tf_op jit(solution)/shard_map/norm/pallas_call | solution.py:975
  3.0 1.3 reshape.55
  4.3 0.7 convert_element_type.5
  5.0 0.6 pad_bitcast_fusion.refs_3_
  5.6 52.5 %fetch.1 = (bf16[2,4,128,256]{3,2,1,0:T(8,128)(2,1)}, bf16[2,4,128,256]{3,2,1,0:T(8,128)(2,1)}, bf16[2,4,128,256]{3,2,1,0:T(8,128)(2,1)}, bf16[2,4,128,256]{3,2,...) custom-call(bf16[2,4,128,256]{3,2,1,0:T(8,128)(2,1)} %get-tuple-elem, ...), custom_call_target="tpu_custom_call" | custom-call | tf_op jit(solution)/shard_map/fetch/pallas_call | solution.py:987
  58.1 0.7 copy.34
  58.8 0.7 reshape.61.refs_15_.refs_3_
  59.5 0.7 copy.29
  60.2 0.6 copy.31.refs_4_
  60.8 0.0 copy-done.9
  60.8 0.6 copy.30.refs_0_
  61.5 105.4 %edges.1 = (f32[2,128,256]{2,1,0:T(8,128)}, f32[2,3,128,256]{3,2,1,0:T(8,128)}, f32[2,4,128,256]{3,2,1,0:T(8,128)}, bf16[2,4,128,256]{3,2,1,0:T(8,128)(2,1)}, bf...) custom-call(s32[2,1]{1,0:T(2,128)} %copy.30.refs_0_, ...), custom_call_target="tpu_custom_call" | custom-call | tf_op jit(solution)/shard_map/edges/pallas_call | solution.py:1035
  166.9 0.0 copy-start
  166.9 0.0 copy-start.3
  166.9 0.0 copy-start.4
  166.9 57.9 %close.1 = (f32[2,128,256]{2,1,0:T(8,128)}, f32[2,3,128,256]{3,2,1,0:T(8,128)}, f32[4,184,128]{2,1,0:T(8,128)}, f32[28,128]{1,0:T(8,128)}) custom-call(f32[2,128,256]{2,1,0:T(8,128)} %refs_0_.2, f32[2,128,256]{2,1,0:T(8,128)} %refs_1_.3, f32[2,3,128,256]{3,2,1,0:T(8,128)} %refs_2_.3, bf16[28,128]{1,0:T(8,128)(2,1)} %reshape.61.refs_15_.refs_3_, ...), custom_call_target="tpu_custom_call" | custom-call | tf_op jit(solution)/shard_map/close/pallas_call | solution.py:1088
  224.8 0.0 copy-start.6
  224.8 0.0 copy-start.7
  224.8 0.0 copy-start.8
  224.8 0.0 copy-start.5
  224.8 0.0 copy-done
  224.9 0.0 copy-done.3
  224.9 0.0 copy-done.4
  224.9 0.0 copy-start.2
  224.9 2.2 multiply_subtract_fusion
  227.1 0.0 copy-start.1
  227.1 0.0 copy-done.6
  227.1 0.0 copy-done.7
  227.1 0.0 copy-done.8
  227.1 1.4 multiply_subtract_fusion.1
  228.6 0.0 copy-done.5
  228.6 0.7 copy.38
  229.3 0.0 copy-done.2
  229.3 0.9 copy.39
  230.2 0.0 copy-done.1
  230.2 0.8 copy.40
Async XLA Ops:
  0.6 60.2 %copy-start.9 = (s32[2,1]{0,1:T(1,128)S(1)}, s32[2,1]{0,1:T(1,128)}, u32[]{:S(2)}) copy-start(s32[2,1]{0,1:T(1,128)} %param.25) | copy-start | bytes 28
  166.9 58.0 %copy-start = (f32[94208]{0:T(1024)S(1)}, f32[94208]{0:T(1024)}, u32[]{:S(2)}) copy-start(f32[94208]{0:T(1024)} %param.19) | copy-start | bytes 1130500
  166.9 58.0 %copy-start.3 = (f32[94208]{0:T(1024)S(1)}, f32[94208]{0:T(1024)}, u32[]{:S(2)}) copy-start(f32[94208]{0:T(1024)} %param.21) | copy-start | bytes 1130500
  166.9 58.0 %copy-start.4 = (f32[94208]{0:T(1024)S(1)}, f32[94208]{0:T(1024)}, u32[]{:S(2)}) copy-start(f32[94208]{0:T(1024)} %param.22) | copy-start | bytes 1130500
  224.8 2.3 %copy-start.6 = (f32[448]{0:T(512)S(1)}, f32[448]{0:T(512)}, u32[]{:S(2)}) copy-start(f32[448]{0:T(512)} %param.20) | copy-start | bytes 5380
  224.8 2.3 %copy-start.7 = (f32[448]{0:T(512)S(1)}, f32[448]{0:T(512)}, u32[]{:S(2)}) copy-start(f32[448]{0:T(512)} %param.23) | copy-start | bytes 5380
  224.8 2.3 %copy-start.8 = (f32[448]{0:T(512)S(1)}, f32[448]{0:T(512)}, u32[]{:S(2)}) copy-start(f32[448]{0:T(512)} %param.24) | copy-start | bytes 5380
  224.8 3.7 %copy-start.5 = (f32[2,128,256]{2,1,0:T(8,128)S(1)}, f32[2,128,256]{2,1,0:T(8,128)}, u32[]{:S(2)}) copy-start(f32[2,128,256]{2,1,0:T(8,128)} %get-tuple-element.81) | copy-start | bytes 786436
  224.9 4.4 %copy-start.2 = (f32[2,3,128,256]{3,2,1,0:T(8,128)S(1)}, f32[2,3,128,256]{3,2,1,0:T(8,128)}, u32[]{:S(2)}) copy-start(f32[2,3,128,256]{3,2,1,0:T(8,128)} %get-tuple-element.82) | copy-start | bytes 2359300
  227.1 3.0 %copy-start.1 = (f32[4,184,128]{2,1,0:T(8,128)S(1)}, f32[4,184,128]{2,1,0:T(8,128)}, u32[]{:S(2)}) copy-start(f32[4,184,128]{2,1,0:T(8,128)} %get-tuple-element.58) | copy-start | bytes 1130500

commit v4 on v3

--- a/solution.py
+++ b/solution.py
@@ -695,9 +695,16 @@
     own_ref, lists_ref, w_ref, v_ref = refs[:4]
     halo_refs = refs[4 : 4 + len(sources)]
     got_lists, got_w, got_v = refs[4 + len(sources) : 7 + len(sources)]
-    halo_send, halo_recv, list_send, list_recv, v_send, v_recv, w_send, w_recv = refs[
-        7 + len(sources) :
-    ]
+    (
+        halo_send,
+        halo_recv,
+        list_send,
+        list_recv,
+        v_send,
+        v_recv,
+        w_send,
+        w_recv,
+    ) = refs[7 + len(sources) :]
     cell_at, depth_at = lax.axis_index("cells"), lax.axis_index("depth")
     sizes = {"cells": cells, "depth": depth}
     places = {"cells": cell_at, "depth": depth_at}
@@ -716,18 +723,28 @@
         started.append(copy)
         return copy
 
-    first = []
-    for by in range(1, cells):
-        there = ahead("cells", by)
-        first.append(
-            start(
-                w_ref.at[depth_at],
-                got_w.at[cell_at, depth_at],
-                w_send.at[0, by],
-                w_recv.at[0, by],
-                there,
-            )
-        )
+    half = cells // 2
+    base, place = cell_at // half * half, cell_at % half
+
+    def beside(by):
+        return base + (place + by) % half
+
+    def from_beside(by):
+        return base + (place + half - by) % half
+
+    opposite = (cell_at + half) % cells
+
+    def send_weight(source_cell, order, target):
+        piece = got_w.at[source_cell, depth_at]
+        return start(piece, piece, w_send.at[0, order], w_recv.at[0, order], {"cells": target})
+
+    origins = {by: from_beside(by) for by in range(1, half)}
+    origins[half] = opposite
+    for by in range(1, half):
+        origins[half + by] = (from_beside(by) + half) % cells
+    first = {half: send_weight(cell_at, half, opposite)}
+    for by in range(1, half):
+        first[by] = send_weight(cell_at, by, beside(by))
     lists = [
         start(
             lists_ref.at[face],
@@ -742,6 +759,10 @@
         start(v_ref, got_v.at[cell_at], v_send.at[by], v_recv.at[by], ahead("cells", by))
         for by in range(1, cells)
     ]
+    order = [half, *range(1, half), *range(half + 1, cells)]
+    first[half].wait_recv()
+    for by in range(1, half):
+        first[half + by] = send_weight(opposite, half + by, beside(by))
     halos = []
     for micro in range(micros):
         for index, (axis, by) in enumerate(sources):
@@ -754,19 +775,24 @@
                     ahead(axis, by),
                 )
             )
-    mate, other = core_mate(depth_at), chip_mate(depth_at)
-    across = []
-    last = []
-    for by in range(1, cells):
-        first[by - 1].wait_recv()
-        piece = got_w.at[(cell_at + cells - by) % cells, depth_at]
-        across.append(
-            start(piece, piece, w_send.at[1, by], w_recv.at[1, by], {"depth": other})
-        )
-        last.append(start(piece, piece, w_send.at[2, by], w_recv.at[2, by], {"depth": mate}))
-    for by in range(1, cells):
-        across[by - 1].wait_recv()
-        piece = got_w.at[(cell_at + cells - by) % cells, other]
+        if micro > 0:
+            continue
+        mate, other = core_mate(depth_at), chip_mate(depth_at)
+        across = []
+        last = []
+        for by in order:
+            if by != half:
+                first[by].wait_recv()
+            piece = got_w.at[origins[by], depth_at]
+            across.append(
+                start(piece, piece, w_send.at[1, by], w_recv.at[1, by], {"depth": other})
+            )
+            last.append(
+                start(piece, piece, w_send.at[2, by], w_recv.at[2, by], {"depth": mate})
+            )
+    for at, by in enumerate(order):
+        across[at].wait_recv()
+        piece = got_w.at[origins[by], other]
         last.append(start(piece, piece, w_send.at[3, by], w_recv.at[3, by], {"depth": mate}))
     for copy in lists + vectors + last + halos:
         copy.wait_recv()
@@ -775,14 +801,35 @@
 
 
 def close_kernel(cells, depth, micros, sources, *refs):
-    x_ref, cotx_ref, cotv_ref, gain_ref, gvec_in, part_ref = refs[:6]
-    refs = refs[6:]
-    gown_ref = refs[0]
-    back_refs = refs[1 : 1 + len(sources)]
-    refs = refs[1 + len(sources) :]
-    gx_ref, gvec_ref, summ_ref, sumv_ref = refs[:4]
-    came, one_in, two_out, two_in, three_out, three_in, held, quad, octo = refs[4:13]
-    halo_send, halo_recv, m_send, m_recv, c_send, c_recv, d_send, d_recv, e_send, e_recv, f_send, f_recv = refs[13:]
+    count = len(sources)
+    x_ref, cotx_ref, cotv_ref, gain_ref, gvec_in, part_ref, gown_ref = refs[:7]
+    back_refs = refs[7 : 7 + count]
+    gx_ref, gvec_ref, summ_ref, sumv_ref = refs[7 + count : 11 + count]
+    (
+        came,
+        one_in,
+        two_out,
+        two_in,
+        three_out,
+        three_in,
+        four_out,
+        four_in,
+        held,
+        quad,
+        octo,
+        halo_send,
+        halo_recv,
+        m_send,
+        m_recv,
+        c_send,
+        c_recv,
+        d_send,
+        d_recv,
+        e_send,
+        e_recv,
+        f_send,
+        f_recv,
+    ) = refs[11 + count :]
     cell_at, depth_at = lax.axis_index("cells"), lax.axis_index("depth")
     sizes = {"cells": cells, "depth": depth}
     places = {"cells": cell_at, "depth": depth_at}
@@ -798,6 +845,19 @@
         copy.start()
         started.append(copy)
         return copy
+
+    def go_home(micro, piece):
+        parts = pl.ds(0, 1) if piece == 0 else pl.ds(1, 3)
+        return [
+            start(
+                back_refs[index].at[micro, parts],
+                came.at[micro, index, parts],
+                halo_send.at[micro, index, piece],
+                halo_recv.at[micro, index, piece],
+                ahead(axis, -by),
+            )
+            for index, (axis, by) in enumerate(sources)
+        ]
 
     mate, other = core_mate(depth_at), chip_mate(depth_at)
     mate_other = chip_mate(mate)
@@ -805,18 +865,8 @@
         part_ref.at[mate_other], one_in.at[1], m_send.at[0], m_recv.at[0], {"depth": mate}
     )
     one_near = start(part_ref.at[mate], one_in.at[0], m_send.at[1], m_recv.at[1], {"depth": mate})
-    halos = []
-    for micro in range(micros):
-        for index, (axis, by) in enumerate(sources):
-            halos.append(
-                start(
-                    back_refs[index].at[micro],
-                    came.at[micro, index],
-                    halo_send.at[micro, index],
-                    halo_recv.at[micro, index],
-                    ahead(axis, -by),
-                )
-            )
+    scalars = [go_home(micro, 0) for micro in range(micros)]
+    vectors = [go_home(0, 1)]
     one_far.wait_recv()
     two_out[...] = (part_ref[other].astype(f32) + one_in[1].astype(f32)).astype(bf16)
     two = start(two_out, two_in, m_send.at[2], m_recv.at[2], {"depth": other})
@@ -829,41 +879,49 @@
             + two_in[cell].astype(f32)
         )
         three_out[cell] = total.astype(bf16)
+    half = cells // 2
+    base, place = cell_at // half * half, cell_at % half
+    opposite = (cell_at + half) % cells
     three = []
-    for by in range(1, cells):
-        there = (cell_at + by) % cells
-        three.append(
-            start(
-                three_out.at[there],
-                three_in.at[by],
-                c_send.at[by],
-                c_recv.at[by],
-                {"cells": there},
+    for by in range(1, half):
+        there = base + (place + by) % half
+        for side in range(2):
+            order = side * half + by
+            three.append(
+                start(
+                    three_out.at[(there + side * half) % cells],
+                    three_in.at[order],
+                    c_send.at[order],
+                    c_recv.at[order],
+                    {"cells": there},
+                )
             )
-        )
-
-    for copy in halos:
-        copy.wait_recv()
-    gain = jnp.concatenate([gain_ref[half : half + 1, :].astype(f32) for half in range(2)], axis=1)
+    for micro in range(1, micros):
+        vectors.append(go_home(micro, 1))
+
+    def back_sum(micro, part):
+        total = gown_ref[micro, part]
+        for index in range(count):
+            total = total + came[micro, index, part].astype(f32)
+        return total
+
+    gain = jnp.concatenate([gain_ref[side : side + 1, :].astype(f32) for side in range(2)], axis=1)
     norm_grads = [jnp.zeros((1, gain.shape[1]), f32) for part in range(2)]
     for micro in range(micros):
-        total = [gown_ref[micro, part] for part in range(4)]
-        for index in range(len(sources)):
-            for part in range(4):
-                total[part] = total[part] + came[micro, index, part].astype(f32)
+        for copy in scalars[micro]:
+            copy.wait_recv()
+        total = back_sum(micro, 0)
         hat, spread = normalise(x_ref[micro])
-        norm_grads[0] += jnp.sum(total[0] * hat, axis=0, keepdims=True)
-        norm_grads[1] += jnp.sum(total[0], axis=0, keepdims=True)
-        g_hat = total[0] * gain
+        norm_grads[0] += jnp.sum(total * hat, axis=0, keepdims=True)
+        norm_grads[1] += jnp.sum(total, axis=0, keepdims=True)
+        g_hat = total * gain
         g_x = spread * (g_hat - lane_mean(g_hat) - hat * lane_mean(g_hat * hat))
         gx_ref[micro] = cotx_ref[micro] + g_x
-        for axis in range(3):
-            gvec_ref[micro, axis] = cotv_ref[micro, axis] + total[1 + axis]
     held[...] = gvec_in[...]
     for part in range(2):
-        for half in range(2):
-            row = 2 * part + half
-            held[row : row + 1, :] = norm_grads[part][:, half * LANES : (half + 1) * LANES]
+        for side in range(2):
+            row = 2 * part + side
+            held[row : row + 1, :] = norm_grads[part][:, side * LANES : (side + 1) * LANES]
     quad[depth_at] = held[...]
     four = [
         start(held, quad.at[depth_at], d_send.at[by], d_recv.at[by], ahead("depth", by))
@@ -872,20 +930,12 @@
 
     for copy in three:
         copy.wait_recv()
-    final = three_out[cell_at].astype(f32)
-    for by in range(1, cells):
-        final = final + three_in[by].astype(f32)
-    summ_ref[depth_at] = final
-    share = [
-        start(
-            summ_ref.at[depth_at],
-            summ_ref.at[depth_at],
-            e_send.at[by],
-            e_recv.at[by],
-            ahead("depth", by),
-        )
-        for by in range(1, depth)
-    ]
+    sums = [three_out[cell_at].astype(f32), three_out[opposite].astype(f32)]
+    for side in range(2):
+        for by in range(1, half):
+            sums[side] = sums[side] + three_in[side * half + by].astype(f32)
+    four_out[...] = sums[1].astype(bf16)
+    crossing = start(four_out, four_in, c_send.at[0], c_recv.at[0], {"cells": opposite})
     for copy in four:
         copy.wait_recv()
     total = quad[0]
@@ -902,6 +952,23 @@
         )
         for by in range(1, cells)
     ]
+    crossing.wait_recv()
+    summ_ref[depth_at] = sums[0] + four_in[...].astype(f32)
+    share = [
+        start(
+            summ_ref.at[depth_at],
+            summ_ref.at[depth_at],
+            e_send.at[by],
+            e_recv.at[by],
+            ahead("depth", by),
+        )
+        for by in range(1, depth)
+    ]
+    for micro in range(micros):
+        for copy in vectors[micro]:
+            copy.wait_recv()
+        for axis in range(3):
+            gvec_ref[micro, axis] = cotv_ref[micro, axis] + back_sum(micro, 1 + axis)
     for copy in eight:
         copy.wait_recv()
     total = octo[0]
@@ -1102,11 +1169,13 @@
             pltpu.VMEM((cells, quarter, LANES), bf16),
             pltpu.VMEM((cells, quarter, LANES), bf16),
             pltpu.VMEM((cells, quarter, LANES), bf16),
+            pltpu.VMEM((quarter, LANES), bf16),
+            pltpu.VMEM((quarter, LANES), bf16),
             pltpu.VMEM((v_rows, LANES), f32),
             pltpu.VMEM((depth, v_rows, LANES), f32),
             pltpu.VMEM((cells, v_rows, LANES), f32),
-            dma((micros, count)),
-            dma((micros, count)),
+            dma((micros, count, 2)),
+            dma((micros, count, 2)),
             dma((3,)),
             dma((3,)),
             dma((cells,)),

time: 230 us -> 218 us (0.948)
  Pallas kernels: 218 us -> 206 us
    pallas_call x1, Pallas kernels: 105 us -> 86.2 us  [shards(): pl.pallas_call(partial(edge_kernel, domains, buckets, block_of), out_shap...]
    pallas_call x1, Pallas kernels: 57.9 us -> 68.5 us  [shards(): pl.pallas_call(partial(close_kernel, cells, depth, micros, sources), out_...]
    pallas_call x1, Pallas kernels: 52.5 us -> 49.3 us  [shards(): pl.pallas_call(partial(fetch_kernel, cells, depth, micros, sources, faces...]
where the time goes in v4:
time: 218 us; the launch traced here: 219 us
  Pallas kernels  206 us (94%)
  local copies, waits for them, and re-layouts  7.65 us (4%)
  other arithmetic  4.36 us (2%)
    pallas_call x1, Pallas kernels, shards(): pl.pallas_call(partial(edge_kernel, domains, buckets, block_of), out_shap...  86.2 us
    pallas_call x1, Pallas kernels, shards(): pl.pallas_call(partial(close_kernel, cells, depth, micros, sources), out_...  68.5 us
    pallas_call x1, Pallas kernels, shards(): pl.pallas_call(partial(fetch_kernel, cells, depth, micros, sources, faces...  49.3 us

profile of v4, /device:TPU:0, one launch (start us, length us, event | category | flops | bytes accessed | tf_op | source)
XLA Modules:
  0.0 219.1 jit_solution(16510316172785991718)
XLA Ops:
  0.6 0.0 copy-start.9
  0.7 2.4 %norm.1 = (bf16[2,4,128,256]{3,2,1,0:T(8,128)(2,1)}, bf16[4,184,128]{2,1,0:T(8,128)(2,1)}) custom-call(f32[2,128,256]{2,1,0:T(8,128)} %refs_0_.2, f32[2,3,128,256]{3,2,1,0:T(8,128)} %refs_6_.1, f32[736,128]{1,0:T(8,128)} %bitcast.19), custom_call_target="tpu_custom_call" | custom-call | tf_op jit(solution)/shard_map/norm/pallas_call | solution.py:1042
  3.0 1.3 reshape.55
  4.3 0.7 convert_element_type.5
  5.0 0.6 pad_bitcast_fusion.refs_3_
  5.6 49.3 %fetch.1 = (bf16[2,4,128,256]{3,2,1,0:T(8,128)(2,1)}, bf16[2,4,128,256]{3,2,1,0:T(8,128)(2,1)}, bf16[2,4,128,256]{3,2,1,0:T(8,128)(2,1)}, bf16[2,4,128,256]{3,2,...) custom-call(bf16[2,4,128,256]{3,2,1,0:T(8,128)(2,1)} %get-tuple-elem, ...), custom_call_target="tpu_custom_call" | custom-call | tf_op jit(solution)/shard_map/fetch/pallas_call | solution.py:1054
  54.9 0.7 copy.34
  55.6 0.7 reshape.61.refs_15_.refs_3_
  56.3 0.7 copy.29
  57.0 0.6 copy.31.refs_4_
  57.6 0.0 copy-done.9
  57.7 0.6 copy.30.refs_0_
  58.3 86.2 %edges.1 = (f32[2,128,256]{2,1,0:T(8,128)}, f32[2,3,128,256]{3,2,1,0:T(8,128)}, f32[2,4,128,256]{3,2,1,0:T(8,128)}, bf16[2,4,128,256]{3,2,1,0:T(8,128)(2,1)}, bf...) custom-call(s32[2,1]{1,0:T(2,128)} %copy.30.refs_0_, ...), custom_call_target="tpu_custom_call" | custom-call | tf_op jit(solution)/shard_map/edges/pallas_call | solution.py:1102
  144.5 0.0 copy-start
  144.5 0.0 copy-start.3
  144.5 0.0 copy-start.4
  144.5 68.5 %close.1 = (f32[2,128,256]{2,1,0:T(8,128)}, f32[2,3,128,256]{3,2,1,0:T(8,128)}, f32[4,184,128]{2,1,0:T(8,128)}, f32[28,128]{1,0:T(8,128)}) custom-call(f32[2,128,256]{2,1,0:T(8,128)} %refs_0_.2, f32[2,128,256]{2,1,0:T(8,128)} %refs_1_.3, f32[2,3,128,256]{3,2,1,0:T(8,128)} %refs_2_.3, bf16[28,128]{1,0:T(8,128)(2,1)} %reshape.61.refs_15_.refs_3_, ...), custom_call_target="tpu_custom_call" | custom-call | tf_op jit(solution)/shard_map/close/pallas_call | solution.py:1155
  213.0 0.0 copy-start.6
  213.0 0.0 copy-start.7
  213.0 0.0 copy-start.8
  213.0 0.0 copy-start.5
  213.0 0.0 copy-done
  213.0 0.0 copy-done.3
  213.0 0.0 copy-done.4
  213.1 0.0 copy-start.2
  213.1 2.2 %multiply_subtract_fusion = (f32[94208]{0:T(1024)}, f32[94208]{0:T(1024)}, f32[94208]{0:T(1024)}) fusion(f32[94208]{0:T(1024)S(1)} %copy-done, f32[94208]{0:T(1024)} %bitcast.20, f32[94208]{0:T(1024)S(1)} %copy-done.3, f32[94208]{0:T(1024)S(1)} %copy-done.4), kind=kLoop, calls=%fused_computation.3 | loop fusion | flops 1318912 | bytes 2637824 | tf_op jit(solution)/shard_map/sub | solution.py:989
  215.3 0.0 copy-start.1
  215.3 0.0 copy-done.6
  215.3 0.0 copy-done.7
  215.3 0.0 copy-done.8
  215.3 1.4 multiply_subtract_fusion.1
  216.8 0.0 copy-done.5
  216.8 0.7 copy.38
  217.5 0.0 copy-done.2
  217.5 0.9 copy.39
  218.3 0.0 copy-done.1
  218.3 0.8 copy.40
Async XLA Ops:
  0.6 57.0 %copy-start.9 = (s32[2,1]{0,1:T(1,128)S(1)}, s32[2,1]{0,1:T(1,128)}, u32[]{:S(2)}) copy-start(s32[2,1]{0,1:T(1,128)} %param.25) | copy-start | bytes 28
  144.5 68.6 %copy-start = (f32[94208]{0:T(1024)S(1)}, f32[94208]{0:T(1024)}, u32[]{:S(2)}) copy-start(f32[94208]{0:T(1024)} %param.19) | copy-start | bytes 1130500
  144.5 68.5 %copy-start.3 = (f32[94208]{0:T(1024)S(1)}, f32[94208]{0:T(1024)}, u32[]{:S(2)}) copy-start(f32[94208]{0:T(1024)} %param.21) | copy-start | bytes 1130500
  144.5 68.5 %copy-start.4 = (f32[94208]{0:T(1024)S(1)}, f32[94208]{0:T(1024)}, u32[]{:S(2)}) copy-start(f32[94208]{0:T(1024)} %param.22) | copy-start | bytes 1130500
  213.0 2.3 %copy-start.6 = (f32[448]{0:T(512)S(1)}, f32[448]{0:T(512)}, u32[]{:S(2)}) copy-start(f32[448]{0:T(512)} %param.20) | copy-start | bytes 5380
  213.0 2.3 %copy-start.7 = (f32[448]{0:T(512)S(1)}, f32[448]{0:T(512)}, u32[]{:S(2)}) copy-start(f32[448]{0:T(512)} %param.23) | copy-start | bytes 5380
  213.0 2.3 %copy-start.8 = (f32[448]{0:T(512)S(1)}, f32[448]{0:T(512)}, u32[]{:S(2)}) copy-start(f32[448]{0:T(512)} %param.24) | copy-start | bytes 5380
  213.0 3.7 %copy-start.5 = (f32[2,128,256]{2,1,0:T(8,128)S(1)}, f32[2,128,256]{2,1,0:T(8,128)}, u32[]{:S(2)}) copy-start(f32[2,128,256]{2,1,0:T(8,128)} %get-tuple-element.81) | copy-start | bytes 786436
  213.1 4.4 %copy-start.2 = (f32[2,3,128,256]{3,2,1,0:T(8,128)S(1)}, f32[2,3,128,256]{3,2,1,0:T(8,128)}, u32[]{:S(2)}) copy-start(f32[2,3,128,256]{3,2,1,0:T(8,128)} %get-tuple-element.82) | copy-start | bytes 2359300
  215.3 3.0 %copy-start.1 = (f32[4,184,128]{2,1,0:T(8,128)S(1)}, f32[4,184,128]{2,1,0:T(8,128)}, u32[]{:S(2)}) copy-start(f32[4,184,128]{2,1,0:T(8,128)} %get-tuple-element.58) | copy-start | bytes 1130500

commit v5 on v4

--- a/solution.py
+++ b/solution.py
@@ -17,7 +17,7 @@
 ROWS = 256
 UNIT = 256
 BLOCK_SLOTS = 4
-TILE = 192
+TILES = ((0.3, 192), (0.625, 128), (1.0, 80))
 
 norm_eps = 1e-05
 cut_radius = 5.0
@@ -56,7 +56,13 @@
     return centered * spread, spread
 
 
-def norm_kernel(x_ref, vec_ref, mats_ref, own_ref, low_ref):
+def norm_kernel(x_ref, vec_ref, mats_ref, list_ref, own_ref, low_ref, lists_ref):
+    micros, faces, halo = list_ref.shape
+    per_face = halo // LANES
+    for face in range(faces):
+        for row in range(micros * per_face):
+            lanes = slice(row % per_face * LANES, (row % per_face + 1) * LANES)
+            lists_ref[face, row : row + 1, :] = list_ref[row // per_face, face : face + 1, lanes]
     quarter = low_ref.shape[1]
     for part in range(low_ref.shape[0]):
         low_ref[part] = mats_ref[part * quarter : (part + 1) * quarter, :].astype(bf16)
@@ -81,8 +87,8 @@
     list_lane = halo_at & (LANES - 1)
     atom_in = nbr
     block_id = jnp.zeros_like(nbr)
-    for row in range(lists.shape[0]):
-        table = jnp.broadcast_to(lists[row : row + 1, :], (slots, atoms))
+    for row, picks in enumerate(lists):
+        table = jnp.broadcast_to(picks, (slots, atoms))
         picked = jnp.take_along_axis(table, list_lane, axis=1)
         here = list_row == row
         atom_in = jnp.where(here, picked, atom_in)
@@ -150,36 +156,58 @@
     for total in totals:
         bases.append(bases[-1] + (((total + (2 * UNIT - 1)) >> 8) << 8))
 
-    def picks(places, b, first):
-        wanted = lax.broadcasted_iota(i32, (TILE, wide), 0) + (b * 1024 + first)
+    def picks(places, b, first, tile):
+        wanted = lax.broadcasted_iota(i32, (tile, wide), 0) + (b * 1024 + first)
         return jnp.where(places == wanted, 1.0, 0.0).astype(bf16)
 
-    def block_body(block, at):
-        first = block * BLOCK_SLOTS
-        places = jnp.concatenate(
-            [place[pl.ds(first + t, 1), :] for t in range(BLOCK_SLOTS)], axis=1
-        )
-        feats = jnp.concatenate([feat[first + t] for t in range(BLOCK_SLOTS)], axis=1)
-        following = []
+    def places_of(block):
+        rows = [place[pl.ds(block * BLOCK_SLOTS + t, 1), :] for t in range(BLOCK_SLOTS)]
+        return jnp.concatenate(rows, axis=1)
+
+    def feats_of(block):
+        parts = [feat[block * BLOCK_SLOTS + t] for t in range(BLOCK_SLOTS)]
+        return jnp.concatenate(parts, axis=1)
+
+    def padded(block, b):
+        return ((count_sc[block, b] + 7) >> 3) << 3
+
+    def block_body(size, block, at):
+        places = places_of(block)
+        feats = feats_of(block)
         for b in range(buckets):
-            number = count_sc[block, b]
-            packed[pl.ds(pl.multiple_of(at[b], 8), TILE), :] = dot_nt(picks(places, b, 0), feats)
-
-            @pl.when(number > TILE)
-            def _(b=b, number=number):
+            made = dot_nt(picks(places, b, 0, size), feats)
+            packed[pl.ds(pl.multiple_of(at[b], 8), size), :] = made
+        return tuple(at[b] + padded(block, b) for b in range(buckets))
+
+    def rest_body(size, block, at):
+        for b in range(buckets):
+            rows = padded(block, b)
+
+            @pl.when(rows > size)
+            def _(b=b, rows=rows):
                 def tile_body(tile, carry):
-                    feats = jnp.concatenate([feat[first + t] for t in range(BLOCK_SLOTS)], axis=1)
-                    pick = picks(places, b, tile * TILE)
-                    start = pl.multiple_of(at[b] + tile * TILE, 8)
-                    packed[pl.ds(start, TILE), :] = dot_nt(pick, feats)
+                    first = jnp.minimum(tile * size, rows - size)
+                    pick = picks(places_of(block), b, first, size)
+                    start = pl.multiple_of(at[b] + first, 8)
+                    packed[pl.ds(start, size), :] = dot_nt(pick, feats_of(block))
                     return carry
 
-                lax.fori_loop(1, (number + (TILE - 1)) // TILE, tile_body, 0)
-
-            following.append(at[b] + (((number + 7) >> 3) << 3))
-        return tuple(following)
-
-    ends = lax.fori_loop(0, blocks, block_body, tuple(bases[:buckets]))
+                lax.fori_loop(1, (rows + (size - 1)) // size, tile_body, 0)
+
+        return tuple(at[b] + padded(block, b) for b in range(buckets))
+
+    begin = 0
+    ends = tuple(bases[:buckets])
+    for share, size in TILES:
+        until = int(blocks * share)
+        ends = lax.fori_loop(begin, until, partial(block_body, size), ends, unroll=2)
+        begin = until
+    begin = 0
+    ends = tuple(bases[:buckets])
+    for share, size in TILES:
+        until = int(blocks * share)
+        ends = lax.fori_loop(begin, until, partial(rest_body, size), ends)
+        begin = until
     zeros = jnp.zeros((UNIT, LANES), f32)
     for end in ends:
         packed[pl.ds(pl.multiple_of(end, 8), UNIT), :] = zeros
@@ -189,7 +217,7 @@
 
 def edge_kernel(domains, buckets, block_of, *refs):
     refs = list(refs)
-    count_ref, nbr_ref, mask_ref, geom_ref, list_ref, x_ref, vec_ref, cotx_ref, cotv_ref = refs[:9]
+    count_ref, list_ref, nbr_ref, mask_ref, geom_ref, x_ref, vec_ref, cotx_ref, cotv_ref = refs[:9]
     halo_refs = refs[9 : 9 + domains - 1]
     at = 9 + domains - 1
     w_ref, v_ref = refs[at : at + 2]
@@ -273,8 +301,14 @@
         heads[...] = jnp.where(head_from == head_to, 0.5, 0.0).astype(bf16)
 
     geom = [geom_ref[0, axis] for axis in range(3)]
+    per_face = len(block_of) // list_ref.shape[0]
+    lists = [
+        list_ref[face, pl.ds(micro * per_face + row, 1), :]
+        for face in range(list_ref.shape[0])
+        for row in range(per_face)
+    ]
     edge_features(
-        nbr_ref[0], mask_ref[0], geom, list_ref[0], block_of, buckets, feat, place, count_vec
+        nbr_ref[0], mask_ref[0], geom, lists, block_of, buckets, feat, place, count_vec
     )
     copy = pltpu.make_async_copy(count_vec, count_sc, sem)
     copy.start()
@@ -866,7 +900,7 @@
     )
     one_near = start(part_ref.at[mate], one_in.at[0], m_send.at[1], m_recv.at[1], {"depth": mate})
     scalars = [go_home(micro, 0) for micro in range(micros)]
-    vectors = [go_home(0, 1)]
+    vectors = [go_home(micro, 1) for micro in range(micros)]
     one_far.wait_recv()
     two_out[...] = (part_ref[other].astype(f32) + one_in[1].astype(f32)).astype(bf16)
     two = start(two_out, two_in, m_send.at[2], m_recv.at[2], {"depth": other})
@@ -896,8 +930,6 @@
                     {"cells": there},
                 )
             )
-    for micro in range(1, micros):
-        vectors.append(go_home(micro, 1))
 
     def back_sum(micro, part):
         total = gown_ref[micro, part]
@@ -1033,22 +1065,19 @@
     any_space = pl.BlockSpec(memory_space=pl.ANY)
     count = len(sources)
     quarter = mats.shape[0] // LANES // depth
-    v_rows = -(-vecs.shape[0] // LANES)
-    v_low = jnp.pad(vecs.astype(bf16), (0, v_rows * LANES - vecs.shape[0])).reshape(v_rows, LANES)
-    faces_first = jnp.moveaxis(
-        send_list.reshape(micros, 6, per_face, LANES), 1, 0
-    ).reshape(6, micros * per_face, LANES)
-
-    own, w_low = pl.pallas_call(
+    list_shape = jax.ShapeDtypeStruct((6, micros * per_face, LANES), i32)
+
+    own, w_low, my_lists = pl.pallas_call(
         norm_kernel,
         out_shape=(
             jax.ShapeDtypeStruct((micros, 4, atoms, width), bf16),
             jax.ShapeDtypeStruct((depth, quarter, LANES), bf16),
+            list_shape,
         ),
-        in_specs=[whole] * 3,
-        out_specs=[whole] * 2,
+        in_specs=[whole] * 4,
+        out_specs=[whole] * 3,
         name="norm",
-    )(x_in, vec_in, mats.reshape(-1, LANES))
+    )(x_in, vec_in, mats.reshape(-1, LANES), send_list)
 
     dma = pltpu.SemaphoreType.DMA
     fetched = pl.pallas_call(
@@ -1056,9 +1085,9 @@
         out_shape=tuple(
             [jax.ShapeDtypeStruct((micros, 4, atoms, width), bf16)] * count
             + [
-                jax.ShapeDtypeStruct(faces_first.shape, i32),
+                list_shape,
                 jax.ShapeDtypeStruct((cells, depth, quarter, LANES), bf16),
-                jax.ShapeDtypeStruct((cells, v_rows, LANES), bf16),
+                jax.ShapeDtypeStruct((cells, 1, vecs.shape[0]), f32),
             ]
         ),
         in_specs=[any_space] + [whole] * 3,
@@ -1077,13 +1106,10 @@
             collective_id=0, has_side_effects=True, vmem_limit_bytes=VMEM_LIMIT
         ),
         name="fetch",
-    )(own, faces_first, w_low, v_low)
+    )(own, my_lists, w_low, vecs.reshape(1, -1))
     halos = fetched[:count]
     got_lists, w_all, v_all = fetched[count:]
-    list_rows = jnp.moveaxis(
-        got_lists.reshape(6, micros, per_face, LANES), 1, 0
-    ).reshape(micros, 6 * per_face, LANES)
-    v_all = v_all.reshape(cells, v_rows * LANES)[:, : vecs.shape[0]].reshape(-1, LANES)
+    v_all = v_all.astype(bf16).reshape(-1, LANES)
     w_rows, v_rows = cells * depth * quarter, v_all.shape[0]
 
     limit = slots * atoms + buckets * (slots // BLOCK_SLOTS) * 8 + buckets * 2 * UNIT
@@ -1093,7 +1119,7 @@
         zeros = (0,) * (len(array.shape) - 1)
         return pl.BlockSpec((1,) + tuple(array.shape[1:]), lambda i: (i,) + zeros)
 
-    per_micro = [neighbours, edge_mask, edge_vec, list_rows, x_in, vec_in, cot_x, cot_vec, *halos]
+    per_micro = [neighbours, edge_mask, edge_vec, x_in, vec_in, cot_x, cot_vec, *halos]
     out_blocks = [
         jax.ShapeDtypeStruct((micros, atoms, width), f32),
         jax.ShapeDtypeStruct((micros, 3, atoms, width), f32),
@@ -1109,7 +1135,7 @@
             ]
         ),
         grid=(micros,),
-        in_specs=[scalars] + [by_micro(array) for array in per_micro] + [whole] * 2,
+        in_specs=[scalars, whole] + [by_micro(array) for array in per_micro] + [whole] * 2,
         out_specs=[by_micro(block) for block in out_blocks] + [whole] * 2,
         scratch_shapes=[
             pltpu.VMEM((slots, LANES, LANES), bf16),
@@ -1148,7 +1174,7 @@
         ],
         compiler_params=pltpu.CompilerParams(vmem_limit_bytes=VMEM_LIMIT),
         name="edges",
-    )(atom_count, *per_micro, w_all, v_all)
+    )(atom_count, got_lists, *per_micro, w_all, v_all)
     out_x, out_vec, g_own = results[:3]
     backs = results[3 : 3 + count]
     part_m, part_v = results[3 + count :]

time: 218 us -> 205 us (0.940); the launches traced: 219 us -> 202 us
  Pallas kernels: 206 us -> 192 us
  local copies, waits for them, and re-layouts: 7.65 us -> 5.06 us
    pallas_call x1, Pallas kernels: 68.5 us -> 58.2 us  [shards(): pl.pallas_call(partial(close_kernel, cells, depth, micros, sources), out_...]
    pallas_call x1, Pallas kernels: 86.2 us -> 81.7 us  [shards(): pl.pallas_call(partial(edge_kernel, domains, buckets, block_of), out_shap...]
    reshape x5 -> x1, local copies, waits for them, and re-layouts: 3.9 us -> 0.69 us  [shards(): v_all = v_all.astype(bf16).reshape(-1, LANES)]
where the time goes in v5:
time: 205 us; the launch traced here: 202 us
  Pallas kernels  192 us (94%)
  local copies, waits for them, and re-layouts  5.06 us (2%)
  other arithmetic  4.44 us (2%)
    pallas_call x1, Pallas kernels, shards(): pl.pallas_call(partial(edge_kernel, domains, buckets, block_of), out_shap...  81.7 us
    pallas_call x1, Pallas kernels, shards(): pl.pallas_call(partial(close_kernel, cells, depth, micros, sources), out_...  58.2 us
    pallas_call x1, Pallas kernels, shards(): pl.pallas_call(partial(fetch_kernel, cells, depth, micros, sources, faces...  49.4 us
    unnamed x25, local copies, waits for them, and re-layouts  4.37 us

profile of v5, /device:TPU:0, one launch (start us, length us, event | category | flops | bytes accessed | tf_op | source)
XLA Modules:
  0.0 201.9 jit_solution(15873702568840208889)
XLA Ops:
  0.6 0.0 copy-start.9
  0.7 1.3 copy.29.list_ref
  2.0 2.3 %norm.1 = (bf16[2,4,128,256]{3,2,1,0:T(8,128)(2,1)}, bf16[4,184,128]{2,1,0:T(8,128)(2,1)}, s32[6,4,128]{2,1,0:T(4,128)}) custom-call(f32[2,128,256]{2,1,0:T(8,128)} %refs_0_.2, f32[2,3,128,256]{3,2,1,0:T(8,128)} %refs_6_.1, f32[736,128]{1,0:T(8,128)} %bitcast.4, s32[2,6,256]{2,1,0:T(8,128)} %copy.29.list_ref), custom_call_target="tpu_custom_call" | custom-call | tf_op jit(solution)/shard_map/norm/pallas_call | solution.py:1070
  4.3 49.4 %fetch.1 = (bf16[2,4,128,256]{3,2,1,0:T(8,128)(2,1)}, bf16[2,4,128,256]{3,2,1,0:T(8,128)(2,1)}, bf16[2,4,128,256]{3,2,1,0:T(8,128)(2,1)}, bf16[2,4,128,256]{3,2,...) custom-call(bf16[2,4,128,256]{3,2,1,0:T(8,128)(2,1)} %get-tuple-elem, ...), custom_call_target="tpu_custom_call" | custom-call | tf_op jit(solution)/shard_map/fetch/pallas_call | solution.py:1083
  53.7 0.8 convert_reduce_fusion
  54.4 0.7 reshape.41.refs_15_.refs_3_
  55.1 0.0 copy-done.9
  55.1 0.6 copy.30.refs_0_
  55.8 81.7 %edges.1 = (f32[2,128,256]{2,1,0:T(8,128)}, f32[2,3,128,256]{3,2,1,0:T(8,128)}, f32[2,4,128,256]{3,2,1,0:T(8,128)}, bf16[2,4,128,256]{3,2,1,0:T(8,128)(2,1)}, bf...) custom-call(s32[2,1]{1,0:T(2,128)} %copy.30.refs_0_, ...), custom_call_target="tpu_custom_call" | custom-call | tf_op jit(solution)/shard_map/edges/pallas_call | solution.py:1128
  137.5 0.0 copy-start
  137.5 0.0 copy-start.3
  137.5 0.0 copy-start.4
  137.5 58.2 %close.1 = (f32[2,128,256]{2,1,0:T(8,128)}, f32[2,3,128,256]{3,2,1,0:T(8,128)}, f32[4,184,128]{2,1,0:T(8,128)}, f32[28,128]{1,0:T(8,128)}) custom-call(f32[2,128,256]{2,1,0:T(8,128)} %refs_0_.2, f32[2,128,256]{2,1,0:T(8,128)} %refs_1_.1, f32[2,3,128,256]{3,2,1,0:T(8,128)} %refs_2_.3, bf16[28,128]{1,0:T(8,128)(2,1)} %reshape.41.refs_15_.refs_3_, ...), custom_call_target="tpu_custom_call" | custom-call | tf_op jit(solution)/shard_map/close/pallas_call | solution.py:1181
  195.7 0.0 copy-start.6
  195.7 0.0 copy-start.7
  195.8 0.0 copy-start.8
  195.8 0.0 copy-start.5
  195.8 0.0 copy-done
  195.8 0.0 copy-done.3
  195.8 0.0 copy-done.4
  195.8 0.0 copy-start.2
  195.8 2.2 %multiply_subtract_fusion = (f32[94208]{0:T(1024)}, f32[94208]{0:T(1024)}, f32[94208]{0:T(1024)}) fusion(f32[94208]{0:T(1024)S(1)} %copy-done, f32[94208]{0:T(1024)} %bitcast.5, f32[94208]{0:T(1024)S(1)} %copy-done.3, f32[94208]{0:T(1024)S(1)} %copy-done.4), kind=kLoop, calls=%fused_computation.3 | loop fusion | flops 1318912 | bytes 2637824 | tf_op jit(solution)/shard_map/sub | solution.py:1021
  198.1 0.0 copy-start.1
  198.1 0.0 copy-done.6
  198.1 0.0 copy-done.7
  198.1 0.0 copy-done.8
  198.1 1.4 multiply_subtract_fusion.1
  199.5 0.0 copy-done.5
  199.5 0.7 copy.34
  200.2 0.0 copy-done.2
  200.2 0.9 copy.35
  201.1 0.0 copy-done.1
  201.1 0.8 copy.36
Async XLA Ops:
  0.6 54.5 %copy-start.9 = (s32[2,1]{0,1:T(1,128)S(1)}, s32[2,1]{0,1:T(1,128)}, u32[]{:S(2)}) copy-start(s32[2,1]{0,1:T(1,128)} %param.25) | copy-start | bytes 28
  137.5 58.3 %copy-start = (f32[94208]{0:T(1024)S(1)}, f32[94208]{0:T(1024)}, u32[]{:S(2)}) copy-start(f32[94208]{0:T(1024)} %param.19) | copy-start | bytes 1130500
  137.5 58.3 %copy-start.3 = (f32[94208]{0:T(1024)S(1)}, f32[94208]{0:T(1024)}, u32[]{:S(2)}) copy-start(f32[94208]{0:T(1024)} %param.21) | copy-start | bytes 1130500
  137.5 58.3 %copy-start.4 = (f32[94208]{0:T(1024)S(1)}, f32[94208]{0:T(1024)}, u32[]{:S(2)}) copy-start(f32[94208]{0:T(1024)} %param.22) | copy-start | bytes 1130500
  195.7 2.3 %copy-start.6 = (f32[448]{0:T(512)S(1)}, f32[448]{0:T(512)}, u32[]{:S(2)}) copy-start(f32[448]{0:T(512)} %param.20) | copy-start | bytes 5380
  195.7 2.3 %copy-start.7 = (f32[448]{0:T(512)S(1)}, f32[448]{0:T(512)}, u32[]{:S(2)}) copy-start(f32[448]{0:T(512)} %param.23) | copy-start | bytes 5380
  195.8 2.3 %copy-start.8 = (f32[448]{0:T(512)S(1)}, f32[448]{0:T(512)}, u32[]{:S(2)}) copy-start(f32[448]{0:T(512)} %param.24) | copy-start | bytes 5380
  195.8 3.7 %copy-start.5 = (f32[2,128,256]{2,1,0:T(8,128)S(1)}, f32[2,128,256]{2,1,0:T(8,128)}, u32[]{:S(2)}) copy-start(f32[2,128,256]{2,1,0:T(8,128)} %get-tuple-element.83) | copy-start | bytes 786436
  195.8 4.4 %copy-start.2 = (f32[2,3,128,256]{3,2,1,0:T(8,128)S(1)}, f32[2,3,128,256]{3,2,1,0:T(8,128)}, u32[]{:S(2)}) copy-start(f32[2,3,128,256]{3,2,1,0:T(8,128)} %get-tuple-element.84) | copy-start | bytes 2359300
  198.1 3.0 %copy-start.1 = (f32[4,184,128]{2,1,0:T(8,128)S(1)}, f32[4,184,128]{2,1,0:T(8,128)}, u32[]{:S(2)}) copy-start(f32[4,184,128]{2,1,0:T(8,128)} %get-tuple-element.60) | copy-start | bytes 1130500

commit v6 on v5

--- a/solution.py
+++ b/solution.py
@@ -593,7 +593,7 @@
                 hits(other, rows_of(unit + 1))
                 mix(scatter_steps(other, unit - 1), on_chunks(heads_stage, mine))
 
-            @pl.when(count_sc[0, 0] >= 0)
+            @pl.when(count_sc[0, 0] >= 0 if at == 0 else unit < total_units)
             def _(unit=unit, mine=mine, other=other):
                 head_sums(mine)
                 mix(
@@ -793,12 +793,9 @@
         start(v_ref, got_v.at[cell_at], v_send.at[by], v_recv.at[by], ahead("cells", by))
         for by in range(1, cells)
     ]
-    order = [half, *range(1, half), *range(half + 1, cells)]
-    first[half].wait_recv()
-    for by in range(1, half):
-        first[half + by] = send_weight(opposite, half + by, beside(by))
     halos = []
-    for micro in range(micros):
+
+    def send_halos(micro):
         for index, (axis, by) in enumerate(sources):
             halos.append(
                 start(
@@ -809,21 +806,26 @@
                     ahead(axis, by),
                 )
             )
-        if micro > 0:
-            continue
-        mate, other = core_mate(depth_at), chip_mate(depth_at)
-        across = []
-        last = []
-        for by in order:
-            if by != half:
-                first[by].wait_recv()
-            piece = got_w.at[origins[by], depth_at]
-            across.append(
-                start(piece, piece, w_send.at[1, by], w_recv.at[1, by], {"depth": other})
-            )
-            last.append(
-                start(piece, piece, w_send.at[2, by], w_recv.at[2, by], {"depth": mate})
-            )
+
+    send_halos(0)
+    order = [half, *range(1, half), *range(half + 1, cells)]
+    first[half].wait_recv()
+    for by in range(1, half):
+        first[half + by] = send_weight(opposite, half + by, beside(by))
+    mate, other = core_mate(depth_at), chip_mate(depth_at)
+    across = []
+    last = []
+    for by in order:
+        if by != half:
+            first[by].wait_recv()
+        piece = got_w.at[origins[by], depth_at]
+        across.append(
+            start(piece, piece, w_send.at[1, by], w_recv.at[1, by], {"depth": other})
+        )
+        last.append(start(piece, piece, w_send.at[2, by], w_recv.at[2, by], {"depth": mate}))
+        if by == order[min(half - 1, cells - 2)]:
+            for micro in range(1, micros):
+                send_halos(micro)
     for at, by in enumerate(order):
         across[at].wait_recv()
         piece = got_w.at[origins[by], other]
@@ -836,7 +838,7 @@
 
 def close_kernel(cells, depth, micros, sources, *refs):
     count = len(sources)
-    x_ref, cotx_ref, cotv_ref, gain_ref, gvec_in, part_ref, gown_ref = refs[:7]
+    x_far, cotx_far, cotv_far, gain_ref, gvec_in, part_ref, gown_far = refs[:7]
     back_refs = refs[7 : 7 + count]
     gx_ref, gvec_ref, summ_ref, sumv_ref = refs[7 + count : 11 + count]
     (
@@ -851,6 +853,11 @@
         held,
         quad,
         octo,
+        x_ref,
+        cotx_ref,
+        cotv_ref,
+        gown_ref,
+        load_sem,
         halo_send,
         halo_recv,
         m_send,
@@ -901,6 +908,14 @@
     one_near = start(part_ref.at[mate], one_in.at[0], m_send.at[1], m_recv.at[1], {"depth": mate})
     scalars = [go_home(micro, 0) for micro in range(micros)]
     vectors = [go_home(micro, 1) for micro in range(micros)]
+    loads = [
+        pltpu.make_async_copy(far, near, load_sem.at[at])
+        for at, (far, near) in enumerate(
+            ((gown_far, gown_ref), (x_far, x_ref), (cotx_far, cotx_ref), (cotv_far, cotv_ref))
+        )
+    ]
+    for load in loads:
+        load.start()
     one_far.wait_recv()
     two_out[...] = (part_ref[other].astype(f32) + one_in[1].astype(f32)).astype(bf16)
     two = start(two_out, two_in, m_send.at[2], m_recv.at[2], {"depth": other})
@@ -939,6 +954,8 @@
 
     gain = jnp.concatenate([gain_ref[side : side + 1, :].astype(f32) for side in range(2)], axis=1)
     norm_grads = [jnp.zeros((1, gain.shape[1]), f32) for part in range(2)]
+    for load in loads:
+        load.wait()
     for micro in range(micros):
         for copy in scalars[micro]:
             copy.wait_recv()
@@ -1022,6 +1039,17 @@
         first_hat / (jnp.sqrt(second_hat) + adam_eps) + decay_rate * weight
     )
     return (weight_new, first_new, second_new)
+
+
+def update_kernel(*refs):
+    ins, outs = refs[:6], refs[6:]
+    outs[0][...] = ins[0][...]
+    outs[1][...] = ins[1][...]
+    grad = ins[2][...]
+    outs[2][...] = grad
+    updated = adam_update(ins[3][...], grad, ins[4][...], ins[5][...])
+    for out, value in zip(outs[3:], updated):
+        out[...] = value
 
 
 def shards(
@@ -1186,7 +1214,7 @@
             jax.ShapeDtypeStruct((depth, quarter, LANES), f32),
             jax.ShapeDtypeStruct((v_rows, LANES), f32),
         ),
-        in_specs=[whole] * 7 + [any_space] * count,
+        in_specs=[any_space] * 3 + [whole] * 3 + [any_space] * (1 + count),
         out_specs=[whole] * 4,
         scratch_shapes=[
             pltpu.VMEM((micros, count, 4, atoms, width), bf16),
@@ -1200,6 +1228,11 @@
             pltpu.VMEM((v_rows, LANES), f32),
             pltpu.VMEM((depth, v_rows, LANES), f32),
             pltpu.VMEM((cells, v_rows, LANES), f32),
+            pltpu.VMEM(x_in.shape, f32),
+            pltpu.VMEM(cot_x.shape, f32),
+            pltpu.VMEM(cot_vec.shape, f32),
+            pltpu.VMEM(g_own.shape, f32),
+            dma((4,)),
             dma((micros, count, 2)),
             dma((micros, count, 2)),
             dma((3,)),
@@ -1227,11 +1260,31 @@
         g_own,
         *backs,
     )
-    sum_mats = sum_mats.reshape(-1)
+    flat = [
+        grad_x.reshape(-1, width),
+        grad_vec.reshape(-1, width),
+        *[array.reshape(-1, LANES) for array in (sum_mats, mats, mats_first, mats_second)],
+    ]
+    steps = 4 if all(array.shape[0] % 32 == 0 for array in flat) else 1
+
+    def by_step(array):
+        return pl.BlockSpec((array.shape[0] // steps, array.shape[1]), lambda i: (i, 0))
+
+    outs = flat[:3] + [flat[3]] * 3
+    grad_x, grad_vec, *matrices = pl.pallas_call(
+        update_kernel,
+        out_shape=tuple(jax.ShapeDtypeStruct(array.shape, f32) for array in outs),
+        grid=(steps,),
+        in_specs=[by_step(array) for array in flat],
+        out_specs=[by_step(array) for array in outs],
+        name="update",
+    )(*flat)
+    grad_x = grad_x.reshape(x_in.shape)
+    grad_vec = grad_vec.reshape(vec_in.shape)
+    sum_mats, new_mats, mats_one, mats_two = [matrix.reshape(-1) for matrix in matrices]
     sum_vecs = lax.dynamic_slice_in_dim(
         sum_vecs.reshape(-1), lax.axis_index("cells") * vecs.shape[0], vecs.shape[0]
     )
-    new_mats, mats_one, mats_two = adam_update(mats, sum_mats, mats_first, mats_second)
     new_vecs, vecs_one, vecs_two = adam_update(vecs, sum_vecs, vecs_first, vecs_second)
     return (
         out_x,

time: 205 us -> 202 us (0.985); the launches traced: 202 us -> 204 us
  Pallas kernels: 192 us -> 199 us
  local copies, waits for them, and re-layouts: 5.06 us -> 2.68 us
  other arithmetic: 4.44 us -> 2.15 us
    pallas_call x1, Pallas kernels: 81.7 us -> 93.6 us  [shards(): pl.pallas_call(partial(edge_kernel, domains, buckets, block_of), out_shap...]
    pallas_call x1, Pallas kernels: 58.2 us -> 51.5 us  [shards(): pl.pallas_call(partial(close_kernel, cells, depth, micros, sources), out_...]
    pallas_call x0 -> x1, Pallas kernels: none -> 4.01 us  [shards(): pl.pallas_call(update_kernel, out_shape=tuple((jax.ShapeDtypeStruct(array...]
    unnamed x25 -> x10, local copies, waits for them, and re-layouts: 4.37 us -> 1.99 us
    pallas_call x1, Pallas kernels: 49.4 us -> 47.1 us  [shards(): pl.pallas_call(partial(fetch_kernel, cells, depth, micros, sources, faces...]
    sub x2 -> x1, other arithmetic: 3.67 us -> 1.38 us  [adam_update(): weight - learn_rate * (first_hat / (jnp.sqrt(second_hat) + adam_eps) + de...]
where the time goes in v6:
time: 202 us; the launch traced here: 204 us
  Pallas kernels  199 us (99%)
  local copies, waits for them, and re-layouts  2.68 us (1%)
  other arithmetic  2.15 us (1%)
    pallas_call x1, Pallas kernels, shards(): pl.pallas_call(partial(edge_kernel, domains, buckets, block_of), out_shap...  93.6 us
    pallas_call x1, Pallas kernels, shards(): pl.pallas_call(partial(close_kernel, cells, depth, micros, sources), out_...  51.5 us
    pallas_call x1, Pallas kernels, shards(): pl.pallas_call(partial(fetch_kernel, cells, depth, micros, sources, faces...  47.1 us

profile of v6, /device:TPU:0, one launch (start us, length us, event | category | flops | bytes accessed | tf_op | source)
XLA Modules:
  0.0 204.1 jit_solution(14313716181483051868)
XLA Ops:
  0.6 0.0 copy-start.3
  0.7 1.3 copy.29.list_ref
  2.0 2.3 %norm.1 = (bf16[2,4,128,256]{3,2,1,0:T(8,128)(2,1)}, bf16[4,184,128]{2,1,0:T(8,128)(2,1)}, s32[6,4,128]{2,1,0:T(4,128)}) custom-call(f32[2,128,256]{2,1,0:T(8,128)} %refs_0_.2, f32[2,3,128,256]{3,2,1,0:T(8,128)} %refs_6_.1, f32[736,128]{1,0:T(8,128)} %bitcast.14, s32[2,6,256]{2,1,0:T(8,128)} %copy.29.list_ref), custom_call_target="tpu_custom_call" | custom-call | tf_op jit(solution)/shard_map/norm/pallas_call | solution.py:1098
  4.3 47.1 %fetch.1 = (bf16[2,4,128,256]{3,2,1,0:T(8,128)(2,1)}, bf16[2,4,128,256]{3,2,1,0:T(8,128)(2,1)}, bf16[2,4,128,256]{3,2,1,0:T(8,128)(2,1)}, bf16[2,4,128,256]{3,2,...) custom-call(bf16[2,4,128,256]{3,2,1,0:T(8,128)(2,1)} %get-tuple-elem, ...), custom_call_target="tpu_custom_call" | custom-call | tf_op jit(solution)/shard_map/fetch/pallas_call | solution.py:1111
  51.4 0.8 convert_reduce_fusion
  52.1 0.7 reshape.72.refs_15_.refs_3_
  52.8 0.0 copy-done.3
  52.8 0.6 copy.30.refs_0_
  53.5 93.6 %edges.1 = (f32[2,128,256]{2,1,0:T(8,128)}, f32[2,3,128,256]{3,2,1,0:T(8,128)}, f32[2,4,128,256]{3,2,1,0:T(8,128)}, bf16[2,4,128,256]{3,2,1,0:T(8,128)(2,1)}, bf...) custom-call(s32[2,1]{1,0:T(2,128)} %copy.30.refs_0_, ...), custom_call_target="tpu_custom_call" | custom-call | tf_op jit(solution)/shard_map/edges/pallas_call | solution.py:1156
  147.1 51.5 %close.1 = (f32[2,128,256]{2,1,0:T(8,128)}, f32[2,3,128,256]{3,2,1,0:T(8,128)}, f32[4,184,128]{2,1,0:T(8,128)}, f32[28,128]{1,0:T(8,128)}) custom-call(f32[2,128,256]{2,1,0:T(8,128)} %refs_0_.2, f32[2,128,256]{2,1,0:T(8,128)} %refs_1_.1, f32[2,3,128,256]{3,2,1,0:T(8,128)} %refs_2_.3, bf16[28,128]{1,0:T(8,128)(2,1)} %reshape.72.refs_15_.refs_3_, ...), custom_call_target="tpu_custom_call" | custom-call | tf_op jit(solution)/shard_map/close/pallas_call | solution.py:1209
  198.6 0.0 copy-start
  198.6 0.0 copy-start.1
  198.6 0.0 copy-start.2
  198.7 4.0 %update.1 = (f32[256,256]{1,0:T(8,128)}, f32[768,256]{1,0:T(8,128)}, f32[736,128]{1,0:T(8,128)}, f32[736,128]{1,0:T(8,128)}, f32[736,128]{1,0:T(8,128)}, /*index=5*/f32[736,128]{1,0:T(8,128)}) custom-call(f32[256,256]{1,0:T(8,128)} %bitcast.20, f32[768,256]{1,0:T(8,128)} %bitcast.16, f32[736,128]{1,0:T(8,128)} %bitcast.19, f32[736,128]{1,0:T(8,128)} %bitcast.15, ...), custom_call_target="tpu_custom_call" | custom-call | tf_op jit(solution)/shard_map/update/pallas_call | solution.py:1274
  202.7 0.0 copy-done
  202.7 0.0 copy-done.1
  202.7 0.0 copy-done.2
  202.7 1.4 multiply_subtract_fusion
Async XLA Ops:
  0.6 52.2 %copy-start.3 = (s32[2,1]{0,1:T(1,128)S(1)}, s32[2,1]{0,1:T(1,128)}, u32[]{:S(2)}) copy-start(s32[2,1]{0,1:T(1,128)} %param.25) | copy-start | bytes 28
  198.6 4.1 %copy-start = (f32[448]{0:T(512)S(1)}, f32[448]{0:T(512)}, u32[]{:S(2)}) copy-start(f32[448]{0:T(512)} %param.20) | copy-start | bytes 5380
  198.6 4.1 %copy-start.1 = (f32[448]{0:T(512)S(1)}, f32[448]{0:T(512)}, u32[]{:S(2)}) copy-start(f32[448]{0:T(512)} %param.23) | copy-start | bytes 5380
  198.6 4.1 %copy-start.2 = (f32[448]{0:T(512)S(1)}, f32[448]{0:T(512)}, u32[]{:S(2)}) copy-start(f32[448]{0:T(512)} %param.24) | copy-start | bytes 5380

commit v7 on v6

--- a/solution.py
+++ b/solution.py
@@ -200,7 +200,7 @@
     ends = tuple(bases[:buckets])
     for share, size in TILES:
         until = int(blocks * share)
-        ends = lax.fori_loop(begin, until, partial(block_body, size), ends, unroll=2)
+        ends = lax.fori_loop(begin, until, partial(block_body, size), ends, unroll=True)
         begin = until
     begin = 0
     ends = tuple(bases[:buckets])

time: 202 us -> 202 us (level); the launches traced: 204 us -> 199 us
  Pallas kernels: 199 us -> 194 us
    pallas_call x1, Pallas kernels: 93.6 us -> 69.9 us  [shards(): pl.pallas_call(partial(edge_kernel, domains, buckets, block_of), out_shap...]
    pallas_call x1, Pallas kernels: 51.5 us -> 70.7 us  [shards(): pl.pallas_call(partial(close_kernel, cells, depth, micros, sources), out_...]
where the time goes in v7:
time: 202 us; the launch traced here: 199 us
  Pallas kernels  194 us (96%)
  local copies, waits for them, and re-layouts  2.68 us (1%)
  other arithmetic  2.15 us (1%)
    pallas_call x1, Pallas kernels, shards(): pl.pallas_call(partial(close_kernel, cells, depth, micros, sources), out_...  70.7 us
    pallas_call x1, Pallas kernels, shards(): pl.pallas_call(partial(edge_kernel, domains, buckets, block_of), out_shap...  69.9 us
    pallas_call x1, Pallas kernels, shards(): pl.pallas_call(partial(fetch_kernel, cells, depth, micros, sources, faces...  47.1 us

profile of v7, /device:TPU:0, one launch (start us, length us, event | category | flops | bytes accessed | tf_op | source)
XLA Modules:
  0.0 199.5 jit_solution(3501763941768618611)
XLA Ops:
  0.6 0.0 copy-start.3
  0.7 1.3 copy.29.list_ref
  2.0 2.3 %norm.1 = (bf16[2,4,128,256]{3,2,1,0:T(8,128)(2,1)}, bf16[4,184,128]{2,1,0:T(8,128)(2,1)}, s32[6,4,128]{2,1,0:T(4,128)}) custom-call(f32[2,128,256]{2,1,0:T(8,128)} %refs_0_.2, f32[2,3,128,256]{3,2,1,0:T(8,128)} %refs_6_.1, f32[736,128]{1,0:T(8,128)} %bitcast.14, s32[2,6,256]{2,1,0:T(8,128)} %copy.29.list_ref), custom_call_target="tpu_custom_call" | custom-call | tf_op jit(solution)/shard_map/norm/pallas_call | solution.py:1098
  4.3 47.1 %fetch.1 = (bf16[2,4,128,256]{3,2,1,0:T(8,128)(2,1)}, bf16[2,4,128,256]{3,2,1,0:T(8,128)(2,1)}, bf16[2,4,128,256]{3,2,1,0:T(8,128)(2,1)}, bf16[2,4,128,256]{3,2,...) custom-call(bf16[2,4,128,256]{3,2,1,0:T(8,128)(2,1)} %get-tuple-elem, ...), custom_call_target="tpu_custom_call" | custom-call | tf_op jit(solution)/shard_map/fetch/pallas_call | solution.py:1111
  51.4 0.8 convert_reduce_fusion
  52.1 0.7 reshape.72.refs_15_.refs_3_
  52.8 0.0 copy-done.3
  52.8 0.6 copy.30.refs_0_
  53.5 69.9 %edges.1 = (f32[2,128,256]{2,1,0:T(8,128)}, f32[2,3,128,256]{3,2,1,0:T(8,128)}, f32[2,4,128,256]{3,2,1,0:T(8,128)}, bf16[2,4,128,256]{3,2,1,0:T(8,128)(2,1)}, bf...) custom-call(s32[2,1]{1,0:T(2,128)} %copy.30.refs_0_, ...), custom_call_target="tpu_custom_call" | custom-call | tf_op jit(solution)/shard_map/edges/pallas_call | solution.py:1156
  123.3 70.7 %close.1 = (f32[2,128,256]{2,1,0:T(8,128)}, f32[2,3,128,256]{3,2,1,0:T(8,128)}, f32[4,184,128]{2,1,0:T(8,128)}, f32[28,128]{1,0:T(8,128)}) custom-call(f32[2,128,256]{2,1,0:T(8,128)} %refs_0_.2, f32[2,128,256]{2,1,0:T(8,128)} %refs_1_.1, f32[2,3,128,256]{3,2,1,0:T(8,128)} %refs_2_.3, bf16[28,128]{1,0:T(8,128)(2,1)} %reshape.72.refs_15_.refs_3_, ...), custom_call_target="tpu_custom_call" | custom-call | tf_op jit(solution)/shard_map/close/pallas_call | solution.py:1209
  194.0 0.0 copy-start
  194.0 0.0 copy-start.1
  194.0 0.0 copy-start.2
  194.0 4.0 %update.1 = (f32[256,256]{1,0:T(8,128)}, f32[768,256]{1,0:T(8,128)}, f32[736,128]{1,0:T(8,128)}, f32[736,128]{1,0:T(8,128)}, f32[736,128]{1,0:T(8,128)}, /*index=5*/f32[736,128]{1,0:T(8,128)}) custom-call(f32[256,256]{1,0:T(8,128)} %bitcast.20, f32[768,256]{1,0:T(8,128)} %bitcast.16, f32[736,128]{1,0:T(8,128)} %bitcast.19, f32[736,128]{1,0:T(8,128)} %bitcast.15, ...), custom_call_target="tpu_custom_call" | custom-call | tf_op jit(solution)/shard_map/update/pallas_call | solution.py:1274
  198.1 0.0 copy-done
  198.1 0.0 copy-done.1
  198.1 0.0 copy-done.2
  198.1 1.4 multiply_subtract_fusion
Async XLA Ops:
  0.6 52.2 %copy-start.3 = (s32[2,1]{0,1:T(1,128)S(1)}, s32[2,1]{0,1:T(1,128)}, u32[]{:S(2)}) copy-start(s32[2,1]{0,1:T(1,128)} %param.25) | copy-start | bytes 28
  194.0 4.1 %copy-start = (f32[448]{0:T(512)S(1)}, f32[448]{0:T(512)}, u32[]{:S(2)}) copy-start(f32[448]{0:T(512)} %param.20) | copy-start | bytes 5380
  194.0 4.1 %copy-start.1 = (f32[448]{0:T(512)S(1)}, f32[448]{0:T(512)}, u32[]{:S(2)}) copy-start(f32[448]{0:T(512)} %param.23) | copy-start | bytes 5380
  194.0 4.1 %copy-start.2 = (f32[448]{0:T(512)S(1)}, f32[448]{0:T(512)}, u32[]{:S(2)}) copy-start(f32[448]{0:T(512)} %param.24) | copy-start | bytes 5380
